TPU v7x, 256 devices: a whole 4x4x8 slice. The times are simulated.
256 devices in a mesh: pipe: 4 (over y), seq: 64 (over x, z, core).
Axes of the slice: x: 4, y: 4, z: 8, core: 2. Of those that a mesh axis runs over, the one named last changes fastest.
Arguments:
- in_flight: bfloat16 [4, 65536, 1024], P('pipe', 'seq'), may hold values from -6 to 6
- fresh_rows: bfloat16 [65536, 1024], P('seq'), may hold values from -6 to 6
- right_factor: bfloat16 [4, 256, 256, 256], P('pipe', 'seq'), may hold values from -0.375 to 0.375
- left_factor: bfloat16 [4, 256, 256, 256], P('pipe', 'seq'), may hold values from -0.375 to 0.375
- gate_gain: float32 [4, 1024], P('pipe'), may hold values from -4 to 4
- gate_bias: float32 [4, 1024], P('pipe'), may hold values from -4 to 4
- norm_gain: float32 [4, 1024], P('pipe'), may hold values from 0.5 to 1.5
- w_up: bfloat16 [4, 4, 256, 512], P('pipe'), may hold values from -0.375 to 0.375
- w_down: bfloat16 [4, 4, 4, 128, 256], P('pipe'), may hold values from -0.25 to 0.25
Outputs:
- first_tick: bfloat16 [4, 65536, 1024], P('pipe', 'seq')
- second_tick: bfloat16 [4, 65536, 1024], P('pipe', 'seq')
All inputs are finite; a program needn't handle non-finite values.
Results may differ from a plain program's by a relative error of at most 0.007.
Values may be sent and summed in bfloat16 or wider, within the bound.
No kernel may reach another device: no remote copies, remote signals or barrier semaphores. Data moves between devices by JAX's collectives and lax.ppermute only.
A program may use at most 128 MiB of HBM per device.

v0:
```python
import jax
import jax.numpy as jnp
from jax import lax
from jax.sharding import PartitionSpec as P

BLOCK = 256


def shifted(block, axis, distance):
    devices = range(lax.axis_size(axis))
    route = [(i - distance, i) for i in devices if i - distance in devices]
    return lax.ppermute(block, axis, route)


def channel_part(rows, returned, gate_slope, gate_shift, gain, up_weight, down_weight):
    input_wide = rows.astype(jnp.float32)
    mixed_seq = returned.reshape(rows.shape).astype(jnp.float32)
    residual = input_wide + mixed_seq * jax.nn.sigmoid(input_wide * gate_slope + gate_shift)
    scale_row = lax.rsqrt(jnp.mean(residual * residual, axis=-1, keepdims=True) + 1e-06)
    normed = (residual * scale_row * gain).astype(jnp.bfloat16)
    blocks_count = up_weight.shape[0]
    up_proj = jnp.einsum(
        "tbd,bdf->tbf",
        normed.reshape(rows.shape[0], blocks_count, -1),
        up_weight,
        preferred_element_type=jnp.float32,
    )
    hidden = jax.nn.gelu(up_proj, approximate=True).astype(jnp.bfloat16)
    hidden = hidden.reshape(rows.shape[0], blocks_count, blocks_count, down_weight.shape[2])
    down_proj = jnp.einsum(
        "tbkq,kbqe->tke", hidden, down_weight, preferred_element_type=jnp.float32
    )
    return (residual + down_proj.reshape(rows.shape)).astype(jnp.bfloat16)


def one_layer(
    rows, right_blocks, left_blocks, gate_slope, gate_shift, gain, up_weight, down_weight
):
    tok_rows, width = rows.shape
    blocks_here = right_blocks.shape[0]
    seq_devices = lax.axis_size("seq")
    cols_here = left_blocks.shape[0]
    blocked = rows.reshape(blocks_here, BLOCK, width)
    first_mix = jnp.einsum(
        "ikj,ijc->ikc", right_blocks, blocked, preferred_element_type=jnp.float32
    ).astype(jnp.bfloat16)
    grouped = first_mix.reshape(blocks_here, seq_devices, cols_here, width)
    arrived = lax.all_to_all(grouped, "seq", split_axis=1, concat_axis=0, tiled=True)
    second_mix = jnp.einsum(
        "jpi,ijc->pjc", left_blocks, arrived[:, 0], preferred_element_type=jnp.float32
    ).astype(jnp.bfloat16)
    regrouped = second_mix.reshape(seq_devices, blocks_here, cols_here, width)
    returned = lax.all_to_all(regrouped, "seq", split_axis=0, concat_axis=2, tiled=True)
    return channel_part(rows, returned, gate_slope, gate_shift, gain, up_weight, down_weight)


def shards(
    in_flight, fresh_rows, right_factor, left_factor, gate_gain, gate_bias, norm_gain, w_up, w_down
):
    segment_index = lax.axis_index("pipe")
    weights = (
        right_factor[0],
        left_factor[0],
        gate_gain[0],
        gate_bias[0],
        norm_gain[0],
        w_up[0],
        w_down[0],
    )
    first_out = one_layer(in_flight[0], *weights)
    received = shifted(first_out, "pipe", 1)
    current = jnp.where(segment_index == 0, fresh_rows, received)
    second_out = one_layer(current, *weights)
    return (first_out[None], second_out[None])


def solution(mesh):
    in_specs = (
        P("pipe", "seq", None),
        P("seq", None),
        P("pipe", "seq", None, None),
        P("pipe", "seq", None, None),
        P("pipe", None),
        P("pipe", None),
        P("pipe", None),
        P("pipe", None, None, None),
        P("pipe", None, None, None, None),
    )
    out_specs = (P("pipe", "seq", None), P("pipe", "seq", None))
    return jax.shard_map(shards, mesh=mesh, in_specs=in_specs, out_specs=out_specs, check_vma=False)
```

profile of v0, /device:TPU:17, one launch (start us, length us, event | category | flops | bytes accessed | tf_op | source)
XLA Modules:
  0.0 409.3 jit_solution(2957488967922057509)
XLA Ops:
  8.5 63.2 %all_to_all.48 = bf16[4,64,4,1024]{3,2,0,1:T(4,128)(2,1)S(1)} all-to-all(bf16[4,64,4,1024]{3,2,0,1:T(4,128)(2,1)S(1)} %copy.62), channel_id=1, replica_groups=mesh['pipe'=4,'seq'=64] {'seq'}, dimensions={1} | all-to-all | bytes 4194304 | tf_op jit(solution)/shard_map/all_to_all | solution.py:48
  76.2 6.4 %all-to-all-start.1 = ((bf16[64,4,4,1024]{3,2,1,0:T(4,128)(2,1)}), bf16[64,4,4,1024]{3,2,1,0:T(4,128)(2,1)}, u32[]{:S(2)}, u32[]{:S(2)}) async-start(bf16[64,4,4,1024]{3,2,1,0:T(4,128)(2,1)} %bitcast.111), calls=%async_computation.1 | async-start | bytes 4194304 | tf_op jit(solution)/shard_map/all_to_all | solution.py:53
  82.6 20.5 %fusion.52 = f32[1024,1024]{1,0:T(8,128)} fusion(bf16[1,1024,1024]{2,1,0:T(8,128)(2,1)S(1)} %copy-done.3), kind=kLoop, calls=%fused_computation.73 | loop fusion | flops 1048576 | bytes 6291456 | tf_op jit(solution)/shard_map/convert_element_type | solution.py:16
  103.1 5.7 %reshape.136 = f32[1024,4,256]{2,1,0:T(4,128)} reshape(f32[1024,1024]{1,0:T(8,128)} %fusion.52) | data formatting | bytes 8388608 | tf_op jit(solution)/shard_map/convert_element_type | solution.py:16
  111.4 5.2 %copy_convert_fusion = f32[1,1024,1024]{2,0,1:T(1,128)} fusion(bf16[1,1024,1024]{2,1,0:T(8,128)(2,1)S(1)} %copy-done.3), kind=kLoop, calls=%fused_computation.40 | loop fusion | flops 1048576 | bytes 6291456 | tf_op jit(solution)/shard_map/convert_element_type | solution.py:16
  116.6 17.0 %all-to-all-done.1 = bf16[64,4,4,1024]{3,2,1,0:T(4,128)(2,1)} async-done(((bf16[64,4,4,1024]{3,2,1,0:T(4,128)(2,1)}), bf16[64,4,4,1024]{3,2,1,0:T(4,128)(2,1)}, u32[]{:S(2)}, u32[]{:S(2)}) %all-to-all-start.1) | async-done | bytes 2097184 | tf_op jit(solution)/shard_map/all_to_all | solution.py:53
  141.3 6.0 %reshape.137 = f32[1024,4,256]{2,1,0:T(4,128)} reshape(f32[1,4,64,4,1024]{4,3,2,1,0:T(4,128)} %copy.66) | data formatting | bytes 8388608 | tf_op jit(solution)/shard_map/convert_element_type | solution.py:17
  147.3 5.3 %reshape.139 = f32[1024,1024]{1,0:T(8,128)} reshape(f32[1,4,64,4,1024]{4,3,2,1,0:T(4,128)} %copy.66) | data formatting | bytes 8388608 | tf_op jit(solution)/shard_map/convert_element_type | solution.py:17
  152.7 5.7 %multiply_reduce_fusion.1 = (f32[1024]{0:T(1024)S(1)}, f32[1024,1024]{1,0:T(8,128)}) fusion(f32[1024,1024]{1,0:T(8,128)} %reshape.139, f32[1024]{0:T(1024)S(1)} %bitcast.116, f32[1024]{0:T(1024)S(1)} %bitcast.119, f32[1,1024,1024]{2,0,1:T(1,128)} %copy_convert_fusion), kind=kLoop, calls=%fused_computation.47 | loop fusion | flops 9436160 | bytes 12595200 | tf_op jit(solution)/shard_map/reduce_sum | solution.py:19
  171.2 5.4 %copy.73 = f32[1024,1024]{1,0:T(8,128)} copy(f32[1024,1024]{0,1:T(8,128)} %bitcast.106) | data formatting | bytes 8388608 | tf_op jit(solution)/shard_map/reshape | solution.py:33
  176.6 5.5 %add_convert_fusion.1 = bf16[1024,1024]{1,0:T(8,128)(2,1)} fusion(f32[1024,1024]{1,0:T(8,128)} %get-tuple-element.7, f32[1024,1024]{1,0:T(8,128)} %copy.73), kind=kLoop, calls=%fused_computation.44 | loop fusion | flops 2097152 | bytes 10485760 | tf_op jit(solution)/shard_map/convert_element_type | solution.py:33
  185.0 46.0 %collective-permute-done = bf16[1024,1024]{1,0:T(8,128)(2,1)} collective-permute-done((bf16[1024,1024]{1,0:T(8,128)(2,1)}, bf16[1024,1024]{1,0:T(8,128)(2,1)}, u32[]{:S(2)}, u32[]{:S(2)}) %collective-permute-start) | collective-permute-done | bytes 2097184 | tf_op jit(solution)/shard_map/ppermute | solution.py:12
  244.5 6.7 %all-to-all-start.2 = ((bf16[4,64,4,1024]{3,2,0,1:T(4,128)(2,1)}), bf16[4,64,4,1024]{3,2,0,1:T(4,128)(2,1)}, u32[]{:S(2)}, u32[]{:S(2)}) async-start(bf16[4,64,4,1024]{3,2,0,1:T(4,128)(2,1)} %copy.74), calls=%async_computation.2 | async-start | bytes 4194304 | tf_op jit(solution)/shard_map/all_to_all | solution.py:48
  251.1 8.6 %copy.65 = f32[1,4,64,4,1024]{4,0,3,2,1:T(1,128)} copy(f32[1,4,64,4,1024]{4,3,1,2,0:T(4,128)} %copy-done.1) | data formatting | bytes 8388608 | tf_op jit(solution)/shard_map/convert_element_type | solution.py:17
  259.7 10.9 %copy.72 = f32[1,1024,1024]{2,0,1:T(1,128)} copy(f32[1,1024,1024]{1,2,0:T(8,128)} %bitcast.107) | data formatting | bytes 8388608 | tf_op jit(solution)/shard_map/reshape | solution.py:33
  270.6 31.6 %all-to-all-done.2 = bf16[4,64,4,1024]{3,2,0,1:T(4,128)(2,1)} async-done(((bf16[4,64,4,1024]{3,2,0,1:T(4,128)(2,1)}), bf16[4,64,4,1024]{3,2,0,1:T(4,128)(2,1)}, u32[]{:S(2)}, u32[]{:S(2)}) %all-to-all-start.2) | async-done | bytes 2097184 | tf_op jit(solution)/shard_map/all_to_all | solution.py:48
  302.3 4.7 %convert_bitcast_fusion.2 = bf16[256,4,1024]{2,0,1:T(8,128)(2,1)} fusion(bf16[256,4,1024]{2,1,0:T(4,128)(2,1)} %bitcast.27, bf16[1,4,256,256]{3,2,1,0:T(8,128)(2,1)} %param.12), kind=kOutput, calls=%fused_computation.56 | convolution fusion | flops 537919488 | bytes 4718592 | tf_op jit(solution)/shard_map/jpi,ijc->pjc/dot_general | solution.py:49
  315.2 6.4 %all-to-all-start.3 = ((bf16[64,4,4,1024]{3,1,2,0:T(4,128)(2,1)}), bf16[64,4,4,1024]{3,1,2,0:T(4,128)(2,1)}, u32[]{:S(2)}, u32[]{:S(2)}) async-start(bf16[64,4,4,1024]{3,1,2,0:T(4,128)(2,1)} %copy.76), calls=%async_computation.3 | async-start | bytes 4194304 | tf_op jit(solution)/shard_map/all_to_all | solution.py:53
  321.6 13.9 %add_convert_fusion.2 = bf16[1,1024,1024]{2,0,1:T(2,128)(2,1)S(1)} fusion(f32[1,1024,1024]{2,0,1:T(1,128)} %copy.72, f32[1,4,64,4,1024]{4,0,3,2,1:T(1,128)} %copy.65, f32[1024]{0:T(1024)S(1)} %bitcast.117, f32[1024]{0:T(1024)S(1)} %bitcast.120, bf16[1,1024,1024]{2,1,0:T(8,128)(2,1)S(1)} %copy-done.3), kind=kLoop, calls=%fused_computation.45 | loop fusion | flops 10485760 | bytes 12591104 | tf_op jit(solution)/shard_map/convert_element_type | solution.py:33
  337.6 34.9 %all-to-all-done.3 = bf16[64,4,4,1024]{3,1,2,0:T(4,128)(2,1)} async-done(((bf16[64,4,4,1024]{3,1,2,0:T(4,128)(2,1)}), bf16[64,4,4,1024]{3,1,2,0:T(4,128)(2,1)}, u32[]{:S(2)}, u32[]{:S(2)}) %all-to-all-start.3) | async-done | bytes 2097184 | tf_op jit(solution)/shard_map/all_to_all | solution.py:53
  375.4 4.7 %copy.77 = f32[1,4,64,4,1024]{4,3,2,1,0:T(4,128)} copy(f32[1,4,64,4,1024]{4,1,3,2,0:T(4,128)S(1)} %convert_bitcast_fusion) | data formatting | bytes 8388608 | tf_op jit(solution)/shard_map/convert_element_type | solution.py:17
  380.1 5.4 %reshape.140 = f32[1024,1024]{1,0:T(8,128)} reshape(f32[1,4,64,4,1024]{4,3,2,1,0:T(4,128)} %copy.77) | data formatting | bytes 8388608 | tf_op jit(solution)/shard_map/convert_element_type | solution.py:17
  398.2 5.4 %copy.82 = f32[1024,1024]{1,0:T(8,128)} copy(f32[1024,1024]{0,1:T(8,128)} %bitcast.110) | data formatting | bytes 8388608 | tf_op jit(solution)/shard_map/reshape | solution.py:33
  403.6 5.5 %fusion.30 = bf16[1,1024,1024]{2,1,0:T(8,128)(2,1)} fusion(f32[1024,1024]{1,0:T(8,128)} %copy-done.2, f32[1024,1024]{1,0:T(8,128)} %copy.82), kind=kLoop, calls=%fused_computation.48 | loop fusion | flops 2097152 | bytes 10485760 | tf_op jit(solution)/shard_map/broadcast_in_dim | solution.py:74
  (62 shorter events, 77.6 us)
Async XLA Ops:
  0.6 163.6 %copy-start = (bf16[1,4,256,512]{3,2,1,0:T(8,128)(2,1)S(1)}, bf16[1,4,256,512]{3,2,1,0:T(8,128)(2,1)}, u32[]{:S(2)}) copy-start(bf16[1,4,256,512]{3,2,1,0:T(8,128)(2,1)} %param.16) | copy-start | bytes 3145732
  7.3 64.4 %copy-start.11 = (bf16[1,4,256,256]{3,2,1,0:T(8,128)(2,1)S(1)}, bf16[1,4,256,256]{3,2,1,0:T(8,128)(2,1)}, u32[]{:S(2)}) copy-start(bf16[1,4,256,256]{3,2,1,0:T(8,128)(2,1)} %param.12) | copy-start | bytes 1572868
  73.3 9.3 %copy-start.3 = (bf16[1,1024,1024]{2,1,0:T(8,128)(2,1)S(1)}, bf16[1,1024,1024]{2,1,0:T(8,128)(2,1)}, u32[]{:S(2)}) copy-start(bf16[1,1024,1024]{2,1,0:T(8,128)(2,1)} %param.9) | copy-start | bytes 6291460
  76.2 57.4 %all-to-all-start.1 = ((bf16[64,4,4,1024]{3,2,1,0:T(4,128)(2,1)}), bf16[64,4,4,1024]{3,2,1,0:T(4,128)(2,1)}, u32[]{:S(2)}, u32[]{:S(2)}) async-start(bf16[64,4,4,1024]{3,2,1,0:T(4,128)(2,1)} %bitcast.111), calls=%async_computation.1 | async-start | bytes 4194304 | tf_op jit(solution)/shard_map/all_to_all | solution.py:53
  103.1 6.2 %copy-start.14 = (f32[1,1024]{1,0:T(1,128)S(1)}, f32[1,1024]{1,0:T(1,128)}, u32[]{:S(2)}) copy-start(f32[1,1024]{1,0:T(1,128)} %param.15) | copy-start | bytes 12292
  103.1 6.9 %copy-start.12 = (f32[1,1024]{1,0:T(1,128)S(1)}, f32[1,1024]{1,0:T(1,128)}, u32[]{:S(2)}) copy-start(f32[1,1024]{1,0:T(1,128)} %param.14) | copy-start | bytes 12292
  103.1 7.6 %copy-start.13 = (f32[1,1024]{1,0:T(1,128)S(1)}, f32[1,1024]{1,0:T(1,128)}, u32[]{:S(2)}) copy-start(f32[1,1024]{1,0:T(1,128)} %param.13) | copy-start | bytes 12292
  136.4 1.9 copy-start.1
  152.7 5.8 %copy-start.6 = (f32[1024,4,256]{2,1,0:T(4,128)S(1)}, f32[1024,4,256]{2,1,0:T(4,128)}, u32[]{:S(2)}) copy-start(f32[1024,4,256]{2,1,0:T(4,128)} %reshape.136) | copy-start | bytes 12582916
  152.7 7.4 %copy-start.7 = (f32[1024,4,256]{2,1,0:T(4,128)S(1)}, f32[1024,4,256]{2,1,0:T(4,128)}, u32[]{:S(2)}) copy-start(f32[1024,4,256]{2,1,0:T(4,128)} %reshape.137) | copy-start | bytes 12582916
  164.3 3.7 copy-start.8
  182.1 48.9 %collective-permute-start = (bf16[1024,1024]{1,0:T(8,128)(2,1)}, bf16[1024,1024]{1,0:T(8,128)(2,1)}, u32[]{:S(2)}, u32[]{:S(2)}) collective-permute-start(bf16[1024,1024]{1,0:T(8,128)(2,1)} %add_convert_fusion.1), channel_id=1, source_target_pairs={{0,64},{64,128},{128,192},{1,65},{65,129},{129,193},{2,66},{66,130... | collective-permute-start | bytes 6291464 | tf_op jit(solution)/shard_map/ppermute | solution.py:12
  185.0 49.2 %copy-start.10 = (bf16[1,4,256,256]{3,2,1,0:T(8,128)(2,1)S(1)}, bf16[1,4,256,256]{3,2,1,0:T(8,128)(2,1)}, u32[]{:S(2)}) copy-start(bf16[1,4,256,256]{3,2,1,0:T(8,128)(2,1)} %param.11) | copy-start | bytes 1572868
  232.9 1.3 copy-start.4
  244.5 57.8 %all-to-all-start.2 = ((bf16[4,64,4,1024]{3,2,0,1:T(4,128)(2,1)}), bf16[4,64,4,1024]{3,2,0,1:T(4,128)(2,1)}, u32[]{:S(2)}, u32[]{:S(2)}) async-start(bf16[4,64,4,1024]{3,2,0,1:T(4,128)(2,1)} %copy.74), calls=%async_computation.2 | async-start | bytes 4194304 | tf_op jit(solution)/shard_map/all_to_all | solution.py:48
  315.2 57.4 %all-to-all-start.3 = ((bf16[64,4,4,1024]{3,1,2,0:T(4,128)(2,1)}), bf16[64,4,4,1024]{3,1,2,0:T(4,128)(2,1)}, u32[]{:S(2)}, u32[]{:S(2)}) async-start(bf16[64,4,4,1024]{3,1,2,0:T(4,128)(2,1)} %copy.76), calls=%async_computation.3 | async-start | bytes 4194304 | tf_op jit(solution)/shard_map/all_to_all | solution.py:53
  380.1 5.4 %copy-start.5 = (bf16[1024,1024]{1,0:T(8,128)(2,1)S(1)}, bf16[1024,1024]{1,0:T(8,128)(2,1)}, u32[]{:S(2)}) copy-start(bf16[1024,1024]{1,0:T(8,128)(2,1)} %copy-done.4) | copy-start | bytes 6291460
  389.3 1.9 copy-start.2
  391.7 3.3 copy-start.9
where the time goes:
time: 416 us; the launch traced here: 409 us
  waiting for transfers between devices  130 us (31%)
  local copies, waits for them, and re-layouts  93.4 us (22%)
  other arithmetic  74.1 us (18%)
  blocking collectives  63.2 us (15%)
  matrix products  25.6 us (6%)
  starting transfers between devices  22.3 us (5%)
    all_to_all x1, blocking collectives, one_layer(): lax.all_to_all(grouped, 'seq', split_axis=1, concat_axis=0, tiled=True)  63.2 us
    all_to_all x2, waiting for transfers between devices, one_layer(): lax.all_to_all(regrouped, 'seq', split_axis=0, concat_axis=2, tiled=True)  51.9 us
    ppermute x1, waiting for transfers between devices, shifted(): return lax.ppermute(block, axis, route)  46 us
    convert_element_type x6, local copies, waits for them, and re-layouts, channel_part(): mixed_seq = returned.reshape(rows.shape).astype(jnp.float32)  32.9 us
    all_to_all x1, waiting for transfers between devices, one_layer(): lax.all_to_all(grouped, 'seq', split_axis=1, concat_axis=0, tiled=True)  31.6 us
    convert_element_type x2, other arithmetic, channel_part(): input_wide = rows.astype(jnp.float32)  25.7 us
    reshape x3, local copies, waits for them, and re-layouts, channel_part(): return (residual + down_proj.reshape(rows.shape)).astype(jnp.bfloat16)  21.7 us
    convert_element_type x2, other arithmetic, channel_part(): return (residual + down_proj.reshape(rows.shape)).astype(jnp.bfloat16)  19.4 us
  transfers between devices with their start and end apart: 4, of which 4 were waited for; matrix products, arithmetic and copies ran while one was open for 17% of the time, Pallas kernels for 0%

commit v1 on v0

v1 whole, which is shorter than its diff:
```python
import jax
import jax.numpy as jnp
from jax import lax
from jax.experimental import pallas as pl
from jax.experimental.pallas import tpu as pltpu
from jax.sharding import PartitionSpec as P


BLOCK = 256
WIDTH = 1024
DEVICES = 64
F32 = jnp.float32
BF16 = jnp.bfloat16
WHOLE = pl.BlockSpec(memory_space=pltpu.MemorySpace.VMEM)


def params(name):
    return dict(
        name=name,
        compiler_params=pltpu.CompilerParams(vmem_limit_bytes=48 * 1024 * 1024),
    )


def low_half(shape):
    return lax.broadcasted_iota(jnp.int32, shape, 1) < 4


def mix_first_tiles(right_ref, load_rows, blocks):
    tiles = []
    for pair in range(blocks // 2):
        even, odd = (
            jnp.dot(right_ref[block], load_rows(block), preferred_element_type=F32).reshape(
                BLOCK // 8, 8, -1
            )
            for block in (2 * pair, 2 * pair + 1)
        )
        low = low_half(even.shape)
        tiles.append(
            (
                jnp.where(low, even, pltpu.roll(odd, 4, 1)),
                jnp.where(low, pltpu.roll(even, 4, 1), odd),
            )
        )
    ordered = [tiles[pair][parity] for parity in range(2) for pair in range(blocks // 2)]
    return jnp.stack(ordered, axis=1).reshape(blocks * BLOCK, -1)


def first_kernel(right_ref, rows_ref, out_ref):
    blocks = right_ref.shape[0]
    load = lambda block: rows_ref[pl.ds(block * BLOCK, BLOCK), :]
    out_ref[...] = mix_first_tiles(right_ref, load, blocks).astype(BF16)


def mix_first(right, rows, chunk=256):
    blocks = right.shape[0]
    column = pl.BlockSpec((blocks * BLOCK, chunk), lambda c: (0, c))
    return pl.pallas_call(
        first_kernel,
        grid=(WIDTH // chunk,),
        in_specs=[pl.BlockSpec((blocks, BLOCK, BLOCK), lambda c: (0, 0, 0)), column],
        out_specs=column,
        out_shape=jax.ShapeDtypeStruct((blocks * BLOCK, WIDTH), BF16),
        **params("mix_first"),
    )(right, rows)


def select_first_kernel(segment_ref, right_ref, fresh_ref, received_ref, out_ref, current_ref):
    blocks = right_ref.shape[0]

    @pl.when(segment_ref[0] == 0)
    def _():
        current_ref[...] = fresh_ref[...]

    @pl.when(segment_ref[0] != 0)
    def _():
        current_ref[...] = received_ref[...]

    load = lambda block: current_ref[pl.ds(block * BLOCK, BLOCK), :]
    out_ref[...] = mix_first_tiles(right_ref, load, blocks).astype(BF16)


def select_mix_first(segment, right, fresh, received, half, chunk=512):
    rows = 2 * BLOCK
    column = pl.BlockSpec((rows, chunk), lambda c: (0, c))
    return pl.pallas_call(
        select_first_kernel,
        grid=(WIDTH // chunk,),
        in_specs=[
            pl.BlockSpec(memory_space=pltpu.MemorySpace.SMEM),
            pl.BlockSpec((2, BLOCK, BLOCK), lambda c: (half, 0, 0)),
            pl.BlockSpec((rows, chunk), lambda c: (half, c)),
            column,
        ],
        out_specs=(column, column),
        out_shape=(jax.ShapeDtypeStruct((rows, WIDTH), BF16),) * 2,
        **params("select_mix_first"),
    )(segment, right, fresh, received)


def spread(left, rows_order, columns_of):
    size = left.shape[-1]
    rows = rows_order(left).reshape(-1, size)
    source = jnp.repeat(columns_of, 4)
    place = (lax.broadcasted_iota(jnp.int32, (size, 4 * size), 0) == source[None]).astype(BF16)
    full = jnp.dot(rows, place, preferred_element_type=F32)
    row = lax.broadcasted_iota(jnp.int32, full.shape, 0)
    column = lax.broadcasted_iota(jnp.int32, full.shape, 1)
    return jnp.where(row % 4 == column % 4, full, 0.0).astype(BF16)


def spread_by_output_half(left):
    split = lambda a: a.reshape(4, DEVICES, 2, 2, BLOCK).transpose(2, 1, 3, 0, 4)
    return spread(left, split, jnp.arange(BLOCK))


def spread_by_input_half(left):
    order = jnp.arange(BLOCK).reshape(DEVICES, 2, 2).transpose(1, 0, 2).reshape(-1)
    return spread(left, lambda a: a.transpose(1, 0, 2), order)


def second_kernel(left_ref, *refs):
    *parts, out_ref = refs
    depth = left_ref.shape[1] // len(parts)
    total = sum(
        jnp.dot(
            left_ref[:, pl.ds(n * depth, depth)], part[...], preferred_element_type=F32
        )
        for n, part in enumerate(parts)
    )
    out_ref[...] = total.astype(BF16)


def mix_second(left, parts, half, rows, chunk=256):
    return pl.pallas_call(
        second_kernel,
        grid=(WIDTH // chunk,),
        in_specs=[pl.BlockSpec((rows, left.shape[1]), lambda c: (half, 0))]
        + [pl.BlockSpec((part.shape[0], chunk), lambda c: (0, c)) for part in parts],
        out_specs=pl.BlockSpec((rows, chunk), lambda c: (0, c)),
        out_shape=jax.ShapeDtypeStruct((rows, WIDTH), BF16),
        **params("mix_second"),
    )(left, *parts)


def channel_kernel(
    returned_ref, rows_ref, slope_ref, shift_ref, gain_ref, up_ref, down_ref, out_ref
):
    blocks, count, width = rows_ref.shape
    arrived = returned_ref[...].astype(F32).reshape(count // 8, 2, blocks // 2, 8, width)
    mixed = []
    for pair in range(blocks // 2):
        even, odd = arrived[:, 0, pair], arrived[:, 1, pair]
        low = low_half(even.shape)
        mixed.append(jnp.where(low, even, pltpu.roll(odd, 4, 1)).reshape(count, width))
        mixed.append(jnp.where(low, pltpu.roll(even, 4, 1), odd).reshape(count, width))
    for block in range(blocks):
        wide = rows_ref[block].astype(F32)
        gate = 0.5 * jnp.tanh(0.5 * (wide * slope_ref[...] + shift_ref[...])) + 0.5
        residual = wide + mixed[block] * gate
        scale = lax.rsqrt(jnp.mean(residual * residual, axis=-1, keepdims=True) + 1e-06)
        normed = (residual * scale * gain_ref[...]).astype(BF16)
        hidden = []
        for b in range(4):
            up = jnp.dot(normed[:, b * 256 : (b + 1) * 256], up_ref[b], preferred_element_type=F32)
            hidden.append(jax.nn.gelu(up, approximate=True).astype(BF16))
        for k in range(4):
            taken = jnp.concatenate([h[:, k * 128 : (k + 1) * 128] for h in hidden], axis=1)
            down = jnp.dot(taken, down_ref[k], preferred_element_type=F32)
            columns = slice(k * 256, (k + 1) * 256)
            out_ref[block, :, columns] = (residual[:, columns] + down).astype(BF16)


def channel_part(returned, rows, start, channel_weights, count=64):
    blocks = returned.shape[0] // BLOCK
    slope, shift, gain, up, down = channel_weights
    fixed = lambda a: pl.BlockSpec(a.shape, lambda s: (0,) * a.ndim)
    return pl.pallas_call(
        channel_kernel,
        grid=(BLOCK // count,),
        in_specs=[
            pl.BlockSpec((blocks * count, WIDTH), lambda s: (s, 0)),
            pl.BlockSpec((blocks, count, WIDTH), lambda s: (start, s, 0)),
            fixed(slope),
            fixed(shift),
            fixed(gain),
            fixed(up),
            fixed(down),
        ],
        out_specs=pl.BlockSpec((blocks, count, WIDTH), lambda s: (0, s, 0)),
        out_shape=jax.ShapeDtypeStruct((blocks, BLOCK, WIDTH), BF16),
        **params("channel_part"),
    )(returned, rows, *channel_weights).reshape(blocks * BLOCK, WIDTH)


def exchange(rows):
    grouped = rows.reshape(DEVICES, -1, WIDTH)
    return lax.all_to_all(grouped, "seq", split_axis=0, concat_axis=0, tiled=True).reshape(
        rows.shape
    )


def shards(
    in_flight, fresh_rows, right_factor, left_factor, gate_gain, gate_bias, norm_gain, w_up, w_down
):
    segment = lax.axis_index("pipe").reshape(1)
    rows, right, left = in_flight[0], right_factor[0], left_factor[0]
    weights = (gate_gain, gate_bias, norm_gain, w_up[0], w_down[0].reshape(4, 512, 256))
    route = [(n, n + 1) for n in range(lax.axis_size("pipe") - 1)]
    leaving = mix_first(right, rows)
    arrived = exchange(leaving)
    left_held, _ = lax.optimization_barrier((left, leaving))
    left_out = spread_by_output_half(left_held)
    left_in = spread_by_input_half(left_held)
    returned = []
    for half in range(2):
        mixed = mix_second(left_out, (arrived,), half, 512)
        returned.append(exchange(mixed))
    blocked = rows.reshape(4, BLOCK, WIDTH)
    firsts, currents, arrivals = [], [], []
    for half in range(2):
        out = channel_part(returned[half], blocked, half, weights)
        firsts.append(out)
        received = lax.ppermute(out, "pipe", route)
        leaving, current = select_mix_first(segment, right, fresh_rows, received, half)
        currents.append(current)
        arrivals.append(exchange(leaving))
    first_out = jnp.concatenate(firsts)
    current = jnp.concatenate(currents)
    mixed = mix_second(left_in, tuple(arrivals), 0, 1024)
    last = exchange(mixed)
    second_out = channel_part(last, current.reshape(4, BLOCK, WIDTH), 0, weights)
    return first_out[None], second_out[None]


def solution(mesh):
    in_specs = (
        P("pipe", "seq", None),
        P("seq", None),
        P("pipe", "seq", None, None),
        P("pipe", "seq", None, None),
        P("pipe", None),
        P("pipe", None),
        P("pipe", None),
        P("pipe", None, None, None),
        P("pipe", None, None, None, None),
    )
    out_specs = (P("pipe", "seq", None), P("pipe", "seq", None))
    return jax.shard_map(shards, mesh=mesh, in_specs=in_specs, out_specs=out_specs, check_vma=False)
```

time: 416 us -> 320 us (0.77); the launches traced: 409 us -> 319 us
  local copies, waits for them, and re-layouts: 93.4 us -> 21.9 us
  other arithmetic: 74.1 us -> 4.38 us
  blocking collectives: 63.2 us -> 0 us
  waiting for transfers between devices: 130 us -> 186 us
  Pallas kernels: 0 us -> 40.7 us
  starting transfers between devices: 22.3 us -> 59.7 us
  matrix products: 25.6 us -> 5.19 us
    all_to_all x1 -> x0, blocking collectives: 63.2 us -> none  [one_layer(): lax.all_to_all(grouped, 'seq', split_axis=1, concat_axis=0, tiled=True)]
    all_to_all x3 -> x6, waiting for transfers between devices: 83.6 us -> 139 us  [exchange(): lax.all_to_all(grouped, 'seq', split_axis=0, concat_axis=0, tiled=True)]
    convert_element_type x8 -> x0, other arithmetic: 55.4 us -> none  [the longest x2 25.7 us: channel_part(): input_wide = rows.astype(jnp.float32)]
    reshape x10 -> x5, local copies, waits for them, and re-layouts: 45.1 us -> 3.08 us  [the longest x2 2.07 us: spread(): rows = rows_order(left).reshape(-1, size)]
    pallas_call x0 -> x9, Pallas kernels: none -> 40.7 us  [the longest x3 24.9 us: channel_part(): pl.pallas_call(channel_kernel, grid=(BLOCK // count,), in_specs=[pl.Block...]
    convert_element_type x7 -> x0, local copies, waits for them, and re-layouts: 38.6 us -> none  [the longest x6 32.9 us: channel_part(): mixed_seq = returned.reshape(rows.shape).astype(jnp.float32)]
    all_to_all x3 -> x6, starting transfers between devices: 19.4 us -> 53.9 us  [exchange(): lax.all_to_all(grouped, 'seq', split_axis=0, concat_axis=0, tiled=True)]
    dot_general x8 -> x2, matrix products: 25.6 us -> 5.19 us  [spread(): full = jnp.dot(rows, place, preferred_element_type=F32)]
  transfers between devices with their start and end apart: 4 -> 8, of which waited for: 4 -> 6; matrix products, arithmetic and copies ran while one was open for 17% -> 5% of each run, Pallas kernels for 0% -> 6%
where the time goes in v1:
time: 320 us; the launch traced here: 319 us
  waiting for transfers between devices  186 us (58%)
  starting transfers between devices  59.7 us (19%)
  Pallas kernels  40.7 us (13%)
  local copies, waits for them, and re-layouts  21.9 us (7%)
  matrix products  5.19 us (2%)
  other arithmetic  4.38 us (1%)
    all_to_all x6, waiting for transfers between devices, exchange(): lax.all_to_all(grouped, 'seq', split_axis=0, concat_axis=0, tiled=True)  139 us
    all_to_all x6, starting transfers between devices, exchange(): lax.all_to_all(grouped, 'seq', split_axis=0, concat_axis=0, tiled=True)  53.9 us
    ppermute x2, waiting for transfers between devices, shards(): received = lax.ppermute(out, 'pipe', route)  46.6 us
    pallas_call x3, Pallas kernels, channel_part(): pl.pallas_call(channel_kernel, grid=(BLOCK // count,), in_specs=[pl.Block...  24.9 us
    unnamed x50, local copies, waits for them, and re-layouts  16.2 us
    pallas_call x3, Pallas kernels, mix_second(): pl.pallas_call(second_kernel, grid=(WIDTH // chunk,), in_specs=[pl.BlockS...  10.9 us
  transfers between devices with their start and end apart: 8, of which 6 were waited for; matrix products, arithmetic and copies ran while one was open for 5% of the time, Pallas kernels for 6%

profile of v1, /device:TPU:17, one launch (start us, length us, event | category | flops | bytes accessed | tf_op | source)
XLA Modules:
  0.0 318.9 jit_solution(18328890845997566851)
XLA Ops:
  6.4 12.3 %all-to-all-start = ((bf16[64,16,1024]{2,1,0:T(8,128)(2,1)}), bf16[64,16,1024]{2,1,0:T(8,128)(2,1)S(1)}, u32[]{:S(2)}, u32[]{:S(2)}) async-start(bf16[64,16,1024]{2,1,0:T(8,128)(2,1)} %bitcast.43), calls=%async_computation | async-start | bytes 4194304 | tf_op jit(solution)/shard_map/all_to_all | solution.py:197
  19.9 2.1 select_convert_fusion.1.left_ref
  21.9 48.0 %all-to-all-done = bf16[64,16,1024]{2,1,0:T(8,128)(2,1)S(1)} async-done(((bf16[64,16,1024]{2,1,0:T(8,128)(2,1)}), bf16[64,16,1024]{2,1,0:T(8,128)(2,1)S(1)}, u32[]{:S(2)}, u32[]{:S(2)}) %all-to-all-start) | async-done | bytes 2097184 | tf_op jit(solution)/shard_map/all_to_all | solution.py:197
  71.5 3.0 mix_second.3
  74.4 5.8 %all-to-all-start.1 = ((bf16[64,8,1024]{2,1,0:T(8,128)(2,1)}), bf16[64,8,1024]{2,1,0:T(8,128)(2,1)S(1)}, u32[]{:S(2)}, u32[]{:S(2)}) async-start(bf16[64,8,1024]{2,1,0:T(8,128)(2,1)} %bitcast.6), calls=%async_computation.1 | async-start | bytes 2097152 | tf_op jit(solution)/shard_map/all_to_all | solution.py:197
  81.9 3.0 mix_second.4
  84.8 24.0 %all-to-all-done.1 = bf16[64,8,1024]{2,1,0:T(8,128)(2,1)S(1)} async-done(((bf16[64,8,1024]{2,1,0:T(8,128)(2,1)}), bf16[64,8,1024]{2,1,0:T(8,128)(2,1)S(1)}, u32[]{:S(2)}, u32[]{:S(2)}) %all-to-all-start.1) | async-done | bytes 1048608 | tf_op jit(solution)/shard_map/all_to_all | solution.py:197
  108.8 6.4 %all-to-all-start.2 = ((bf16[64,8,1024]{2,1,0:T(8,128)(2,1)}), bf16[64,8,1024]{2,1,0:T(8,128)(2,1)}, u32[]{:S(2)}, u32[]{:S(2)}) async-start(bf16[64,8,1024]{2,1,0:T(8,128)(2,1)} %bitcast.12), calls=%async_computation.2 | async-start | bytes 2097152 | tf_op jit(solution)/shard_map/all_to_all | solution.py:197
  116.5 6.9 %channel_part.3 = bf16[2,256,1024]{2,1,0:T(8,128)(2,1)} custom-call(bf16[512,1024]{1,0:T(8,128)(2,1)S(1)} %bitcast.48, bf16[4,256,1024]{2,1,0:T(8,128)(2,1)} %bitcast.31, f32[1,1024]{1,0:T(1,128)S(1)} %copy-done.21, f32[1,1024]{1,0:T(1,128)S(1)} %copy-done.22, f32[1,1024]{1,0:T(1,128)S(1)} %copy-done.23, bf16[4,256,512]{2,1,0:T(8,128)(2,1)S(1)} %bitcast.36, ...), custom_call_target="tpu_custom_call" | custom-call | tf_op jit(solution)/shard_map/channel_part/pallas_call | solution.py:177
  123.4 2.9 collective-permute-start
  126.3 23.5 %collective-permute-done.received_ref = bf16[512,1024]{1,0:T(8,128)(2,1)} collective-permute-done((bf16[512,1024]{1,0:T(8,128)(2,1)}, bf16[512,1024]{1,0:T(8,128)(2,1)}, u32[]{:S(2)}, u32[]{:S(2)}) %collective-permute-start) | collective-permute-done | bytes 1048608 | tf_op jit(solution)/shard_map/ppermute | solution.py:223
  155.4 11.5 %all-to-all-start.3 = ((bf16[64,8,1024]{2,1,0:T(8,128)(2,1)}), bf16[64,8,1024]{2,1,0:T(8,128)(2,1)}, u32[]{:S(2)}, u32[]{:S(2)}) async-start(bf16[64,8,1024]{2,1,0:T(8,128)(2,1)} %bitcast.52), calls=%async_computation.3 | async-start | bytes 2097152 | tf_op jit(solution)/shard_map/all_to_all | solution.py:197
  167.0 6.5 %channel_part.4 = bf16[2,256,1024]{2,1,0:T(8,128)(2,1)S(1)} custom-call(bf16[512,1024]{1,0:T(8,128)(2,1)} %bitcast.13.returned_ref, bf16[4,256,1024]{2,1,0:T(8,128)(2,1)} %bitcast.32, f32[1,1024]{1,0:T(1,128)S(1)} %copy-done.21, f32[1,1024]{1,0:T(1,128)S(1)} %copy-done.22, f32[1,1024]{1,0:T(1,128)S(1)} %copy-done.23, bf16[4,256,512]{2,1,0:T(8,128)(2,1)S(1)} %bitcast.37, ...), custom_call_target="tpu_custom_call" | custom-call | tf_op jit(solution)/shard_map/channel_part/pallas_call | solution.py:177
  174.4 2.9 collective-permute-start.1
  177.3 23.2 %collective-permute-done.1.received_ref = bf16[512,1024]{1,0:T(8,128)(2,1)S(1)} collective-permute-done((bf16[512,1024]{1,0:T(8,128)(2,1)S(1)}, bf16[512,1024]{1,0:T(8,128)(2,1)S(1)}, u32[]{:S(2)}, u32[]{:S(2)}) %collective-permute-start.1) | collective-permute-done | bytes 1048608 | tf_op jit(solution)/shard_map/ppermute | solution.py:223
  203.6 11.3 %all-to-all-start.4 = ((bf16[64,8,1024]{2,1,0:T(8,128)(2,1)}), bf16[64,8,1024]{2,1,0:T(8,128)(2,1)S(1)}, u32[]{:S(2)}, u32[]{:S(2)}) async-start(bf16[64,8,1024]{2,1,0:T(8,128)(2,1)} %bitcast.51), calls=%async_computation.4 | async-start | bytes 2097152 | tf_op jit(solution)/shard_map/all_to_all | solution.py:197
  215.3 2.2 copy.12
  219.5 3.1 select_convert_fusion.left_ref
  222.6 20.8 %all-to-all-done.4 = bf16[64,8,1024]{2,1,0:T(8,128)(2,1)S(1)} async-done(((bf16[64,8,1024]{2,1,0:T(8,128)(2,1)}), bf16[64,8,1024]{2,1,0:T(8,128)(2,1)S(1)}, u32[]{:S(2)}, u32[]{:S(2)}) %all-to-all-start.4) | async-done | bytes 1048608 | tf_op jit(solution)/shard_map/all_to_all | solution.py:197
  243.4 5.0 %mix_second.5 = bf16[1024,1024]{1,0:T(8,128)(2,1)S(1)} custom-call(bf16[1024,1024]{1,0:T(8,128)(2,1)} %select_convert_fusion.left_ref, bf16[512,1024]{1,0:T(8,128)(2,1)} %bitcast.19.refs_0_, bf16[512,1024]{1,0:T(8,128)(2,1)S(1)} %bitcast.47), custom_call_target="tpu_custom_call" | custom-call | tf_op jit(solution)/shard_map/mix_second/pallas_call | solution.py:134
  249.8 6.5 %all-to-all-start.5 = ((bf16[64,16,1024]{2,1,0:T(8,128)(2,1)}), bf16[64,16,1024]{2,1,0:T(8,128)(2,1)}, u32[]{:S(2)}, u32[]{:S(2)}) async-start(bf16[64,16,1024]{2,1,0:T(8,128)(2,1)} %bitcast.42), calls=%async_computation.5 | async-start | bytes 4194304 | tf_op jit(solution)/shard_map/all_to_all | solution.py:197
  256.3 2.9 maximum_bitcast_fusion
  260.7 46.7 %all-to-all-done.5 = bf16[64,16,1024]{2,1,0:T(8,128)(2,1)} async-done(((bf16[64,16,1024]{2,1,0:T(8,128)(2,1)}), bf16[64,16,1024]{2,1,0:T(8,128)(2,1)}, u32[]{:S(2)}, u32[]{:S(2)}) %all-to-all-start.5) | async-done | bytes 2097184 | tf_op jit(solution)/shard_map/all_to_all | solution.py:197
  307.4 11.5 %channel_part.5 = bf16[4,256,1024]{2,1,0:T(8,128)(2,1)} custom-call(bf16[1024,1024]{1,0:T(8,128)(2,1)} %bitcast.23.returned_ref, bf16[4,256,1024]{2,1,0:T(8,128)(2,1)} %bitcast.53, f32[1,1024]{1,0:T(1,128)S(1)} %copy-done.21, f32[1,1024]{1,0:T(1,128)S(1)} %copy-done.22, f32[1,1024]{1,0:T(1,128)S(1)} %copy-done.23, bf16[4,256,512]{2,1,0:T(8,128)(2,1)S(1)} %bitcast.38, ...), custom_call_target="tpu_custom_call" | custom-call | tf_op jit(solution)/shard_map/channel_part/pallas_call | solution.py:177
  (68 shorter events, 26.0 us)
Async XLA Ops:
  0.6 1.6 copy-start
  6.4 12.4 %copy-start.24 = (bf16[1,4,256,256]{3,2,1,0:T(8,128)(2,1)S(1)}, bf16[1,4,256,256]{3,2,1,0:T(8,128)(2,1)}, u32[]{:S(2)}) copy-start(bf16[1,4,256,256]{3,2,1,0:T(8,128)(2,1)} %param.12) | copy-start | bytes 1572868
  6.4 63.5 %all-to-all-start = ((bf16[64,16,1024]{2,1,0:T(8,128)(2,1)}), bf16[64,16,1024]{2,1,0:T(8,128)(2,1)S(1)}, u32[]{:S(2)}, u32[]{:S(2)}) async-start(bf16[64,16,1024]{2,1,0:T(8,128)(2,1)} %bitcast.43), calls=%async_computation | async-start | bytes 4194304 | tf_op jit(solution)/shard_map/all_to_all | solution.py:197
  69.9 1.6 copy-start.7
  74.4 34.4 %all-to-all-start.1 = ((bf16[64,8,1024]{2,1,0:T(8,128)(2,1)}), bf16[64,8,1024]{2,1,0:T(8,128)(2,1)S(1)}, u32[]{:S(2)}, u32[]{:S(2)}) async-start(bf16[64,8,1024]{2,1,0:T(8,128)(2,1)} %bitcast.6), calls=%async_computation.1 | async-start | bytes 2097152 | tf_op jit(solution)/shard_map/all_to_all | solution.py:197
  80.3 1.6 copy-start.8
  81.9 33.3 %copy-start.23 = (f32[1,1024]{1,0:T(1,128)S(1)}, f32[1,1024]{1,0:T(1,128)}, u32[]{:S(2)}) copy-start(f32[1,1024]{1,0:T(1,128)} %gain_ref.5) | copy-start | bytes 12292
  84.8 30.4 %copy-start.1 = (bf16[1,4,256,512]{3,2,1,0:T(8,128)(2,1)S(1)}, bf16[1,4,256,512]{3,2,1,0:T(8,128)(2,1)}, u32[]{:S(2)}) copy-start(bf16[1,4,256,512]{3,2,1,0:T(8,128)(2,1)} %param.16) | copy-start | bytes 3145732
  84.8 30.4 %copy-start.2 = (bf16[1,4,4,128,256]{4,3,2,1,0:T(8,128)(2,1)S(1)}, bf16[1,4,4,128,256]{4,3,2,1,0:T(8,128)(2,1)}, u32[]{:S(2)}) copy-start(bf16[1,4,4,128,256]{4,3,2,1,0:T(8,128)(2,1)} %param.17) | copy-start | bytes 3145732
  84.8 30.4 %copy-start.21 = (f32[1,1024]{1,0:T(1,128)S(1)}, f32[1,1024]{1,0:T(1,128)}, u32[]{:S(2)}) copy-start(f32[1,1024]{1,0:T(1,128)} %slope_ref.5) | copy-start | bytes 12292
  84.8 30.4 %copy-start.22 = (f32[1,1024]{1,0:T(1,128)S(1)}, f32[1,1024]{1,0:T(1,128)}, u32[]{:S(2)}) copy-start(f32[1,1024]{1,0:T(1,128)} %shift_ref.5) | copy-start | bytes 12292
  108.8 6.4 %copy-start.11 = (bf16[64,8,1024]{2,1,0:T(8,128)(2,1)}, bf16[64,8,1024]{2,1,0:T(8,128)(2,1)S(1)}, u32[]{:S(2)}) copy-start(bf16[64,8,1024]{2,1,0:T(8,128)(2,1)S(1)} %all-to-all-done.1) | copy-start | bytes 3145732
  108.8 46.6 %all-to-all-start.2 = ((bf16[64,8,1024]{2,1,0:T(8,128)(2,1)}), bf16[64,8,1024]{2,1,0:T(8,128)(2,1)}, u32[]{:S(2)}, u32[]{:S(2)}) async-start(bf16[64,8,1024]{2,1,0:T(8,128)(2,1)} %bitcast.12), calls=%async_computation.2 | async-start | bytes 2097152 | tf_op jit(solution)/shard_map/all_to_all | solution.py:197
  116.5 33.3 %copy-start.10 = (bf16[1,4,256,256]{3,2,1,0:T(8,128)(2,1)S(1)}, bf16[1,4,256,256]{3,2,1,0:T(8,128)(2,1)}, u32[]{:S(2)}) copy-start(bf16[1,4,256,256]{3,2,1,0:T(8,128)(2,1)} %param.11) | copy-start | bytes 1572868
  123.4 26.4 %collective-permute-start = (bf16[512,1024]{1,0:T(8,128)(2,1)}, bf16[512,1024]{1,0:T(8,128)(2,1)}, u32[]{:S(2)}, u32[]{:S(2)}) collective-permute-start(bf16[512,1024]{1,0:T(8,128)(2,1)} %bitcast.11), channel_id=1, source_target_pairs={{0,64},{64,128},{128,192},{1,65},{65,129},{129,193},{2,66},{66,130... | collective-permute-start | bytes 3145736 | tf_op jit(solution)/shard_map/ppermute | solution.py:223
  149.8 1.6 copy-start.4
  155.4 48.2 %all-to-all-start.3 = ((bf16[64,8,1024]{2,1,0:T(8,128)(2,1)}), bf16[64,8,1024]{2,1,0:T(8,128)(2,1)}, u32[]{:S(2)}, u32[]{:S(2)}) async-start(bf16[64,8,1024]{2,1,0:T(8,128)(2,1)} %bitcast.52), calls=%async_computation.3 | async-start | bytes 2097152 | tf_op jit(solution)/shard_map/all_to_all | solution.py:197
  166.9 33.6 %copy-start.5 = (bf16[1024,1024]{1,0:T(8,128)(2,1)S(1)}, bf16[1024,1024]{1,0:T(8,128)(2,1)}, u32[]{:S(2)}) copy-start(bf16[1024,1024]{1,0:T(8,128)(2,1)} %fresh_ref.3) | copy-start | bytes 6291460
  174.4 26.1 %collective-permute-start.1 = (bf16[512,1024]{1,0:T(8,128)(2,1)S(1)}, bf16[512,1024]{1,0:T(8,128)(2,1)S(1)}, u32[]{:S(2)}, u32[]{:S(2)}) collective-permute-start(bf16[512,1024]{1,0:T(8,128)(2,1)S(1)} %bitcast.49), channel_id=1, source_target_pairs={{0,64},{64,128},{128,192},{1,65},{65,129},{129,193},{2,66},{66,130... | collective-permute-start | bytes 3145736 | tf_op jit(solution)/shard_map/ppermute | solution.py:223
  203.6 39.8 %all-to-all-start.4 = ((bf16[64,8,1024]{2,1,0:T(8,128)(2,1)}), bf16[64,8,1024]{2,1,0:T(8,128)(2,1)S(1)}, u32[]{:S(2)}, u32[]{:S(2)}) async-start(bf16[64,8,1024]{2,1,0:T(8,128)(2,1)} %bitcast.51), calls=%async_computation.4 | async-start | bytes 2097152 | tf_op jit(solution)/shard_map/all_to_all | solution.py:197
  249.8 6.5 %copy-start.14 = (bf16[2,256,1024]{2,1,0:T(8,128)(2,1)S(1)}, bf16[2,256,1024]{2,1,0:T(8,128)(2,1)}, u32[]{:S(2)}) copy-start(bf16[2,256,1024]{2,1,0:T(8,128)(2,1)} %copy-done.13) | copy-start | bytes 3145732
  249.8 57.6 %all-to-all-start.5 = ((bf16[64,16,1024]{2,1,0:T(8,128)(2,1)}), bf16[64,16,1024]{2,1,0:T(8,128)(2,1)}, u32[]{:S(2)}, u32[]{:S(2)}) async-start(bf16[64,16,1024]{2,1,0:T(8,128)(2,1)} %bitcast.42), calls=%async_computation.5 | async-start | bytes 4194304 | tf_op jit(solution)/shard_map/all_to_all | solution.py:197
  256.3 2.9 copy-start.18
  256.3 2.9 copy-start.20
  (9 other events, 9.9 us)

commit v2 on v0

v2 whole, which is shorter than its diff:
```python
import functools

import jax
import jax.numpy as jnp
from jax import lax
from jax.experimental import pallas as pl
from jax.experimental.pallas import tpu as pltpu
from jax.sharding import PartitionSpec as P


BLOCK = 256
WIDTH = 1024
DEVICES = 64
F32 = jnp.float32
BF16 = jnp.bfloat16
HBM = pltpu.MemorySpace.HBM
VMEM = pltpu.MemorySpace.VMEM


def in_hbm(array):
    return pltpu.with_memory_space_constraint(array, HBM)


def in_vmem(array):
    return pltpu.with_memory_space_constraint(array, VMEM)


def params(name):
    return dict(
        name=name,
        compiler_params=pltpu.CompilerParams(vmem_limit_bytes=48 * 1024 * 1024),
    )


def low_half(shape):
    return lax.broadcasted_iota(jnp.int32, shape, 1) < 4


def mix_first_tiles(right_ref, load_rows, blocks):
    tiles = []
    for pair in range(blocks // 2):
        even, odd = (
            jnp.dot(right_ref[block], load_rows(block), preferred_element_type=F32).reshape(
                BLOCK // 8, 8, -1
            )
            for block in (2 * pair, 2 * pair + 1)
        )
        low = low_half(even.shape)
        tiles.append(
            (
                jnp.where(low, even, pltpu.roll(odd, 4, 1)),
                jnp.where(low, pltpu.roll(even, 4, 1), odd),
            )
        )
    ordered = [tiles[pair][parity] for parity in range(2) for pair in range(blocks // 2)]
    return jnp.stack(ordered, axis=1).reshape(blocks * BLOCK, -1)


def first_kernel(right_ref, *refs):
    *rows_refs, out_ref = refs
    blocks = right_ref.shape[0]

    def load(block):
        if len(rows_refs) > 1:
            return rows_refs[block][...]
        return rows_refs[0][pl.ds(block * BLOCK, BLOCK), :]

    out_ref[...] = mix_first_tiles(right_ref, load, blocks).astype(BF16)


def mix_first(right, parts, blocks, start, chunk):
    column = lambda rows: pl.BlockSpec((rows, chunk), lambda c: (0, c))
    return pl.pallas_call(
        first_kernel,
        grid=(WIDTH // chunk,),
        in_specs=[pl.BlockSpec((blocks, BLOCK, BLOCK), lambda c: (start, 0, 0))]
        + [column(part.shape[0]) for part in parts],
        out_specs=column(blocks * BLOCK),
        out_shape=HBM((blocks * BLOCK, WIDTH), BF16),
        **params("mix_first"),
    )(in_hbm(right), *parts)


def spread_kernel(half, rows_ref, out_ref):
    size = rows_ref.shape[1]
    chunk = 2 * size
    for start in range(0, out_ref.shape[1], chunk):
        column = start + lax.broadcasted_iota(jnp.int32, (size, chunk), 1)
        if half is None:
            source = column >> 2
        else:
            source = ((column >> 3) << 2) + 2 * half + ((column >> 2) & 1)
        place = jnp.where(lax.broadcasted_iota(jnp.int32, (size, chunk), 0) == source, 1.0, 0.0)
        full = jnp.dot(rows_ref[...], place.astype(BF16), preferred_element_type=F32)
        row = lax.broadcasted_iota(jnp.int32, full.shape, 0)
        offset = lax.broadcasted_iota(jnp.int32, full.shape, 1)
        kept = jnp.where((row & 3) == (offset & 3), full, 0.0)
        out_ref[:, start : start + chunk] = kept.astype(BF16)


def spread(rows, half=None):
    columns = 4 * BLOCK if half is None else 2 * BLOCK
    return pl.pallas_call(
        functools.partial(spread_kernel, half),
        out_shape=VMEM((4 * BLOCK, columns), BF16),
        **params("spread"),
    )(rows)


def rows_by_output_half(left):
    split = left.reshape(4, DEVICES, 2, 2, BLOCK).transpose(2, 1, 3, 0, 4)
    return split.reshape(-1, BLOCK)


def rows_by_output(left):
    return left.transpose(1, 0, 2).reshape(-1, BLOCK)


def second_kernel(start, left_ref, part_ref, *refs):
    *held_refs, out_ref = refs
    left = left_ref[pl.ds(start, out_ref.shape[0]), :]
    total = jnp.dot(left, part_ref[...], preferred_element_type=F32)
    for held_ref in held_refs:
        total = total + held_ref[...]
    out_ref[...] = total.astype(out_ref.dtype)


def mix_second(left, part, start, out_shape, held=(), chunk=256):
    column = lambda rows: pl.BlockSpec((rows, chunk), lambda c: (0, c))
    return pl.pallas_call(
        functools.partial(second_kernel, start),
        grid=(WIDTH // chunk,),
        in_specs=[pl.BlockSpec(memory_space=VMEM), column(part.shape[0])]
        + [column(array.shape[0]) for array in held],
        out_specs=column(out_shape.shape[0]),
        out_shape=out_shape,
        **params("mix_second"),
    )(in_vmem(left), in_vmem(part), *(in_hbm(array) for array in held))


def gelu(u):
    inner = u * (0.7978845608028654 + 0.035677408136300125 * (u * u))
    half = 0.5 * u
    return half + half * jnp.tanh(inner)


def channel_rows(which, arrived, rows_refs, weight_refs):
    slope_ref, shift_ref, gain_ref, up_ref, down_ref = weight_refs
    width = arrived.shape[-1]
    mixed = []
    for place in which:
        even, odd = arrived[:, 0, place // 2], arrived[:, 1, place // 2]
        low = low_half(even.shape)
        if place % 2:
            mixed.append(jnp.where(low, pltpu.roll(even, 4, 1), odd).reshape(-1, width))
        else:
            mixed.append(jnp.where(low, even, pltpu.roll(odd, 4, 1)).reshape(-1, width))
    mixed = jnp.concatenate(mixed)
    wide = jnp.concatenate([ref[...].reshape(-1, width) for ref in rows_refs]).astype(F32)
    gate = 0.5 * jnp.tanh(wide * (0.5 * slope_ref[...]) + 0.5 * shift_ref[...]) + 0.5
    residual = wide + mixed * gate
    scale = lax.rsqrt(jnp.mean(residual * residual, axis=-1, keepdims=True) + 1e-06)
    normed = (residual * scale * gain_ref[...]).astype(BF16)
    hidden = []
    for b in range(4):
        up = jnp.dot(normed[:, b * 256 : (b + 1) * 256], up_ref[b], preferred_element_type=F32)
        hidden.append(gelu(up).astype(BF16))
    out = []
    for k in range(4):
        taken = jnp.concatenate([h[:, k * 128 : (k + 1) * 128] for h in hidden], axis=1)
        down = jnp.dot(taken, down_ref[k], preferred_element_type=F32)
        out.append((residual[:, k * 256 : (k + 1) * 256] + down).astype(BF16))
    return jnp.concatenate(out, axis=1)


def arrived_tiles(returned_ref, pairs):
    width = returned_ref.shape[-1]
    return returned_ref[...].astype(F32).reshape(-1, 2, pairs, 8, width)


def relay_kernel(place, last_ref, returned_ref, rows_ref, fresh_ref, *refs):
    *weight_refs, out_ref, sent_ref = refs
    arrived = arrived_tiles(returned_ref, 1)
    out = channel_rows((place,), arrived, (rows_ref,), weight_refs)
    out_ref[...] = out

    @pl.when(last_ref[0] == 0)
    def _():
        sent_ref[...] = out

    @pl.when(last_ref[0] != 0)
    def _():
        sent_ref[...] = fresh_ref[...]


def fixed(array):
    return pl.BlockSpec(array.shape, lambda s: (0,) * array.ndim)


def channel_relay(last, returned, rows, fresh, block, weights, count=128):
    steps = BLOCK // count
    local = pl.BlockSpec((count, WIDTH), lambda s: (block * steps + s, 0))
    plain = pl.BlockSpec((count, WIDTH), lambda s: (s, 0))
    return pl.pallas_call(
        functools.partial(relay_kernel, block % 2),
        grid=(steps,),
        in_specs=[
            pl.BlockSpec(memory_space=pltpu.MemorySpace.SMEM),
            pl.BlockSpec((2 * count, WIDTH), lambda s: (s, 0)),
            local,
            local,
            *(fixed(array) for array in weights),
        ],
        out_specs=(plain, plain),
        out_shape=(HBM((BLOCK, WIDTH), BF16),) * 2,
        **params("channel_relay"),
    )(last, in_hbm(returned), in_hbm(rows), in_hbm(fresh), *weights)


def last_kernel(returned_ref, *refs):
    *rest, out_ref = refs
    rows_refs, weight_refs = rest[:4], rest[4:]
    arrived = arrived_tiles(returned_ref, 2)
    out = channel_rows((0, 1, 2, 3), arrived, rows_refs, weight_refs)
    out_ref[...] = out.reshape(out_ref.shape)


def channel_last(returned, parts, weights, count=64):
    plain = pl.BlockSpec((count, WIDTH), lambda s: (s, 0))
    return pl.pallas_call(
        last_kernel,
        grid=(BLOCK // count,),
        in_specs=[
            pl.BlockSpec((4 * count, WIDTH), lambda s: (s, 0)),
            *(plain for _ in parts),
            *(fixed(array) for array in weights),
        ],
        out_specs=pl.BlockSpec((4, count, WIDTH), lambda s: (0, s, 0)),
        out_shape=HBM((4, BLOCK, WIDTH), BF16),
        **params("channel_last"),
    )(in_hbm(returned), *parts, *weights)


def exchange(rows):
    grouped = rows.reshape(DEVICES, -1, WIDTH)
    return lax.all_to_all(grouped, "seq", split_axis=0, concat_axis=0, tiled=True).reshape(
        rows.shape
    )


def shards(
    in_flight, fresh_rows, right_factor, left_factor, gate_gain, gate_bias, norm_gain, w_up, w_down
):
    sections = lax.axis_size("pipe")
    last = (lax.axis_index("pipe") == sections - 1).astype(jnp.int32).reshape(1)
    rows, right, left = in_flight[0], right_factor[0], left_factor[0]
    weights = (gate_gain, gate_bias, norm_gain, w_up[0], w_down[0].reshape(4, 512, 256))
    route = [(n, (n + 1) % sections) for n in range(sections)]
    leaving = mix_first(right, (in_hbm(rows),), 4, 0, 256)
    arrived = exchange(leaving)
    left_held, _ = lax.optimization_barrier((left, leaving))
    left_out = spread(rows_by_output_half(left_held))
    by_output = rows_by_output(left_held)
    returned = []
    for half in range(2):
        mixed = mix_second(left_out, arrived, 512 * half, HBM((512, WIDTH), BF16))
        returned.append(exchange(mixed))
    firsts, currents, arrivals = [], [], []
    for half in range(2):
        for block in (2 * half, 2 * half + 1):
            out, sent = channel_relay(last, returned[half], rows, fresh_rows, block, weights)
            firsts.append(out)
            currents.append(in_hbm(lax.ppermute(sent, "pipe", route)))
        leaving = mix_first(right, currents[2 * half :], 2, half, 512)
        arrivals.append(exchange(leaving))
    first_out = jnp.concatenate(firsts)
    left_in = [spread(by_output, half) for half in range(2)]
    partial = mix_second(left_in[0], arrivals[0], 0, HBM((1024, WIDTH), F32))
    mixed = mix_second(
        left_in[1], arrivals[1], 0, HBM((1024, WIDTH), BF16), (partial,)
    )
    final = exchange(mixed)
    second_out = channel_last(final, currents, weights)
    return first_out[None], second_out.reshape(1, 1024, WIDTH)


def solution(mesh):
    in_specs = (
        P("pipe", "seq", None),
        P("seq", None),
        P("pipe", "seq", None, None),
        P("pipe", "seq", None, None),
        P("pipe", None),
        P("pipe", None),
        P("pipe", None),
        P("pipe", None, None, None),
        P("pipe", None, None, None, None),
    )
    out_specs = (P("pipe", "seq", None), P("pipe", "seq", None))
    return jax.shard_map(
        shards, mesh=mesh, in_specs=in_specs, out_specs=out_specs, check_vma=False
    )
```

time: 416 us -> 314 us (0.75)
  local copies, waits for them, and re-layouts: 93.4 us -> 8.94 us
  other arithmetic: 74.1 us -> 2.79 us
  blocking collectives: 63.2 us -> 0 us
  waiting for transfers between devices: 130 us -> 187 us
  Pallas kernels: 0 us -> 53.3 us
  starting transfers between devices: 22.3 us -> 57.3 us
  matrix products: 25.6 us -> 0 us
    all_to_all x1 -> x0, blocking collectives: 63.2 us -> none  [one_layer(): lax.all_to_all(grouped, 'seq', split_axis=1, concat_axis=0, tiled=True)]
    all_to_all x3 -> x6, waiting for transfers between devices: 83.6 us -> 141 us  [exchange(): lax.all_to_all(grouped, 'seq', split_axis=0, concat_axis=0, tiled=True)]
    convert_element_type x8 -> x0, other arithmetic: 55.4 us -> none  [the longest x2 25.7 us: channel_part(): input_wide = rows.astype(jnp.float32)]
    pallas_call x0 -> x15, Pallas kernels: none -> 53.3 us  [the longest x4 17.4 us: mix_second(): pl.pallas_call(functools.partial(second_kernel, start), grid=(WIDTH // ch...]
    reshape x10 -> x4, local copies, waits for them, and re-layouts: 45.1 us -> 2.17 us  [the longest x1 1.16 us: rows_by_output(): return left.transpose(1, 0, 2).reshape(-1, BLOCK)]
    convert_element_type x7 -> x0, local copies, waits for them, and re-layouts: 38.6 us -> none  [the longest x6 32.9 us: channel_part(): mixed_seq = returned.reshape(rows.shape).astype(jnp.float32)]
    all_to_all x3 -> x6, starting transfers between devices: 19.4 us -> 53.9 us  [exchange(): lax.all_to_all(grouped, 'seq', split_axis=0, concat_axis=0, tiled=True)]
    dot_general x8 -> x0, matrix products: 25.6 us -> none  [the longest x2 6.91 us: channel_part(): jnp.einsum('tbd,bdf->tbf', normed.reshape(rows.shape[0], blocks_count, -1...]
  transfers between devices with their start and end apart: 4 -> 10, of which waited for: 4 -> 8; matrix products, arithmetic and copies ran while one was open for 17% -> 2% of each run, Pallas kernels for 0% -> 10%
where the time goes in v2:
time: 314 us; the launch traced here: 310 us
  waiting for transfers between devices  187 us (60%)
  starting transfers between devices  57.3 us (18%)
  Pallas kernels  53.3 us (17%)
  local copies, waits for them, and re-layouts  8.94 us (3%)
    all_to_all x6, waiting for transfers between devices, exchange(): lax.all_to_all(grouped, 'seq', split_axis=0, concat_axis=0, tiled=True)  141 us
    all_to_all x6, starting transfers between devices, exchange(): lax.all_to_all(grouped, 'seq', split_axis=0, concat_axis=0, tiled=True)  53.9 us
    ppermute x4, waiting for transfers between devices, shards(): currents.append(in_hbm(lax.ppermute(sent, 'pipe', route)))  45.2 us
    pallas_call x4, Pallas kernels, mix_second(): pl.pallas_call(functools.partial(second_kernel, start), grid=(WIDTH // ch...  17.4 us
    pallas_call x4, Pallas kernels, channel_relay(): pl.pallas_call(functools.partial(relay_kernel, block % 2), grid=(steps,),...  16.1 us
    pallas_call x3, Pallas kernels, mix_first(): pl.pallas_call(first_kernel, grid=(WIDTH // chunk,), in_specs=[pl.BlockSp...  9.69 us
    pallas_call x1, Pallas kernels, channel_last(): pl.pallas_call(last_kernel, grid=(BLOCK // count,), in_specs=[pl.BlockSpe...  8.45 us
  transfers between devices with their start and end apart: 10, of which 8 were waited for; matrix products, arithmetic and copies ran while one was open for 2% of the time, Pallas kernels for 10%

profile of v2, /device:TPU:17, one launch (start us, length us, event | category | flops | bytes accessed | tf_op | source)
XLA Modules:
  0.0 309.8 jit_solution(7868450354502306281)
XLA Ops:
  0.6 4.5 %mix_first.3 = bf16[1024,1024]{1,0:T(8,128)(2,1)} custom-call(bf16[4,256,256]{2,1,0:T(8,128)(2,1)} %bitcast.47, bf16[1024,1024]{1,0:T(8,128)(2,1)} %bitcast.36), custom_call_target="tpu_custom_call" | custom-call | tf_op jit(solution)/shard_map/mix_first/pallas_call | solution.py:73
  5.1 12.5 %all-to-all-start = ((bf16[64,16,1024]{2,1,0:T(8,128)(2,1)}), bf16[64,16,1024]{2,1,0:T(8,128)(2,1)}, u32[]{:S(2)}, u32[]{:S(2)}) async-start(bf16[64,16,1024]{2,1,0:T(8,128)(2,1)} %bitcast.45), calls=%async_computation | async-start | bytes 4194304 | tf_op jit(solution)/shard_map/all_to_all | solution.py:246
  19.4 49.4 %all-to-all-done = bf16[64,16,1024]{2,1,0:T(8,128)(2,1)} async-done(((bf16[64,16,1024]{2,1,0:T(8,128)(2,1)}), bf16[64,16,1024]{2,1,0:T(8,128)(2,1)}, u32[]{:S(2)}, u32[]{:S(2)}) %all-to-all-start) | async-done | bytes 2097184 | tf_op jit(solution)/shard_map/all_to_all | solution.py:246
  68.7 4.4 %mix_second.4 = bf16[512,1024]{1,0:T(8,128)(2,1)} custom-call(bf16[1024,1024]{1,0:T(8,128)(2,1)S(1)} %spread.3.left_ref, bf16[1024,1024]{1,0:T(8,128)(2,1)} %bitcast.6.part_ref), custom_call_target="tpu_custom_call" | custom-call | tf_op jit(solution)/shard_map/mix_second/pallas_call | solution.py:130
  73.1 5.8 %all-to-all-start.1 = ((bf16[64,8,1024]{2,1,0:T(8,128)(2,1)}), bf16[64,8,1024]{2,1,0:T(8,128)(2,1)S(1)}, u32[]{:S(2)}, u32[]{:S(2)}) async-start(bf16[64,8,1024]{2,1,0:T(8,128)(2,1)} %bitcast.51), calls=%async_computation.1 | async-start | bytes 2097152 | tf_op jit(solution)/shard_map/all_to_all | solution.py:246
  79.0 4.4 %mix_second.5 = bf16[512,1024]{1,0:T(8,128)(2,1)} custom-call(bf16[1024,1024]{1,0:T(8,128)(2,1)S(1)} %spread.3.left_ref, bf16[1024,1024]{1,0:T(8,128)(2,1)} %bitcast.6.part_ref), custom_call_target="tpu_custom_call" | custom-call | tf_op jit(solution)/shard_map/mix_second/pallas_call | solution.py:130
  83.4 24.1 %all-to-all-done.1 = bf16[64,8,1024]{2,1,0:T(8,128)(2,1)S(1)} async-done(((bf16[64,8,1024]{2,1,0:T(8,128)(2,1)}), bf16[64,8,1024]{2,1,0:T(8,128)(2,1)S(1)}, u32[]{:S(2)}, u32[]{:S(2)}) %all-to-all-start.1) | async-done | bytes 1048608 | tf_op jit(solution)/shard_map/all_to_all | solution.py:246
  108.5 6.2 %all-to-all-start.2 = ((bf16[64,8,1024]{2,1,0:T(8,128)(2,1)}), bf16[64,8,1024]{2,1,0:T(8,128)(2,1)S(1)}, u32[]{:S(2)}, u32[]{:S(2)}) async-start(bf16[64,8,1024]{2,1,0:T(8,128)(2,1)} %bitcast.50), calls=%async_computation.2 | async-start | bytes 2097152 | tf_op jit(solution)/shard_map/all_to_all | solution.py:246
  114.7 4.0 %channel_relay.5 = (bf16[256,1024]{1,0:T(8,128)(2,1)}, bf16[256,1024]{1,0:T(8,128)(2,1)}) custom-call(s32[1]{0:T(128)} %bitcast.last_ref, bf16[512,1024]{1,0:T(8,128)(2,1)} %bitcast.43, bf16[1024,1024]{1,0:T(8,128)(2,1)} %bitcast.37, bf16[1024,1024]{1,0:T(8,128)(2,1)} %fresh_ref.7, f32[1,1024]{1,0:T(1,128)S(1)} %copy-done.6, f32[1,1024]{1,0:T(1,128)S(1)} %copy-done.7, ...), custom_call_target="tpu_custom_call" | custom-call | tf_op jit(solution)/shard_map/channel_relay/pallas_call | solution.py:204
  118.7 4.0 %channel_relay.4 = (bf16[256,1024]{1,0:T(8,128)(2,1)}, bf16[256,1024]{1,0:T(8,128)(2,1)}) custom-call(s32[1]{0:T(128)} %bitcast.last_ref, bf16[512,1024]{1,0:T(8,128)(2,1)} %bitcast.44, bf16[1024,1024]{1,0:T(8,128)(2,1)} %bitcast.38, bf16[1024,1024]{1,0:T(8,128)(2,1)} %fresh_ref.7, f32[1,1024]{1,0:T(1,128)S(1)} %copy-done.6, f32[1,1024]{1,0:T(1,128)S(1)} %copy-done.7, ...), custom_call_target="tpu_custom_call" | custom-call | tf_op jit(solution)/shard_map/channel_relay/pallas_call | solution.py:204
  123.9 12.1 %collective-permute-done.2.refs_0_ = bf16[256,1024]{1,0:T(8,128)(2,1)S(1)} collective-permute-done((bf16[256,1024]{1,0:T(8,128)(2,1)}, bf16[256,1024]{1,0:T(8,128)(2,1)S(1)}, u32[]{:S(2)}, u32[]{:S(2)}) %collective-permute-start.2) | collective-permute-done | bytes 524320 | tf_op jit(solution)/shard_map/ppermute | solution.py:273
  136.0 11.2 %collective-permute-done.3.refs_1_ = bf16[256,1024]{1,0:T(8,128)(2,1)S(1)} collective-permute-done((bf16[256,1024]{1,0:T(8,128)(2,1)S(1)}, bf16[256,1024]{1,0:T(8,128)(2,1)S(1)}, u32[]{:S(2)}, u32[]{:S(2)}) %collective-permute-start.3) | collective-permute-done | bytes 524320 | tf_op jit(solution)/shard_map/ppermute | solution.py:273
  151.6 11.3 %all-to-all-start.4 = ((bf16[64,8,1024]{2,1,0:T(8,128)(2,1)}), bf16[64,8,1024]{2,1,0:T(8,128)(2,1)S(1)}, u32[]{:S(2)}, u32[]{:S(2)}) async-start(bf16[64,8,1024]{2,1,0:T(8,128)(2,1)} %bitcast.52), calls=%async_computation.4 | async-start | bytes 2097152 | tf_op jit(solution)/shard_map/all_to_all | solution.py:246
  162.9 4.0 %channel_relay.7 = (bf16[256,1024]{1,0:T(8,128)(2,1)}, bf16[256,1024]{1,0:T(8,128)(2,1)}) custom-call(s32[1]{0:T(128)} %bitcast.last_ref, bf16[512,1024]{1,0:T(8,128)(2,1)} %bitcast.41, bf16[1024,1024]{1,0:T(8,128)(2,1)} %bitcast.39, bf16[1024,1024]{1,0:T(8,128)(2,1)} %fresh_ref.7, f32[1,1024]{1,0:T(1,128)S(1)} %copy-done.6, f32[1,1024]{1,0:T(1,128)S(1)} %copy-done.7, ...), custom_call_target="tpu_custom_call" | custom-call | tf_op jit(solution)/shard_map/channel_relay/pallas_call | solution.py:204
  166.9 4.1 %channel_relay.6 = (bf16[256,1024]{1,0:T(8,128)(2,1)}, bf16[256,1024]{1,0:T(8,128)(2,1)}) custom-call(s32[1]{0:T(128)} %bitcast.last_ref, bf16[512,1024]{1,0:T(8,128)(2,1)} %bitcast.42, bf16[1024,1024]{1,0:T(8,128)(2,1)} %bitcast.40, bf16[1024,1024]{1,0:T(8,128)(2,1)} %fresh_ref.7, f32[1,1024]{1,0:T(1,128)S(1)} %copy-done.6, f32[1,1024]{1,0:T(1,128)S(1)} %copy-done.7, ...), custom_call_target="tpu_custom_call" | custom-call | tf_op jit(solution)/shard_map/channel_relay/pallas_call | solution.py:204
  173.2 10.6 %collective-permute-done.1.refs_1_.refs_3_ = bf16[256,1024]{1,0:T(8,128)(2,1)S(1)} collective-permute-done((bf16[256,1024]{1,0:T(8,128)(2,1)S(1)}, bf16[256,1024]{1,0:T(8,128)(2,1)S(1)}, u32[]{:S(2)}, u32[]{:S(2)}) %collective-permute-start.1) | collective-permute-done | bytes 524320 | tf_op jit(solution)/shard_map/ppermute | solution.py:273
  183.8 11.2 %collective-permute-done.refs_0_.refs_2_ = bf16[256,1024]{1,0:T(8,128)(2,1)S(1)} collective-permute-done((bf16[256,1024]{1,0:T(8,128)(2,1)}, bf16[256,1024]{1,0:T(8,128)(2,1)S(1)}, u32[]{:S(2)}, u32[]{:S(2)}) %collective-permute-start) | collective-permute-done | bytes 524320 | tf_op jit(solution)/shard_map/ppermute | solution.py:273
  198.4 11.6 %all-to-all-start.3 = ((bf16[64,8,1024]{2,1,0:T(8,128)(2,1)}), bf16[64,8,1024]{2,1,0:T(8,128)(2,1)}, u32[]{:S(2)}, u32[]{:S(2)}) async-start(bf16[64,8,1024]{2,1,0:T(8,128)(2,1)} %bitcast.53), calls=%async_computation.3 | async-start | bytes 2097152 | tf_op jit(solution)/shard_map/all_to_all | solution.py:246
  215.4 3.4 %mix_second.6.refs_0_ = f32[1024,1024]{1,0:T(8,128)} custom-call(bf16[1024,512]{1,0:T(8,128)(2,1)S(1)} %spread.5.left_ref, bf16[512,1024]{1,0:T(8,128)(2,1)S(1)} %bitcast.35), custom_call_target="tpu_custom_call" | custom-call | tf_op jit(solution)/shard_map/mix_second/pallas_call | solution.py:130
  218.8 19.7 %all-to-all-done.3 = bf16[64,8,1024]{2,1,0:T(8,128)(2,1)} async-done(((bf16[64,8,1024]{2,1,0:T(8,128)(2,1)}), bf16[64,8,1024]{2,1,0:T(8,128)(2,1)}, u32[]{:S(2)}, u32[]{:S(2)}) %all-to-all-start.3) | async-done | bytes 1048608 | tf_op jit(solution)/shard_map/all_to_all | solution.py:246
  238.5 5.2 %mix_second.7 = bf16[1024,1024]{1,0:T(8,128)(2,1)} custom-call(bf16[1024,512]{1,0:T(8,128)(2,1)S(1)} %copy-done.5, bf16[512,1024]{1,0:T(8,128)(2,1)} %bitcast.16.part_ref, f32[1024,1024]{1,0:T(8,128)} %mix_second.6.refs_0_), custom_call_target="tpu_custom_call" | custom-call | tf_op jit(solution)/shard_map/mix_second/pallas_call | solution.py:130
  243.7 6.5 %all-to-all-start.5 = ((bf16[64,16,1024]{2,1,0:T(8,128)(2,1)}), bf16[64,16,1024]{2,1,0:T(8,128)(2,1)}, u32[]{:S(2)}, u32[]{:S(2)}) async-start(bf16[64,16,1024]{2,1,0:T(8,128)(2,1)} %bitcast.46), calls=%async_computation.5 | async-start | bytes 4194304 | tf_op jit(solution)/shard_map/all_to_all | solution.py:246
  253.0 48.3 %all-to-all-done.5 = bf16[64,16,1024]{2,1,0:T(8,128)(2,1)} async-done(((bf16[64,16,1024]{2,1,0:T(8,128)(2,1)}), bf16[64,16,1024]{2,1,0:T(8,128)(2,1)}, u32[]{:S(2)}, u32[]{:S(2)}) %all-to-all-start.5) | async-done | bytes 2097184 | tf_op jit(solution)/shard_map/all_to_all | solution.py:246
  301.3 8.5 %channel_last.1 = bf16[4,256,1024]{2,1,0:T(8,128)(2,1)} custom-call(bf16[1024,1024]{1,0:T(8,128)(2,1)} %bitcast.20.returned_ref, bf16[256,1024]{1,0:T(8,128)(2,1)} %copy-done.11, bf16[256,1024]{1,0:T(8,128)(2,1)} %copy-done.12, bf16[256,1024]{1,0:T(8,128)(2,1)} %copy-done.14, bf16[256,1024]{1,0:T(8,128)(2,1)} %copy-done.13, f32[1,1024]{1,0:T(1,128)S(1)} %copy-done.6, ...), custom_call_target="tpu_custom_call" | custom-call | tf_op jit(solution)/shard_map/channel_last/pallas_call | solution.py:230
  (57 shorter events, 21.9 us)
Async XLA Ops:
  5.1 12.5 %copy-start.15 = (bf16[1,4,256,256]{3,2,1,0:T(8,128)(2,1)S(1)}, bf16[1,4,256,256]{3,2,1,0:T(8,128)(2,1)}, u32[]{:S(2)}) copy-start(bf16[1,4,256,256]{3,2,1,0:T(8,128)(2,1)} %param.12) | copy-start | bytes 1572868
  5.1 63.6 %all-to-all-start = ((bf16[64,16,1024]{2,1,0:T(8,128)(2,1)}), bf16[64,16,1024]{2,1,0:T(8,128)(2,1)}, u32[]{:S(2)}, u32[]{:S(2)}) async-start(bf16[64,16,1024]{2,1,0:T(8,128)(2,1)} %bitcast.45), calls=%async_computation | async-start | bytes 4194304 | tf_op jit(solution)/shard_map/all_to_all | solution.py:246
  73.1 34.4 %all-to-all-start.1 = ((bf16[64,8,1024]{2,1,0:T(8,128)(2,1)}), bf16[64,8,1024]{2,1,0:T(8,128)(2,1)S(1)}, u32[]{:S(2)}, u32[]{:S(2)}) async-start(bf16[64,8,1024]{2,1,0:T(8,128)(2,1)} %bitcast.51), calls=%async_computation.1 | async-start | bytes 2097152 | tf_op jit(solution)/shard_map/all_to_all | solution.py:246
  83.4 31.3 %copy-start = (bf16[1,4,256,512]{3,2,1,0:T(8,128)(2,1)S(1)}, bf16[1,4,256,512]{3,2,1,0:T(8,128)(2,1)}, u32[]{:S(2)}) copy-start(bf16[1,4,256,512]{3,2,1,0:T(8,128)(2,1)} %param.16) | copy-start | bytes 3145732
  83.4 31.3 %copy-start.1 = (bf16[1,4,4,128,256]{4,3,2,1,0:T(8,128)(2,1)S(1)}, bf16[1,4,4,128,256]{4,3,2,1,0:T(8,128)(2,1)}, u32[]{:S(2)}) copy-start(bf16[1,4,4,128,256]{4,3,2,1,0:T(8,128)(2,1)} %param.17) | copy-start | bytes 3145732
  83.4 31.3 %copy-start.6 = (f32[1,1024]{1,0:T(1,128)S(1)}, f32[1,1024]{1,0:T(1,128)}, u32[]{:S(2)}) copy-start(f32[1,1024]{1,0:T(1,128)} %refs_4_.1) | copy-start | bytes 12292
  83.4 31.3 %copy-start.7 = (f32[1,1024]{1,0:T(1,128)S(1)}, f32[1,1024]{1,0:T(1,128)}, u32[]{:S(2)}) copy-start(f32[1,1024]{1,0:T(1,128)} %refs_5_.1) | copy-start | bytes 12292
  83.4 31.3 %copy-start.8 = (f32[1,1024]{1,0:T(1,128)S(1)}, f32[1,1024]{1,0:T(1,128)}, u32[]{:S(2)}) copy-start(f32[1,1024]{1,0:T(1,128)} %refs_6_.1) | copy-start | bytes 12292
  108.5 42.2 %all-to-all-start.2 = ((bf16[64,8,1024]{2,1,0:T(8,128)(2,1)}), bf16[64,8,1024]{2,1,0:T(8,128)(2,1)S(1)}, u32[]{:S(2)}, u32[]{:S(2)}) async-start(bf16[64,8,1024]{2,1,0:T(8,128)(2,1)} %bitcast.50), calls=%async_computation.2 | async-start | bytes 2097152 | tf_op jit(solution)/shard_map/all_to_all | solution.py:246
  118.7 5.1 %copy-start.18 = (bf16[256,1024]{1,0:T(8,128)(2,1)S(1)}, bf16[256,1024]{1,0:T(8,128)(2,1)}, u32[]{:S(2)}) copy-start(bf16[256,1024]{1,0:T(8,128)(2,1)} %get-tuple-element.19) | copy-start | bytes 1572868
  122.8 13.2 %collective-permute-start.2 = (bf16[256,1024]{1,0:T(8,128)(2,1)}, bf16[256,1024]{1,0:T(8,128)(2,1)S(1)}, u32[]{:S(2)}, u32[]{:S(2)}) collective-permute-start(bf16[256,1024]{1,0:T(8,128)(2,1)} %get-tuple-element.18), channel_id=1, source_target_pairs={{0,64},{64,128},{128,192},{192,0},{1,65},{65,129},{129,193},{193,1... | collective-permute-start | bytes 1572872 | tf_op jit(solution)/shard_map/ppermute | solution.py:273
  123.8 23.4 %collective-permute-start.3 = (bf16[256,1024]{1,0:T(8,128)(2,1)S(1)}, bf16[256,1024]{1,0:T(8,128)(2,1)S(1)}, u32[]{:S(2)}, u32[]{:S(2)}) collective-permute-start(bf16[256,1024]{1,0:T(8,128)(2,1)S(1)} %copy-done.18), channel_id=1, source_target_pairs={{0,64},{64,128},{128,192},{192,0},{1,65},{65,129},{129,193},{193,1... | collective-permute-start | bytes 1572872 | tf_op jit(solution)/shard_map/ppermute | solution.py:273
  136.0 11.2 %copy-start.11 = (bf16[256,1024]{1,0:T(8,128)(2,1)}, bf16[256,1024]{1,0:T(8,128)(2,1)S(1)}, u32[]{:S(2)}) copy-start(bf16[256,1024]{1,0:T(8,128)(2,1)S(1)} %collective-permute-done.2.refs_0_) | copy-start | bytes 1572868
  151.6 46.8 %all-to-all-start.4 = ((bf16[64,8,1024]{2,1,0:T(8,128)(2,1)}), bf16[64,8,1024]{2,1,0:T(8,128)(2,1)S(1)}, u32[]{:S(2)}, u32[]{:S(2)}) async-start(bf16[64,8,1024]{2,1,0:T(8,128)(2,1)} %bitcast.52), calls=%async_computation.4 | async-start | bytes 2097152 | tf_op jit(solution)/shard_map/all_to_all | solution.py:246
  166.9 4.1 %copy-start.19 = (bf16[256,1024]{1,0:T(8,128)(2,1)S(1)}, bf16[256,1024]{1,0:T(8,128)(2,1)}, u32[]{:S(2)}) copy-start(bf16[256,1024]{1,0:T(8,128)(2,1)} %get-tuple-element.17) | copy-start | bytes 1572868
  171.0 12.9 %collective-permute-start.1 = (bf16[256,1024]{1,0:T(8,128)(2,1)S(1)}, bf16[256,1024]{1,0:T(8,128)(2,1)S(1)}, u32[]{:S(2)}, u32[]{:S(2)}) collective-permute-start(bf16[256,1024]{1,0:T(8,128)(2,1)S(1)} %copy-done.19), channel_id=1, source_target_pairs={{0,64},{64,128},{128,192},{192,0},{1,65},{65,129},{129,193},{193,1... | collective-permute-start | bytes 1572872 | tf_op jit(solution)/shard_map/ppermute | solution.py:273
  172.1 23.0 %collective-permute-start = (bf16[256,1024]{1,0:T(8,128)(2,1)}, bf16[256,1024]{1,0:T(8,128)(2,1)S(1)}, u32[]{:S(2)}, u32[]{:S(2)}) collective-permute-start(bf16[256,1024]{1,0:T(8,128)(2,1)} %get-tuple-element.16), channel_id=1, source_target_pairs={{0,64},{64,128},{128,192},{192,0},{1,65},{65,129},{129,193},{193,1... | collective-permute-start | bytes 1572872 | tf_op jit(solution)/shard_map/ppermute | solution.py:273
  183.8 11.2 %copy-start.13 = (bf16[256,1024]{1,0:T(8,128)(2,1)}, bf16[256,1024]{1,0:T(8,128)(2,1)S(1)}, u32[]{:S(2)}) copy-start(bf16[256,1024]{1,0:T(8,128)(2,1)S(1)} %collective-permute-done.1.refs_1_.refs_3_) | copy-start | bytes 1572868
  198.4 11.6 %copy-start.2 = (bf16[64,8,1024]{2,1,0:T(8,128)(2,1)}, bf16[64,8,1024]{2,1,0:T(8,128)(2,1)S(1)}, u32[]{:S(2)}) copy-start(bf16[64,8,1024]{2,1,0:T(8,128)(2,1)S(1)} %all-to-all-done.4) | copy-start | bytes 3145732
  198.4 40.1 %all-to-all-start.3 = ((bf16[64,8,1024]{2,1,0:T(8,128)(2,1)}), bf16[64,8,1024]{2,1,0:T(8,128)(2,1)}, u32[]{:S(2)}, u32[]{:S(2)}) async-start(bf16[64,8,1024]{2,1,0:T(8,128)(2,1)} %bitcast.53), calls=%async_computation.3 | async-start | bytes 2097152 | tf_op jit(solution)/shard_map/all_to_all | solution.py:246
  215.4 23.1 %copy-start.5 = (bf16[1024,512]{1,0:T(8,128)(2,1)S(1)}, bf16[1024,512]{1,0:T(8,128)(2,1)}, u32[]{:S(2)}) copy-start(bf16[1024,512]{1,0:T(8,128)(2,1)} %copy-done.4) | copy-start | bytes 3145732
  243.7 6.5 %copy-start.16 = (bf16[256,1024]{1,0:T(8,128)(2,1)S(1)}, bf16[256,1024]{1,0:T(8,128)(2,1)}, u32[]{:S(2)}) copy-start(bf16[256,1024]{1,0:T(8,128)(2,1)} %get-tuple-element.13) | copy-start | bytes 1572868
  243.7 6.6 %copy-start.17 = (bf16[256,1024]{1,0:T(8,128)(2,1)S(1)}, bf16[256,1024]{1,0:T(8,128)(2,1)}, u32[]{:S(2)}) copy-start(bf16[256,1024]{1,0:T(8,128)(2,1)} %get-tuple-element.12) | copy-start | bytes 1572868
  243.7 57.7 %all-to-all-start.5 = ((bf16[64,16,1024]{2,1,0:T(8,128)(2,1)}), bf16[64,16,1024]{2,1,0:T(8,128)(2,1)}, u32[]{:S(2)}, u32[]{:S(2)}) async-start(bf16[64,16,1024]{2,1,0:T(8,128)(2,1)} %bitcast.46), calls=%async_computation.5 | async-start | bytes 4194304 | tf_op jit(solution)/shard_map/all_to_all | solution.py:246
  (6 other events, 6.4 us)

commit v3 on v2

--- a/solution.py
+++ b/solution.py
@@ -56,29 +56,59 @@
     return jnp.stack(ordered, axis=1).reshape(blocks * BLOCK, -1)
 
 
-def first_kernel(right_ref, *refs):
-    *rows_refs, out_ref = refs
-    blocks = right_ref.shape[0]
-
-    def load(block):
-        if len(rows_refs) > 1:
-            return rows_refs[block][...]
-        return rows_refs[0][pl.ds(block * BLOCK, BLOCK), :]
-
-    out_ref[...] = mix_first_tiles(right_ref, load, blocks).astype(BF16)
-
-
-def mix_first(right, parts, blocks, start, chunk):
-    column = lambda rows: pl.BlockSpec((rows, chunk), lambda c: (0, c))
+def first_kernel(right_ref, rows_ref, out_ref):
+    load = lambda block: rows_ref[pl.ds(block * BLOCK, BLOCK), :]
+    out_ref[...] = mix_first_tiles(right_ref, load, right_ref.shape[0]).astype(BF16)
+
+
+def mix_first(right, rows, chunk=256):
+    column = pl.BlockSpec((rows.shape[0], chunk), lambda c: (0, c))
     return pl.pallas_call(
         first_kernel,
         grid=(WIDTH // chunk,),
-        in_specs=[pl.BlockSpec((blocks, BLOCK, BLOCK), lambda c: (start, 0, 0))]
-        + [column(part.shape[0]) for part in parts],
-        out_specs=column(blocks * BLOCK),
-        out_shape=HBM((blocks * BLOCK, WIDTH), BF16),
+        in_specs=[pl.BlockSpec(right.shape, lambda c: (0, 0, 0)), column],
+        out_specs=column,
+        out_shape=HBM(rows.shape, BF16),
         **params("mix_first"),
-    )(in_hbm(right), *parts)
+    )(in_hbm(right), in_hbm(rows))
+
+
+def relayed_kernel(half, chunk, section_ref, right_ref, fresh_ref, *refs):
+    *received_refs, out_ref, current_ref, sem = refs
+    columns = pl.ds(pl.program_id(0) * chunk, chunk)
+
+    @pl.when(section_ref[0] == 0)
+    def _():
+        source = fresh_ref.at[pl.ds(2 * half * BLOCK, 2 * BLOCK), columns]
+        copy = pltpu.make_async_copy(source, current_ref, sem)
+        copy.start()
+        copy.wait()
+
+    @pl.when(section_ref[0] != 0)
+    def _():
+        for block, received_ref in enumerate(received_refs):
+            current_ref[pl.ds(block * BLOCK, BLOCK), :] = received_ref[:, columns]
+
+    load = lambda block: current_ref[pl.ds(block * BLOCK, BLOCK), :]
+    out_ref[...] = mix_first_tiles(right_ref, load, 2).astype(BF16)
+
+
+def mix_first_relayed(section, right, fresh, received, half, chunk=512):
+    column = pl.BlockSpec((2 * BLOCK, chunk), lambda c: (0, c))
+    return pl.pallas_call(
+        functools.partial(relayed_kernel, half, chunk),
+        grid=(WIDTH // chunk,),
+        in_specs=[
+            pl.BlockSpec(memory_space=pltpu.MemorySpace.SMEM),
+            pl.BlockSpec((2, BLOCK, BLOCK), lambda c: (half, 0, 0)),
+            pl.BlockSpec(memory_space=pl.ANY),
+            *(pl.BlockSpec(memory_space=VMEM) for _ in received),
+        ],
+        out_specs=(column, column),
+        out_shape=(HBM((2 * BLOCK, WIDTH), BF16),) * 2,
+        scratch_shapes=[pltpu.SemaphoreType.DMA],
+        **params("mix_first_relayed"),
+    )(section, right, in_hbm(fresh), *(in_vmem(part) for part in received))
 
 
 def spread_kernel(half, rows_ref, out_ref):
@@ -102,7 +132,7 @@
     columns = 4 * BLOCK if half is None else 2 * BLOCK
     return pl.pallas_call(
         functools.partial(spread_kernel, half),
-        out_shape=VMEM((4 * BLOCK, columns), BF16),
+        out_shape=VMEM((rows.shape[0], columns), BF16),
         **params("spread"),
     )(rows)
 
@@ -116,19 +146,18 @@
     return left.transpose(1, 0, 2).reshape(-1, BLOCK)
 
 
-def second_kernel(start, left_ref, part_ref, *refs):
+def second_kernel(left_ref, part_ref, *refs):
     *held_refs, out_ref = refs
-    left = left_ref[pl.ds(start, out_ref.shape[0]), :]
-    total = jnp.dot(left, part_ref[...], preferred_element_type=F32)
+    total = jnp.dot(left_ref[...], part_ref[...], preferred_element_type=F32)
     for held_ref in held_refs:
         total = total + held_ref[...]
     out_ref[...] = total.astype(out_ref.dtype)
 
 
-def mix_second(left, part, start, out_shape, held=(), chunk=256):
+def mix_second(left, part, out_shape, held=(), chunk=256):
     column = lambda rows: pl.BlockSpec((rows, chunk), lambda c: (0, c))
     return pl.pallas_call(
-        functools.partial(second_kernel, start),
+        second_kernel,
         grid=(WIDTH // chunk,),
         in_specs=[pl.BlockSpec(memory_space=VMEM), column(part.shape[0])]
         + [column(array.shape[0]) for array in held],
@@ -178,67 +207,54 @@
     return returned_ref[...].astype(F32).reshape(-1, 2, pairs, 8, width)
 
 
-def relay_kernel(place, last_ref, returned_ref, rows_ref, fresh_ref, *refs):
-    *weight_refs, out_ref, sent_ref = refs
+def relay_kernel(place, returned_ref, rows_ref, *refs):
+    *weight_refs, out_ref = refs
     arrived = arrived_tiles(returned_ref, 1)
-    out = channel_rows((place,), arrived, (rows_ref,), weight_refs)
-    out_ref[...] = out
-
-    @pl.when(last_ref[0] == 0)
-    def _():
-        sent_ref[...] = out
-
-    @pl.when(last_ref[0] != 0)
-    def _():
-        sent_ref[...] = fresh_ref[...]
+    out_ref[...] = channel_rows((place,), arrived, (rows_ref,), weight_refs)
 
 
 def fixed(array):
     return pl.BlockSpec(array.shape, lambda s: (0,) * array.ndim)
 
 
-def channel_relay(last, returned, rows, fresh, block, weights, count=128):
+def channel_relay(returned, rows, block, weights, count=128):
     steps = BLOCK // count
-    local = pl.BlockSpec((count, WIDTH), lambda s: (block * steps + s, 0))
-    plain = pl.BlockSpec((count, WIDTH), lambda s: (s, 0))
     return pl.pallas_call(
         functools.partial(relay_kernel, block % 2),
         grid=(steps,),
         in_specs=[
-            pl.BlockSpec(memory_space=pltpu.MemorySpace.SMEM),
             pl.BlockSpec((2 * count, WIDTH), lambda s: (s, 0)),
-            local,
-            local,
+            pl.BlockSpec((count, WIDTH), lambda s: (block * steps + s, 0)),
             *(fixed(array) for array in weights),
         ],
-        out_specs=(plain, plain),
-        out_shape=(HBM((BLOCK, WIDTH), BF16),) * 2,
+        out_specs=pl.BlockSpec((count, WIDTH), lambda s: (s, 0)),
+        out_shape=HBM((BLOCK, WIDTH), BF16),
         **params("channel_relay"),
-    )(last, in_hbm(returned), in_hbm(rows), in_hbm(fresh), *weights)
+    )(in_vmem(returned) if block % 2 == 0 else in_hbm(returned), in_hbm(rows), *weights)
 
 
 def last_kernel(returned_ref, *refs):
     *rest, out_ref = refs
-    rows_refs, weight_refs = rest[:4], rest[4:]
+    rows_refs, weight_refs = rest[:2], rest[2:]
     arrived = arrived_tiles(returned_ref, 2)
     out = channel_rows((0, 1, 2, 3), arrived, rows_refs, weight_refs)
     out_ref[...] = out.reshape(out_ref.shape)
 
 
 def channel_last(returned, parts, weights, count=64):
-    plain = pl.BlockSpec((count, WIDTH), lambda s: (s, 0))
+    pair = pl.BlockSpec((2, count, WIDTH), lambda s: (0, s, 0))
     return pl.pallas_call(
         last_kernel,
         grid=(BLOCK // count,),
         in_specs=[
             pl.BlockSpec((4 * count, WIDTH), lambda s: (s, 0)),
-            *(plain for _ in parts),
+            *(pair for _ in parts),
             *(fixed(array) for array in weights),
         ],
         out_specs=pl.BlockSpec((4, count, WIDTH), lambda s: (0, s, 0)),
         out_shape=HBM((4, BLOCK, WIDTH), BF16),
         **params("channel_last"),
-    )(in_hbm(returned), *parts, *weights)
+    )(in_hbm(returned), *(in_hbm(p) for p in parts), *weights)
 
 
 def exchange(rows):
@@ -251,34 +267,34 @@
 def shards(
     in_flight, fresh_rows, right_factor, left_factor, gate_gain, gate_bias, norm_gain, w_up, w_down
 ):
-    sections = lax.axis_size("pipe")
-    last = (lax.axis_index("pipe") == sections - 1).astype(jnp.int32).reshape(1)
+    section = lax.axis_index("pipe").reshape(1)
     rows, right, left = in_flight[0], right_factor[0], left_factor[0]
     weights = (gate_gain, gate_bias, norm_gain, w_up[0], w_down[0].reshape(4, 512, 256))
-    route = [(n, (n + 1) % sections) for n in range(sections)]
-    leaving = mix_first(right, (in_hbm(rows),), 4, 0, 256)
+    route = [(n, n + 1) for n in range(lax.axis_size("pipe") - 1)]
+    leaving = mix_first(right, rows)
     arrived = exchange(leaving)
     left_held, _ = lax.optimization_barrier((left, leaving))
-    left_out = spread(rows_by_output_half(left_held))
+    left_out = rows_by_output_half(left_held)
     by_output = rows_by_output(left_held)
     returned = []
     for half in range(2):
-        mixed = mix_second(left_out, arrived, 512 * half, HBM((512, WIDTH), BF16))
+        matrix = spread(left_out[512 * half : 512 * half + 512])
+        mixed = mix_second(matrix, arrived, HBM((512, WIDTH), BF16))
         returned.append(exchange(mixed))
     firsts, currents, arrivals = [], [], []
     for half in range(2):
+        received = []
         for block in (2 * half, 2 * half + 1):
-            out, sent = channel_relay(last, returned[half], rows, fresh_rows, block, weights)
+            out = channel_relay(returned[half], rows, block, weights)
             firsts.append(out)
-            currents.append(in_hbm(lax.ppermute(sent, "pipe", route)))
-        leaving = mix_first(right, currents[2 * half :], 2, half, 512)
+            received.append(lax.ppermute(out, "pipe", route))
+        leaving, current = mix_first_relayed(section, right, fresh_rows, received, half)
+        currents.append(current.reshape(2, BLOCK, WIDTH))
         arrivals.append(exchange(leaving))
     first_out = jnp.concatenate(firsts)
     left_in = [spread(by_output, half) for half in range(2)]
-    partial = mix_second(left_in[0], arrivals[0], 0, HBM((1024, WIDTH), F32))
-    mixed = mix_second(
-        left_in[1], arrivals[1], 0, HBM((1024, WIDTH), BF16), (partial,)
-    )
+    partial = mix_second(left_in[0], arrivals[0], HBM((1024, WIDTH), F32))
+    mixed = mix_second(left_in[1], arrivals[1], HBM((1024, WIDTH), BF16), (partial,))
     final = exchange(mixed)
     second_out = channel_last(final, currents, weights)
     return first_out[None], second_out.reshape(1, 1024, WIDTH)

time: 314 us -> 314 us (level)
  starting transfers between devices: 57.3 us -> 63.8 us
    ppermute x4, starting transfers between devices: 3.39 us -> 9.77 us  [shards(): received.append(lax.ppermute(out, 'pipe', route))]
    pallas_call x3 -> x1, Pallas kernels: 9.69 us -> 4.5 us  [mix_first(): pl.pallas_call(first_kernel, grid=(WIDTH // chunk,), in_specs=[pl.BlockSp...]
    pallas_call x7 -> x10, Pallas kernels: 19 us -> 22.1 us  [the longest x4 16 us: mix_second(): pl.pallas_call(second_kernel, grid=(WIDTH // chunk,), in_specs=[pl.BlockS...]
  transfers between devices with their start and end apart: 10 -> 10, of which waited for: 8 -> 8; matrix products, arithmetic and copies ran while one was open for 2% -> 2% of each run, Pallas kernels for 10% -> 9%
where the time goes in v3:
time: 314 us; the launch traced here: 311 us
  waiting for transfers between devices  185 us (59%)
  starting transfers between devices  63.8 us (20%)
  Pallas kernels  50.4 us (16%)
  local copies, waits for them, and re-layouts  7.63 us (2%)
    all_to_all x6, waiting for transfers between devices, exchange(): lax.all_to_all(grouped, 'seq', split_axis=0, concat_axis=0, tiled=True)  142 us
    all_to_all x6, starting transfers between devices, exchange(): lax.all_to_all(grouped, 'seq', split_axis=0, concat_axis=0, tiled=True)  54 us
    ppermute x4, waiting for transfers between devices, shards(): received.append(lax.ppermute(out, 'pipe', route))  43.1 us
    pallas_call x4, Pallas kernels, mix_second(): pl.pallas_call(second_kernel, grid=(WIDTH // chunk,), in_specs=[pl.BlockS...  16 us
    pallas_call x4, Pallas kernels, channel_relay(): pl.pallas_call(functools.partial(relay_kernel, block % 2), grid=(steps,),...  15.2 us
    ppermute x4, starting transfers between devices, shards(): received.append(lax.ppermute(out, 'pipe', route))  9.77 us
    pallas_call x1, Pallas kernels, channel_last(): pl.pallas_call(last_kernel, grid=(BLOCK // count,), in_specs=[pl.BlockSpe...  8.56 us
  transfers between devices with their start and end apart: 10, of which 8 were waited for; matrix products, arithmetic and copies ran while one was open for 2% of the time, Pallas kernels for 9%

profile of v3, /device:TPU:17, one launch (start us, length us, event | category | flops | bytes accessed | tf_op | source)
XLA Modules:
  0.0 311.0 jit_solution(3613625208497345274)
XLA Ops:
  0.6 4.5 %mix_first.1 = bf16[1024,1024]{1,0:T(8,128)(2,1)} custom-call(bf16[4,256,256]{2,1,0:T(8,128)(2,1)} %bitcast.43, bf16[1024,1024]{1,0:T(8,128)(2,1)} %bitcast.46), custom_call_target="tpu_custom_call" | custom-call | tf_op jit(solution)/shard_map/mix_first/pallas_call | solution.py:66
  5.1 12.3 %all-to-all-start = ((bf16[64,16,1024]{2,1,0:T(8,128)(2,1)}), bf16[64,16,1024]{2,1,0:T(8,128)(2,1)S(1)}, u32[]{:S(2)}, u32[]{:S(2)}) async-start(bf16[64,16,1024]{2,1,0:T(8,128)(2,1)} %bitcast.51), calls=%async_computation | async-start | bytes 4194304 | tf_op jit(solution)/shard_map/all_to_all | solution.py:262
  19.7 48.9 %all-to-all-done = bf16[64,16,1024]{2,1,0:T(8,128)(2,1)S(1)} async-done(((bf16[64,16,1024]{2,1,0:T(8,128)(2,1)}), bf16[64,16,1024]{2,1,0:T(8,128)(2,1)S(1)}, u32[]{:S(2)}, u32[]{:S(2)}) %all-to-all-start) | async-done | bytes 2097184 | tf_op jit(solution)/shard_map/all_to_all | solution.py:262
  71.6 5.8 %all-to-all-start.1 = ((bf16[64,8,1024]{2,1,0:T(8,128)(2,1)}), bf16[64,8,1024]{2,1,0:T(8,128)(2,1)S(1)}, u32[]{:S(2)}, u32[]{:S(2)}) async-start(bf16[64,8,1024]{2,1,0:T(8,128)(2,1)} %bitcast.54), calls=%async_computation.1 | async-start | bytes 2097152 | tf_op jit(solution)/shard_map/all_to_all | solution.py:262
  78.9 3.0 mix_second.5
  81.9 24.0 %all-to-all-done.1 = bf16[64,8,1024]{2,1,0:T(8,128)(2,1)S(1)} async-done(((bf16[64,8,1024]{2,1,0:T(8,128)(2,1)}), bf16[64,8,1024]{2,1,0:T(8,128)(2,1)S(1)}, u32[]{:S(2)}, u32[]{:S(2)}) %all-to-all-start.1) | async-done | bytes 1048608 | tf_op jit(solution)/shard_map/all_to_all | solution.py:262
  106.9 6.2 %all-to-all-start.2 = ((bf16[64,8,1024]{2,1,0:T(8,128)(2,1)}), bf16[64,8,1024]{2,1,0:T(8,128)(2,1)S(1)}, u32[]{:S(2)}, u32[]{:S(2)}) async-start(bf16[64,8,1024]{2,1,0:T(8,128)(2,1)} %bitcast.53), calls=%async_computation.2 | async-start | bytes 2097152 | tf_op jit(solution)/shard_map/all_to_all | solution.py:262
  113.2 3.9 %channel_relay.5 = bf16[256,1024]{1,0:T(8,128)(2,1)} custom-call(bf16[512,1024]{1,0:T(8,128)(2,1)} %bitcast.41, bf16[1024,1024]{1,0:T(8,128)(2,1)} %bitcast.47, f32[1,1024]{1,0:T(1,128)S(1)} %copy-done.10, f32[1,1024]{1,0:T(1,128)S(1)} %copy-done.11, f32[1,1024]{1,0:T(1,128)S(1)} %copy-done.12, bf16[4,256,512]{2,1,0:T(8,128)(2,1)S(1)} %bitcast.27, ...), custom_call_target="tpu_custom_call" | custom-call | tf_op jit(solution)/shard_map/channel_relay/pallas_call | solution.py:222
  117.1 3.7 %channel_relay.4 = bf16[256,1024]{1,0:T(8,128)(2,1)} custom-call(bf16[512,1024]{1,0:T(8,128)(2,1)S(1)} %bitcast.42, bf16[1024,1024]{1,0:T(8,128)(2,1)} %bitcast.48, f32[1,1024]{1,0:T(1,128)S(1)} %copy-done.10, f32[1,1024]{1,0:T(1,128)S(1)} %copy-done.11, f32[1,1024]{1,0:T(1,128)S(1)} %copy-done.12, bf16[4,256,512]{2,1,0:T(8,128)(2,1)S(1)} %bitcast.28, ...), custom_call_target="tpu_custom_call" | custom-call | tf_op jit(solution)/shard_map/channel_relay/pallas_call | solution.py:222
  125.7 10.4 %collective-permute-done.2.refs_0_ = bf16[256,1024]{1,0:T(8,128)(2,1)} collective-permute-done((bf16[256,1024]{1,0:T(8,128)(2,1)}, bf16[256,1024]{1,0:T(8,128)(2,1)}, u32[]{:S(2)}, u32[]{:S(2)}) %collective-permute-start.2) | collective-permute-done | bytes 524320 | tf_op jit(solution)/shard_map/ppermute | solution.py:290
  136.0 11.2 %collective-permute-done.3.refs_1_ = bf16[256,1024]{1,0:T(8,128)(2,1)} collective-permute-done((bf16[256,1024]{1,0:T(8,128)(2,1)}, bf16[256,1024]{1,0:T(8,128)(2,1)}, u32[]{:S(2)}, u32[]{:S(2)}) %collective-permute-start.3) | collective-permute-done | bytes 524320 | tf_op jit(solution)/shard_map/ppermute | solution.py:290
  151.1 11.4 %all-to-all-start.4 = ((bf16[64,8,1024]{2,1,0:T(8,128)(2,1)}), bf16[64,8,1024]{2,1,0:T(8,128)(2,1)}, u32[]{:S(2)}, u32[]{:S(2)}) async-start(bf16[64,8,1024]{2,1,0:T(8,128)(2,1)} %bitcast.61), calls=%async_computation.4 | async-start | bytes 2097152 | tf_op jit(solution)/shard_map/all_to_all | solution.py:262
  162.6 3.8 %channel_relay.7 = bf16[256,1024]{1,0:T(8,128)(2,1)} custom-call(bf16[512,1024]{1,0:T(8,128)(2,1)} %bitcast.39, bf16[1024,1024]{1,0:T(8,128)(2,1)} %bitcast.49, f32[1,1024]{1,0:T(1,128)S(1)} %copy-done.10, f32[1,1024]{1,0:T(1,128)S(1)} %copy-done.11, f32[1,1024]{1,0:T(1,128)S(1)} %copy-done.12, bf16[4,256,512]{2,1,0:T(8,128)(2,1)S(1)} %bitcast.29, ...), custom_call_target="tpu_custom_call" | custom-call | tf_op jit(solution)/shard_map/channel_relay/pallas_call | solution.py:222
  167.7 3.8 %channel_relay.6 = bf16[256,1024]{1,0:T(8,128)(2,1)} custom-call(bf16[512,1024]{1,0:T(8,128)(2,1)S(1)} %bitcast.40, bf16[1024,1024]{1,0:T(8,128)(2,1)} %bitcast.50, f32[1,1024]{1,0:T(1,128)S(1)} %copy-done.10, f32[1,1024]{1,0:T(1,128)S(1)} %copy-done.11, f32[1,1024]{1,0:T(1,128)S(1)} %copy-done.12, bf16[4,256,512]{2,1,0:T(8,128)(2,1)S(1)} %bitcast.30, ...), custom_call_target="tpu_custom_call" | custom-call | tf_op jit(solution)/shard_map/channel_relay/pallas_call | solution.py:222
  171.4 3.0 collective-permute-start
  176.4 10.3 %collective-permute-done.refs_0_ = bf16[256,1024]{1,0:T(8,128)(2,1)S(1)} collective-permute-done((bf16[256,1024]{1,0:T(8,128)(2,1)}, bf16[256,1024]{1,0:T(8,128)(2,1)S(1)}, u32[]{:S(2)}, u32[]{:S(2)}) %collective-permute-start) | collective-permute-done | bytes 524320 | tf_op jit(solution)/shard_map/ppermute | solution.py:290
  186.7 11.1 %collective-permute-done.1.refs_1_ = bf16[256,1024]{1,0:T(8,128)(2,1)S(1)} collective-permute-done((bf16[256,1024]{1,0:T(8,128)(2,1)S(1)}, bf16[256,1024]{1,0:T(8,128)(2,1)S(1)}, u32[]{:S(2)}, u32[]{:S(2)}) %collective-permute-start.1) | collective-permute-done | bytes 524320 | tf_op jit(solution)/shard_map/ppermute | solution.py:290
  199.4 11.7 %all-to-all-start.3 = ((bf16[64,8,1024]{2,1,0:T(8,128)(2,1)}), bf16[64,8,1024]{2,1,0:T(8,128)(2,1)}, u32[]{:S(2)}, u32[]{:S(2)}) async-start(bf16[64,8,1024]{2,1,0:T(8,128)(2,1)} %bitcast.62), calls=%async_computation.3 | async-start | bytes 2097152 | tf_op jit(solution)/shard_map/all_to_all | solution.py:262
  213.6 4.9 %mix_second.6.refs_0_ = f32[1024,1024]{1,0:T(8,128)} custom-call(bf16[1024,512]{1,0:T(8,128)(2,1)S(1)} %spread.7.left_ref, bf16[512,1024]{1,0:T(8,128)(2,1)} %bitcast.18.part_ref), custom_call_target="tpu_custom_call" | custom-call | tf_op jit(solution)/shard_map/mix_second/pallas_call | solution.py:159
  218.5 21.1 %all-to-all-done.3 = bf16[64,8,1024]{2,1,0:T(8,128)(2,1)} async-done(((bf16[64,8,1024]{2,1,0:T(8,128)(2,1)}), bf16[64,8,1024]{2,1,0:T(8,128)(2,1)}, u32[]{:S(2)}, u32[]{:S(2)}) %all-to-all-start.3) | async-done | bytes 1048608 | tf_op jit(solution)/shard_map/all_to_all | solution.py:262
  239.6 5.2 %mix_second.7 = bf16[1024,1024]{1,0:T(8,128)(2,1)} custom-call(bf16[1024,512]{1,0:T(8,128)(2,1)S(1)} %copy-done.9, bf16[512,1024]{1,0:T(8,128)(2,1)} %bitcast.16.part_ref, f32[1024,1024]{1,0:T(8,128)} %mix_second.6.refs_0_), custom_call_target="tpu_custom_call" | custom-call | tf_op jit(solution)/shard_map/mix_second/pallas_call | solution.py:159
  244.8 6.5 %all-to-all-start.5 = ((bf16[64,16,1024]{2,1,0:T(8,128)(2,1)}), bf16[64,16,1024]{2,1,0:T(8,128)(2,1)}, u32[]{:S(2)}, u32[]{:S(2)}) async-start(bf16[64,16,1024]{2,1,0:T(8,128)(2,1)} %bitcast.52), calls=%async_computation.5 | async-start | bytes 4194304 | tf_op jit(solution)/shard_map/all_to_all | solution.py:262
  254.2 48.2 %all-to-all-done.5 = bf16[64,16,1024]{2,1,0:T(8,128)(2,1)} async-done(((bf16[64,16,1024]{2,1,0:T(8,128)(2,1)}), bf16[64,16,1024]{2,1,0:T(8,128)(2,1)}, u32[]{:S(2)}, u32[]{:S(2)}) %all-to-all-start.5) | async-done | bytes 2097184 | tf_op jit(solution)/shard_map/all_to_all | solution.py:262
  302.4 8.6 %channel_last.1 = bf16[4,256,1024]{2,1,0:T(8,128)(2,1)} custom-call(bf16[1024,1024]{1,0:T(8,128)(2,1)} %bitcast.20.returned_ref, bf16[2,256,1024]{2,1,0:T(8,128)(2,1)} %bitcast.59, bf16[2,256,1024]{2,1,0:T(8,128)(2,1)} %bitcast.60, f32[1,1024]{1,0:T(1,128)S(1)} %copy-done.10, f32[1,1024]{1,0:T(1,128)S(1)} %copy-done.11, f32[1,1024]{1,0:T(1,128)S(1)} %copy-done.12, ...), custom_call_target="tpu_custom_call" | custom-call | tf_op jit(solution)/shard_map/channel_last/pallas_call | solution.py:246
  (56 shorter events, 26.3 us)
Async XLA Ops:
  5.1 12.3 %copy-start.13 = (bf16[1,4,256,256]{3,2,1,0:T(8,128)(2,1)S(1)}, bf16[1,4,256,256]{3,2,1,0:T(8,128)(2,1)}, u32[]{:S(2)}) copy-start(bf16[1,4,256,256]{3,2,1,0:T(8,128)(2,1)} %param.12) | copy-start | bytes 1572868
  5.1 63.5 %all-to-all-start = ((bf16[64,16,1024]{2,1,0:T(8,128)(2,1)}), bf16[64,16,1024]{2,1,0:T(8,128)(2,1)S(1)}, u32[]{:S(2)}, u32[]{:S(2)}) async-start(bf16[64,16,1024]{2,1,0:T(8,128)(2,1)} %bitcast.51), calls=%async_computation | async-start | bytes 4194304 | tf_op jit(solution)/shard_map/all_to_all | solution.py:262
  71.6 34.4 %all-to-all-start.1 = ((bf16[64,8,1024]{2,1,0:T(8,128)(2,1)}), bf16[64,8,1024]{2,1,0:T(8,128)(2,1)S(1)}, u32[]{:S(2)}, u32[]{:S(2)}) async-start(bf16[64,8,1024]{2,1,0:T(8,128)(2,1)} %bitcast.54), calls=%async_computation.1 | async-start | bytes 2097152 | tf_op jit(solution)/shard_map/all_to_all | solution.py:262
  78.9 34.2 %copy-start.11 = (f32[1,1024]{1,0:T(1,128)S(1)}, f32[1,1024]{1,0:T(1,128)}, u32[]{:S(2)}) copy-start(f32[1,1024]{1,0:T(1,128)} %refs_3_.1) | copy-start | bytes 12292
  78.9 34.2 %copy-start.12 = (f32[1,1024]{1,0:T(1,128)S(1)}, f32[1,1024]{1,0:T(1,128)}, u32[]{:S(2)}) copy-start(f32[1,1024]{1,0:T(1,128)} %refs_4_.1) | copy-start | bytes 12292
  81.9 31.2 %copy-start = (bf16[1,4,256,512]{3,2,1,0:T(8,128)(2,1)S(1)}, bf16[1,4,256,512]{3,2,1,0:T(8,128)(2,1)}, u32[]{:S(2)}) copy-start(bf16[1,4,256,512]{3,2,1,0:T(8,128)(2,1)} %param.16) | copy-start | bytes 3145732
  81.9 31.3 %copy-start.1 = (bf16[1,4,4,128,256]{4,3,2,1,0:T(8,128)(2,1)S(1)}, bf16[1,4,4,128,256]{4,3,2,1,0:T(8,128)(2,1)}, u32[]{:S(2)}) copy-start(bf16[1,4,4,128,256]{4,3,2,1,0:T(8,128)(2,1)} %param.17) | copy-start | bytes 3145732
  81.9 31.3 %copy-start.10 = (f32[1,1024]{1,0:T(1,128)S(1)}, f32[1,1024]{1,0:T(1,128)}, u32[]{:S(2)}) copy-start(f32[1,1024]{1,0:T(1,128)} %refs_2_.9) | copy-start | bytes 12292
  106.9 44.2 %all-to-all-start.2 = ((bf16[64,8,1024]{2,1,0:T(8,128)(2,1)}), bf16[64,8,1024]{2,1,0:T(8,128)(2,1)S(1)}, u32[]{:S(2)}, u32[]{:S(2)}) async-start(bf16[64,8,1024]{2,1,0:T(8,128)(2,1)} %bitcast.53), calls=%async_computation.2 | async-start | bytes 2097152 | tf_op jit(solution)/shard_map/all_to_all | solution.py:262
  113.2 4.0 %copy-start.5 = (bf16[64,8,1024]{2,1,0:T(8,128)(2,1)S(1)}, bf16[64,8,1024]{2,1,0:T(8,128)(2,1)}, u32[]{:S(2)}) copy-start(bf16[64,8,1024]{2,1,0:T(8,128)(2,1)} %copy-done.4) | copy-start | bytes 3145732
  120.8 15.2 %collective-permute-start.2 = (bf16[256,1024]{1,0:T(8,128)(2,1)}, bf16[256,1024]{1,0:T(8,128)(2,1)}, u32[]{:S(2)}, u32[]{:S(2)}) collective-permute-start(bf16[256,1024]{1,0:T(8,128)(2,1)} %channel_relay.4), channel_id=1, source_target_pairs={{0,64},{64,128},{128,192},{1,65},{65,129},{129,193},{2,66},{66,130... | collective-permute-start | bytes 1572872 | tf_op jit(solution)/shard_map/ppermute | solution.py:290
  123.7 23.6 %collective-permute-start.3 = (bf16[256,1024]{1,0:T(8,128)(2,1)}, bf16[256,1024]{1,0:T(8,128)(2,1)}, u32[]{:S(2)}, u32[]{:S(2)}) collective-permute-start(bf16[256,1024]{1,0:T(8,128)(2,1)} %channel_relay.5), channel_id=1, source_target_pairs={{0,64},{64,128},{128,192},{1,65},{65,129},{129,193},{2,66},{66,130... | collective-permute-start | bytes 1572872 | tf_op jit(solution)/shard_map/ppermute | solution.py:290
  151.1 11.5 %copy-start.2 = (bf16[64,8,1024]{2,1,0:T(8,128)(2,1)}, bf16[64,8,1024]{2,1,0:T(8,128)(2,1)S(1)}, u32[]{:S(2)}) copy-start(bf16[64,8,1024]{2,1,0:T(8,128)(2,1)S(1)} %all-to-all-done.2) | copy-start | bytes 3145732
  151.1 48.3 %all-to-all-start.4 = ((bf16[64,8,1024]{2,1,0:T(8,128)(2,1)}), bf16[64,8,1024]{2,1,0:T(8,128)(2,1)}, u32[]{:S(2)}, u32[]{:S(2)}) async-start(bf16[64,8,1024]{2,1,0:T(8,128)(2,1)} %bitcast.61), calls=%async_computation.4 | async-start | bytes 2097152 | tf_op jit(solution)/shard_map/all_to_all | solution.py:262
  167.7 6.8 %copy-start.16 = (bf16[256,1024]{1,0:T(8,128)(2,1)S(1)}, bf16[256,1024]{1,0:T(8,128)(2,1)}, u32[]{:S(2)}) copy-start(bf16[256,1024]{1,0:T(8,128)(2,1)} %channel_relay.7) | copy-start | bytes 1572868
  167.7 30.2 %copy-start.7 = (bf16[1,4,256,256]{3,2,1,0:T(8,128)(2,1)S(1)}, bf16[1,4,256,256]{3,2,1,0:T(8,128)(2,1)}, u32[]{:S(2)}) copy-start(bf16[1,4,256,256]{3,2,1,0:T(8,128)(2,1)} %param.11) | copy-start | bytes 1572868
  171.4 39.7 %copy-start.14 = (bf16[1,4,256,256]{3,2,1,0:T(8,128)(2,1)S(1)}, bf16[1,4,256,256]{3,2,1,0:T(8,128)(2,1)}, u32[]{:S(2)}) copy-start(bf16[1,4,256,256]{3,2,1,0:T(8,128)(2,1)} %param.12) | copy-start | bytes 1572868
  171.4 15.3 %collective-permute-start = (bf16[256,1024]{1,0:T(8,128)(2,1)}, bf16[256,1024]{1,0:T(8,128)(2,1)S(1)}, u32[]{:S(2)}, u32[]{:S(2)}) collective-permute-start(bf16[256,1024]{1,0:T(8,128)(2,1)} %channel_relay.6), channel_id=1, source_target_pairs={{0,64},{64,128},{128,192},{1,65},{65,129},{129,193},{2,66},{66,130... | collective-permute-start | bytes 1572872 | tf_op jit(solution)/shard_map/ppermute | solution.py:290
  174.5 23.4 %collective-permute-start.1 = (bf16[256,1024]{1,0:T(8,128)(2,1)S(1)}, bf16[256,1024]{1,0:T(8,128)(2,1)S(1)}, u32[]{:S(2)}, u32[]{:S(2)}) collective-permute-start(bf16[256,1024]{1,0:T(8,128)(2,1)S(1)} %copy-done.16), channel_id=1, source_target_pairs={{0,64},{64,128},{128,192},{1,65},{65,129},{129,193},{2,66},{66,130... | collective-permute-start | bytes 1572872 | tf_op jit(solution)/shard_map/ppermute | solution.py:290
  199.4 40.2 %all-to-all-start.3 = ((bf16[64,8,1024]{2,1,0:T(8,128)(2,1)}), bf16[64,8,1024]{2,1,0:T(8,128)(2,1)}, u32[]{:S(2)}, u32[]{:S(2)}) async-start(bf16[64,8,1024]{2,1,0:T(8,128)(2,1)} %bitcast.62), calls=%async_computation.3 | async-start | bytes 2097152 | tf_op jit(solution)/shard_map/all_to_all | solution.py:262
  213.6 26.0 %copy-start.9 = (bf16[1024,512]{1,0:T(8,128)(2,1)S(1)}, bf16[1024,512]{1,0:T(8,128)(2,1)}, u32[]{:S(2)}) copy-start(bf16[1024,512]{1,0:T(8,128)(2,1)} %copy-done.8) | copy-start | bytes 3145732
  244.8 6.5 %copy-start.15 = (bf16[256,1024]{1,0:T(8,128)(2,1)S(1)}, bf16[256,1024]{1,0:T(8,128)(2,1)}, u32[]{:S(2)}) copy-start(bf16[256,1024]{1,0:T(8,128)(2,1)} %channel_relay.4) | copy-start | bytes 1572868
  244.8 6.5 %copy-start.17 = (bf16[256,1024]{1,0:T(8,128)(2,1)S(1)}, bf16[256,1024]{1,0:T(8,128)(2,1)}, u32[]{:S(2)}) copy-start(bf16[256,1024]{1,0:T(8,128)(2,1)} %channel_relay.7) | copy-start | bytes 1572868
  244.8 57.6 %all-to-all-start.5 = ((bf16[64,16,1024]{2,1,0:T(8,128)(2,1)}), bf16[64,16,1024]{2,1,0:T(8,128)(2,1)}, u32[]{:S(2)}, u32[]{:S(2)}) async-start(bf16[64,16,1024]{2,1,0:T(8,128)(2,1)} %bitcast.52), calls=%async_computation.5 | async-start | bytes 4194304 | tf_op jit(solution)/shard_map/all_to_all | solution.py:262
  (4 other events, 4.2 us)

commit v4 on v3

--- a/solution.py
+++ b/solution.py
@@ -28,7 +28,7 @@
 def params(name):
     return dict(
         name=name,
-        compiler_params=pltpu.CompilerParams(vmem_limit_bytes=48 * 1024 * 1024),
+        compiler_params=pltpu.CompilerParams(vmem_limit_bytes=32 * 1024 * 1024),
     )
 
 
@@ -74,15 +74,24 @@
 
 
 def relayed_kernel(half, chunk, section_ref, right_ref, fresh_ref, *refs):
-    *received_refs, out_ref, current_ref, sem = refs
-    columns = pl.ds(pl.program_id(0) * chunk, chunk)
+    *received_refs, out_ref, current_ref, held_ref, sems = refs
+    step = pl.program_id(0)
+    columns = pl.ds(step * chunk, chunk)
+
+    def fetch(n):
+        place = pl.ds(n * chunk, chunk)
+        source = fresh_ref.at[pl.ds(2 * half * BLOCK, 2 * BLOCK), place]
+        return pltpu.make_async_copy(source, held_ref.at[n], sems.at[n])
 
     @pl.when(section_ref[0] == 0)
     def _():
-        source = fresh_ref.at[pl.ds(2 * half * BLOCK, 2 * BLOCK), columns]
-        copy = pltpu.make_async_copy(source, current_ref, sem)
-        copy.start()
-        copy.wait()
+        @pl.when(step == 0)
+        def _():
+            for n in range(WIDTH // chunk):
+                fetch(n).start()
+
+        fetch(step).wait()
+        current_ref[...] = held_ref[step]
 
     @pl.when(section_ref[0] != 0)
     def _():
@@ -106,7 +115,10 @@
         ],
         out_specs=(column, column),
         out_shape=(HBM((2 * BLOCK, WIDTH), BF16),) * 2,
-        scratch_shapes=[pltpu.SemaphoreType.DMA],
+        scratch_shapes=[
+            VMEM((WIDTH // chunk, 2 * BLOCK, chunk), BF16),
+            pltpu.SemaphoreType.DMA((WIDTH // chunk,)),
+        ],
         **params("mix_first_relayed"),
     )(section, right, in_hbm(fresh), *(in_vmem(part) for part in received))
 
@@ -120,7 +132,7 @@
             source = column >> 2
         else:
             source = ((column >> 3) << 2) + 2 * half + ((column >> 2) & 1)
-        place = jnp.where(lax.broadcasted_iota(jnp.int32, (size, chunk), 0) == source, 1.0, 0.0)
+        place = jnp.where(lax.broadcasted_iota(jnp.int32, (size, chunk), 0) == source, 0.5, 0.0)
         full = jnp.dot(rows_ref[...], place.astype(BF16), preferred_element_type=F32)
         row = lax.broadcasted_iota(jnp.int32, full.shape, 0)
         offset = lax.broadcasted_iota(jnp.int32, full.shape, 1)
@@ -129,10 +141,10 @@
 
 
 def spread(rows, half=None):
-    columns = 4 * BLOCK if half is None else 2 * BLOCK
+    columns, place = (4 * BLOCK, VMEM) if half is None else (2 * BLOCK, HBM)
     return pl.pallas_call(
         functools.partial(spread_kernel, half),
-        out_shape=VMEM((rows.shape[0], columns), BF16),
+        out_shape=place((rows.shape[0], columns), BF16),
         **params("spread"),
     )(rows)
 
@@ -146,31 +158,52 @@
     return left.transpose(1, 0, 2).reshape(-1, BLOCK)
 
 
-def second_kernel(left_ref, part_ref, *refs):
-    *held_refs, out_ref = refs
-    total = jnp.dot(left_ref[...], part_ref[...], preferred_element_type=F32)
-    for held_ref in held_refs:
-        total = total + held_ref[...]
-    out_ref[...] = total.astype(out_ref.dtype)
-
-
-def mix_second(left, part, out_shape, held=(), chunk=256):
-    column = lambda rows: pl.BlockSpec((rows, chunk), lambda c: (0, c))
+def second_kernel(*refs):
+    *in_refs, out_ref = refs
+    total = sum(
+        jnp.dot(left_ref[...], part_ref[...], preferred_element_type=F32)
+        for left_ref, part_ref in zip(in_refs[0::2], in_refs[1::2])
+    )
+    out_ref[...] = total.astype(BF16)
+
+
+def mix_second_last(lefts, parts, count=256):
+    rows = lefts[0].shape[0]
+    block = lambda width: pl.BlockSpec((count, width), lambda r: (r, 0))
+    specs, arrays = [], []
+    for left, part in zip(lefts, parts):
+        specs += [block(left.shape[1]), pl.BlockSpec(memory_space=VMEM)]
+        arrays += [in_hbm(left), in_vmem(part)]
+    return pl.pallas_call(
+        second_kernel,
+        grid=(rows // count,),
+        in_specs=specs,
+        out_specs=block(WIDTH),
+        out_shape=HBM((rows, WIDTH), BF16),
+        **params("mix_second_last"),
+    )(*arrays)
+
+
+def mix_second(pairs, chunk=256):
+    rows = pairs[0][0].shape[0]
+    column = lambda count: pl.BlockSpec((count, chunk), lambda c: (0, c))
+    specs, arrays = [], []
+    for left, part, place in pairs:
+        specs += [pl.BlockSpec(memory_space=VMEM), column(part.shape[0])]
+        arrays += [in_vmem(left), place(part)]
     return pl.pallas_call(
         second_kernel,
         grid=(WIDTH // chunk,),
-        in_specs=[pl.BlockSpec(memory_space=VMEM), column(part.shape[0])]
-        + [column(array.shape[0]) for array in held],
-        out_specs=column(out_shape.shape[0]),
-        out_shape=out_shape,
+        in_specs=specs,
+        out_specs=column(rows),
+        out_shape=HBM((rows, WIDTH), BF16),
         **params("mix_second"),
-    )(in_vmem(left), in_vmem(part), *(in_hbm(array) for array in held))
-
-
-def gelu(u):
-    inner = u * (0.7978845608028654 + 0.035677408136300125 * (u * u))
-    half = 0.5 * u
-    return half + half * jnp.tanh(inner)
+    )(*arrays)
+
+
+def gelu_of_twice(v):
+    inner = v * (v * v * BF16(8 * 0.7978845608028654 * 0.044715) + BF16(2 * 0.7978845608028654))
+    return v + v * jnp.tanh(inner)
 
 
 def channel_rows(which, arrived, rows_refs, weight_refs):
@@ -186,14 +219,14 @@
             mixed.append(jnp.where(low, even, pltpu.roll(odd, 4, 1)).reshape(-1, width))
     mixed = jnp.concatenate(mixed)
     wide = jnp.concatenate([ref[...].reshape(-1, width) for ref in rows_refs]).astype(F32)
-    gate = 0.5 * jnp.tanh(wide * (0.5 * slope_ref[...]) + 0.5 * shift_ref[...]) + 0.5
-    residual = wide + mixed * gate
+    gate = jnp.tanh(wide * (0.5 * slope_ref[...]) + 0.5 * shift_ref[...])
+    residual = wide + mixed + mixed * gate
     scale = lax.rsqrt(jnp.mean(residual * residual, axis=-1, keepdims=True) + 1e-06)
-    normed = (residual * scale * gain_ref[...]).astype(BF16)
+    normed = (residual * scale * (0.5 * gain_ref[...])).astype(BF16)
     hidden = []
     for b in range(4):
         up = jnp.dot(normed[:, b * 256 : (b + 1) * 256], up_ref[b], preferred_element_type=F32)
-        hidden.append(gelu(up).astype(BF16))
+        hidden.append(gelu_of_twice(up.astype(BF16)))
     out = []
     for k in range(4):
         taken = jnp.concatenate([h[:, k * 128 : (k + 1) * 128] for h in hidden], axis=1)
@@ -218,19 +251,26 @@
 
 
 def channel_relay(returned, rows, block, weights, count=128):
+    first = block % 2 == 0
     steps = BLOCK // count
+    start = 0 if first else block * steps
+    if first:
+        rows = in_vmem(rows[block * BLOCK : (block + 1) * BLOCK])
+        returned = in_vmem(returned)
+    else:
+        rows, returned = in_hbm(rows), in_hbm(returned)
     return pl.pallas_call(
         functools.partial(relay_kernel, block % 2),
         grid=(steps,),
         in_specs=[
             pl.BlockSpec((2 * count, WIDTH), lambda s: (s, 0)),
-            pl.BlockSpec((count, WIDTH), lambda s: (block * steps + s, 0)),
+            pl.BlockSpec((count, WIDTH), lambda s: (start + s, 0)),
             *(fixed(array) for array in weights),
         ],
         out_specs=pl.BlockSpec((count, WIDTH), lambda s: (s, 0)),
         out_shape=HBM((BLOCK, WIDTH), BF16),
         **params("channel_relay"),
-    )(in_vmem(returned) if block % 2 == 0 else in_hbm(returned), in_hbm(rows), *weights)
+    )(returned, rows, *weights)
 
 
 def last_kernel(returned_ref, *refs):
@@ -279,7 +319,7 @@
     returned = []
     for half in range(2):
         matrix = spread(left_out[512 * half : 512 * half + 512])
-        mixed = mix_second(matrix, arrived, HBM((512, WIDTH), BF16))
+        mixed = mix_second([(matrix, arrived, in_vmem)])
         returned.append(exchange(mixed))
     firsts, currents, arrivals = [], [], []
     for half in range(2):
@@ -292,9 +332,7 @@
         currents.append(current.reshape(2, BLOCK, WIDTH))
         arrivals.append(exchange(leaving))
     first_out = jnp.concatenate(firsts)
-    left_in = [spread(by_output, half) for half in range(2)]
-    partial = mix_second(left_in[0], arrivals[0], HBM((1024, WIDTH), F32))
-    mixed = mix_second(left_in[1], arrivals[1], HBM((1024, WIDTH), BF16), (partial,))
+    mixed = mix_second_last([spread(by_output, half) for half in range(2)], arrivals)
     final = exchange(mixed)
     second_out = channel_last(final, currents, weights)
     return first_out[None], second_out.reshape(1, 1024, WIDTH)

time: 314 us -> 311 us (level)
  Pallas kernels: 50.4 us -> 43.5 us
  waiting for transfers between devices: 185 us -> 189 us
    all_to_all x6, waiting for transfers between devices: 142 us -> 146 us  [exchange(): lax.all_to_all(grouped, 'seq', split_axis=0, concat_axis=0, tiled=True)]
    pallas_call x4, Pallas kernels: 15.2 us -> 11.9 us  [channel_relay(): pl.pallas_call(functools.partial(relay_kernel, block % 2), grid=(steps,),...]
    pallas_call x8 -> x7, Pallas kernels: 17.8 us -> 15.7 us  [the longest x2 5.94 us: mix_second(): pl.pallas_call(second_kernel, grid=(WIDTH // chunk,), in_specs=specs, out...]
  transfers between devices with their start and end apart: 10 -> 10, of which waited for: 8 -> 8; matrix products, arithmetic and copies ran while one was open for 2% -> 3% of each run, Pallas kernels for 9% -> 7%
where the time goes in v4:
time: 311 us; the launch traced here: 309 us
  waiting for transfers between devices  189 us (61%)
  starting transfers between devices  63.7 us (20%)
  Pallas kernels  43.5 us (14%)
  local copies, waits for them, and re-layouts  8.69 us (3%)
    all_to_all x6, waiting for transfers between devices, exchange(): lax.all_to_all(grouped, 'seq', split_axis=0, concat_axis=0, tiled=True)  146 us
    all_to_all x6, starting transfers between devices, exchange(): lax.all_to_all(grouped, 'seq', split_axis=0, concat_axis=0, tiled=True)  54 us
    ppermute x4, waiting for transfers between devices, shards(): received.append(lax.ppermute(out, 'pipe', route))  42.9 us
    pallas_call x4, Pallas kernels, channel_relay(): pl.pallas_call(functools.partial(relay_kernel, block % 2), grid=(steps,),...  11.9 us
    ppermute x4, starting transfers between devices, shards(): received.append(lax.ppermute(out, 'pipe', route))  9.77 us
    pallas_call x1, Pallas kernels, channel_last(): pl.pallas_call(last_kernel, grid=(BLOCK // count,), in_specs=[pl.BlockSpe...  7.15 us
  transfers between devices with their start and end apart: 10, of which 8 were waited for; matrix products, arithmetic and copies ran while one was open for 3% of the time, Pallas kernels for 7%

profile of v4, /device:TPU:17, one launch (start us, length us, event | category | flops | bytes accessed | tf_op | source)
XLA Modules:
  0.0 308.8 jit_solution(4384126787443382446)
XLA Ops:
  0.6 4.5 %mix_first.1 = bf16[1024,1024]{1,0:T(8,128)(2,1)} custom-call(bf16[4,256,256]{2,1,0:T(8,128)(2,1)} %bitcast.47, bf16[1024,1024]{1,0:T(8,128)(2,1)} %bitcast.50), custom_call_target="tpu_custom_call" | custom-call | tf_op jit(solution)/shard_map/mix_first/pallas_call | solution.py:66
  5.1 12.3 %all-to-all-start = ((bf16[64,16,1024]{2,1,0:T(8,128)(2,1)}), bf16[64,16,1024]{2,1,0:T(8,128)(2,1)S(1)}, u32[]{:S(2)}, u32[]{:S(2)}) async-start(bf16[64,16,1024]{2,1,0:T(8,128)(2,1)} %bitcast.54), calls=%async_computation | async-start | bytes 4194304 | tf_op jit(solution)/shard_map/all_to_all | solution.py:302
  19.7 48.9 %all-to-all-done = bf16[64,16,1024]{2,1,0:T(8,128)(2,1)S(1)} async-done(((bf16[64,16,1024]{2,1,0:T(8,128)(2,1)}), bf16[64,16,1024]{2,1,0:T(8,128)(2,1)S(1)}, u32[]{:S(2)}, u32[]{:S(2)}) %all-to-all-start) | async-done | bytes 2097184 | tf_op jit(solution)/shard_map/all_to_all | solution.py:302
  68.6 3.0 mix_second.2
  71.6 5.8 %all-to-all-start.1 = ((bf16[64,8,1024]{2,1,0:T(8,128)(2,1)}), bf16[64,8,1024]{2,1,0:T(8,128)(2,1)S(1)}, u32[]{:S(2)}, u32[]{:S(2)}) async-start(bf16[64,8,1024]{2,1,0:T(8,128)(2,1)} %bitcast.56), calls=%async_computation.1 | async-start | bytes 2097152 | tf_op jit(solution)/shard_map/all_to_all | solution.py:302
  78.9 3.0 mix_second.3
  81.9 24.1 %all-to-all-done.1 = bf16[64,8,1024]{2,1,0:T(8,128)(2,1)S(1)} async-done(((bf16[64,8,1024]{2,1,0:T(8,128)(2,1)}), bf16[64,8,1024]{2,1,0:T(8,128)(2,1)S(1)}, u32[]{:S(2)}, u32[]{:S(2)}) %all-to-all-start.1) | async-done | bytes 1048608 | tf_op jit(solution)/shard_map/all_to_all | solution.py:302
  106.9 6.3 %all-to-all-start.2 = ((bf16[64,8,1024]{2,1,0:T(8,128)(2,1)}), bf16[64,8,1024]{2,1,0:T(8,128)(2,1)S(1)}, u32[]{:S(2)}, u32[]{:S(2)}) async-start(bf16[64,8,1024]{2,1,0:T(8,128)(2,1)} %bitcast.55), calls=%async_computation.2 | async-start | bytes 2097152 | tf_op jit(solution)/shard_map/all_to_all | solution.py:302
  115.4 3.6 %channel_relay.5 = bf16[256,1024]{1,0:T(8,128)(2,1)} custom-call(bf16[512,1024]{1,0:T(8,128)(2,1)} %bitcast.45, bf16[1024,1024]{1,0:T(8,128)(2,1)} %bitcast.51, f32[1,1024]{1,0:T(1,128)S(1)} %copy-done.9, f32[1,1024]{1,0:T(1,128)S(1)} %copy-done.10, f32[1,1024]{1,0:T(1,128)S(1)} %copy-done.11, bf16[4,256,512]{2,1,0:T(8,128)(2,1)S(1)} %bitcast.31, ...), custom_call_target="tpu_custom_call" | custom-call | tf_op jit(solution)/shard_map/channel_relay/pallas_call | solution.py:262
  121.3 2.9 collective-permute-start.1
  126.2 10.4 %collective-permute-done.1.refs_1_ = bf16[256,1024]{1,0:T(8,128)(2,1)} collective-permute-done((bf16[256,1024]{1,0:T(8,128)(2,1)}, bf16[256,1024]{1,0:T(8,128)(2,1)}, u32[]{:S(2)}, u32[]{:S(2)}) %collective-permute-start.1) | collective-permute-done | bytes 524320 | tf_op jit(solution)/shard_map/ppermute | solution.py:330
  136.6 11.2 %collective-permute-done.refs_0_ = bf16[256,1024]{1,0:T(8,128)(2,1)} collective-permute-done((bf16[256,1024]{1,0:T(8,128)(2,1)}, bf16[256,1024]{1,0:T(8,128)(2,1)}, u32[]{:S(2)}, u32[]{:S(2)}) %collective-permute-start) | collective-permute-done | bytes 524320 | tf_op jit(solution)/shard_map/ppermute | solution.py:330
  148.8 2.8 mix_first_relayed.2
  151.6 11.4 %all-to-all-start.3 = ((bf16[64,8,1024]{2,1,0:T(8,128)(2,1)}), bf16[64,8,1024]{2,1,0:T(8,128)(2,1)}, u32[]{:S(2)}, u32[]{:S(2)}) async-start(bf16[64,8,1024]{2,1,0:T(8,128)(2,1)} %bitcast.63), calls=%async_computation.3 | async-start | bytes 2097152 | tf_op jit(solution)/shard_map/all_to_all | solution.py:302
  163.1 3.6 %channel_relay.7 = bf16[256,1024]{1,0:T(8,128)(2,1)} custom-call(bf16[512,1024]{1,0:T(8,128)(2,1)} %bitcast.43, bf16[1024,1024]{1,0:T(8,128)(2,1)} %bitcast.52, f32[1,1024]{1,0:T(1,128)S(1)} %copy-done.9, f32[1,1024]{1,0:T(1,128)S(1)} %copy-done.10, f32[1,1024]{1,0:T(1,128)S(1)} %copy-done.11, bf16[4,256,512]{2,1,0:T(8,128)(2,1)S(1)} %bitcast.33, ...), custom_call_target="tpu_custom_call" | custom-call | tf_op jit(solution)/shard_map/channel_relay/pallas_call | solution.py:262
  170.3 3.0 collective-permute-start.3
  175.2 10.1 %collective-permute-done.3.refs_1_ = bf16[256,1024]{1,0:T(8,128)(2,1)S(1)} collective-permute-done((bf16[256,1024]{1,0:T(8,128)(2,1)S(1)}, bf16[256,1024]{1,0:T(8,128)(2,1)S(1)}, u32[]{:S(2)}, u32[]{:S(2)}) %collective-permute-start.3) | collective-permute-done | bytes 524320 | tf_op jit(solution)/shard_map/ppermute | solution.py:330
  185.3 11.1 %collective-permute-done.2.refs_0_ = bf16[256,1024]{1,0:T(8,128)(2,1)S(1)} collective-permute-done((bf16[256,1024]{1,0:T(8,128)(2,1)}, bf16[256,1024]{1,0:T(8,128)(2,1)S(1)}, u32[]{:S(2)}, u32[]{:S(2)}) %collective-permute-start.2) | collective-permute-done | bytes 524320 | tf_op jit(solution)/shard_map/ppermute | solution.py:330
  198.0 11.5 %all-to-all-start.4 = ((bf16[64,8,1024]{2,1,0:T(8,128)(2,1)}), bf16[64,8,1024]{2,1,0:T(8,128)(2,1)}, u32[]{:S(2)}, u32[]{:S(2)}) async-start(bf16[64,8,1024]{2,1,0:T(8,128)(2,1)} %bitcast.64), calls=%async_computation.4 | async-start | bytes 2097152 | tf_op jit(solution)/shard_map/all_to_all | solution.py:302
  213.0 25.0 %all-to-all-done.4 = bf16[64,8,1024]{2,1,0:T(8,128)(2,1)} async-done(((bf16[64,8,1024]{2,1,0:T(8,128)(2,1)}), bf16[64,8,1024]{2,1,0:T(8,128)(2,1)}, u32[]{:S(2)}, u32[]{:S(2)}) %all-to-all-start.4) | async-done | bytes 1048608 | tf_op jit(solution)/shard_map/all_to_all | solution.py:302
  238.0 5.9 %mix_second_last.1 = bf16[1024,1024]{1,0:T(8,128)(2,1)} custom-call(bf16[1024,512]{1,0:T(8,128)(2,1)} %spread.6.refs_0_, bf16[512,1024]{1,0:T(8,128)(2,1)} %bitcast.18.refs_1_, bf16[1024,512]{1,0:T(8,128)(2,1)} %spread.7.refs_2_, bf16[512,1024]{1,0:T(8,128)(2,1)} %bitcast.20.refs_3_), custom_call_target="tpu_custom_call" | custom-call | tf_op jit(solution)/shard_map/mix_second_last/pallas_call | solution.py:177
  244.0 6.5 %all-to-all-start.5 = ((bf16[64,16,1024]{2,1,0:T(8,128)(2,1)}), bf16[64,16,1024]{2,1,0:T(8,128)(2,1)}, u32[]{:S(2)}, u32[]{:S(2)}) async-start(bf16[64,16,1024]{2,1,0:T(8,128)(2,1)} %bitcast.53), calls=%async_computation.5 | async-start | bytes 4194304 | tf_op jit(solution)/shard_map/all_to_all | solution.py:302
  253.3 48.4 %all-to-all-done.5 = bf16[64,16,1024]{2,1,0:T(8,128)(2,1)} async-done(((bf16[64,16,1024]{2,1,0:T(8,128)(2,1)}), bf16[64,16,1024]{2,1,0:T(8,128)(2,1)}, u32[]{:S(2)}, u32[]{:S(2)}) %all-to-all-start.5) | async-done | bytes 2097184 | tf_op jit(solution)/shard_map/all_to_all | solution.py:302
  301.6 7.1 %channel_last.1 = bf16[4,256,1024]{2,1,0:T(8,128)(2,1)} custom-call(bf16[1024,1024]{1,0:T(8,128)(2,1)} %bitcast.22.returned_ref, bf16[2,256,1024]{2,1,0:T(8,128)(2,1)} %bitcast.61, bf16[2,256,1024]{2,1,0:T(8,128)(2,1)} %bitcast.62, f32[1,1024]{1,0:T(1,128)S(1)} %copy-done.9, f32[1,1024]{1,0:T(1,128)S(1)} %copy-done.10, f32[1,1024]{1,0:T(1,128)S(1)} %copy-done.11, ...), custom_call_target="tpu_custom_call" | custom-call | tf_op jit(solution)/shard_map/channel_last/pallas_call | solution.py:286
  (54 shorter events, 25.3 us)
Async XLA Ops:
  5.1 12.3 %copy-start.12 = (bf16[1,4,256,256]{3,2,1,0:T(8,128)(2,1)S(1)}, bf16[1,4,256,256]{3,2,1,0:T(8,128)(2,1)}, u32[]{:S(2)}) copy-start(bf16[1,4,256,256]{3,2,1,0:T(8,128)(2,1)} %param.12) | copy-start | bytes 1572868
  5.1 63.5 %all-to-all-start = ((bf16[64,16,1024]{2,1,0:T(8,128)(2,1)}), bf16[64,16,1024]{2,1,0:T(8,128)(2,1)S(1)}, u32[]{:S(2)}, u32[]{:S(2)}) async-start(bf16[64,16,1024]{2,1,0:T(8,128)(2,1)} %bitcast.54), calls=%async_computation | async-start | bytes 4194304 | tf_op jit(solution)/shard_map/all_to_all | solution.py:302
  71.6 34.4 %all-to-all-start.1 = ((bf16[64,8,1024]{2,1,0:T(8,128)(2,1)}), bf16[64,8,1024]{2,1,0:T(8,128)(2,1)S(1)}, u32[]{:S(2)}, u32[]{:S(2)}) async-start(bf16[64,8,1024]{2,1,0:T(8,128)(2,1)} %bitcast.56), calls=%async_computation.1 | async-start | bytes 2097152 | tf_op jit(solution)/shard_map/all_to_all | solution.py:302
  106.0 9.4 %copy-start = (bf16[1,4,256,512]{3,2,1,0:T(8,128)(2,1)S(1)}, bf16[1,4,256,512]{3,2,1,0:T(8,128)(2,1)}, u32[]{:S(2)}) copy-start(bf16[1,4,256,512]{3,2,1,0:T(8,128)(2,1)} %param.16) | copy-start | bytes 3145732
  106.0 9.4 %copy-start.1 = (bf16[1,4,4,128,256]{4,3,2,1,0:T(8,128)(2,1)S(1)}, bf16[1,4,4,128,256]{4,3,2,1,0:T(8,128)(2,1)}, u32[]{:S(2)}) copy-start(bf16[1,4,4,128,256]{4,3,2,1,0:T(8,128)(2,1)} %param.17) | copy-start | bytes 3145732
  106.0 9.4 %copy-start.9 = (f32[1,1024]{1,0:T(1,128)S(1)}, f32[1,1024]{1,0:T(1,128)}, u32[]{:S(2)}) copy-start(f32[1,1024]{1,0:T(1,128)} %refs_2_.9) | copy-start | bytes 12292
  106.0 9.4 %copy-start.10 = (f32[1,1024]{1,0:T(1,128)S(1)}, f32[1,1024]{1,0:T(1,128)}, u32[]{:S(2)}) copy-start(f32[1,1024]{1,0:T(1,128)} %refs_3_.1) | copy-start | bytes 12292
  106.0 9.4 %copy-start.11 = (f32[1,1024]{1,0:T(1,128)S(1)}, f32[1,1024]{1,0:T(1,128)}, u32[]{:S(2)}) copy-start(f32[1,1024]{1,0:T(1,128)} %refs_4_.1) | copy-start | bytes 12292
  106.9 44.7 %all-to-all-start.2 = ((bf16[64,8,1024]{2,1,0:T(8,128)(2,1)}), bf16[64,8,1024]{2,1,0:T(8,128)(2,1)S(1)}, u32[]{:S(2)}, u32[]{:S(2)}) async-start(bf16[64,8,1024]{2,1,0:T(8,128)(2,1)} %bitcast.55), calls=%async_computation.2 | async-start | bytes 2097152 | tf_op jit(solution)/shard_map/all_to_all | solution.py:302
  115.4 3.6 %copy-start.5 = (bf16[64,8,1024]{2,1,0:T(8,128)(2,1)S(1)}, bf16[64,8,1024]{2,1,0:T(8,128)(2,1)}, u32[]{:S(2)}) copy-start(bf16[64,8,1024]{2,1,0:T(8,128)(2,1)} %copy-done.4) | copy-start | bytes 3145732
  121.3 15.2 %collective-permute-start.1 = (bf16[256,1024]{1,0:T(8,128)(2,1)}, bf16[256,1024]{1,0:T(8,128)(2,1)}, u32[]{:S(2)}, u32[]{:S(2)}) collective-permute-start(bf16[256,1024]{1,0:T(8,128)(2,1)} %channel_relay.5), channel_id=1, source_target_pairs={{0,64},{64,128},{128,192},{1,65},{65,129},{129,193},{2,66},{66,130... | collective-permute-start | bytes 1572872 | tf_op jit(solution)/shard_map/ppermute | solution.py:330
  124.2 23.6 %collective-permute-start = (bf16[256,1024]{1,0:T(8,128)(2,1)}, bf16[256,1024]{1,0:T(8,128)(2,1)}, u32[]{:S(2)}, u32[]{:S(2)}) collective-permute-start(bf16[256,1024]{1,0:T(8,128)(2,1)} %channel_relay.4), channel_id=1, source_target_pairs={{0,64},{64,128},{128,192},{1,65},{65,129},{129,193},{2,66},{66,130... | collective-permute-start | bytes 1572872 | tf_op jit(solution)/shard_map/ppermute | solution.py:330
  151.6 11.5 %copy-start.2 = (bf16[64,8,1024]{2,1,0:T(8,128)(2,1)}, bf16[64,8,1024]{2,1,0:T(8,128)(2,1)S(1)}, u32[]{:S(2)}) copy-start(bf16[64,8,1024]{2,1,0:T(8,128)(2,1)S(1)} %all-to-all-done.2) | copy-start | bytes 3145732
  151.6 46.4 %all-to-all-start.3 = ((bf16[64,8,1024]{2,1,0:T(8,128)(2,1)}), bf16[64,8,1024]{2,1,0:T(8,128)(2,1)}, u32[]{:S(2)}, u32[]{:S(2)}) async-start(bf16[64,8,1024]{2,1,0:T(8,128)(2,1)} %bitcast.63), calls=%async_computation.3 | async-start | bytes 2097152 | tf_op jit(solution)/shard_map/all_to_all | solution.py:302
  163.1 3.6 %copy-start.8 = (bf16[256,1024]{1,0:T(8,128)(2,1)S(1)}, bf16[256,1024]{1,0:T(8,128)(2,1)}, u32[]{:S(2)}) copy-start(bf16[256,1024]{1,0:T(8,128)(2,1)} %get-tuple-element.13.rows_ref) | copy-start | bytes 1572868
  167.9 2.4 copy-start.15
  167.9 28.6 %copy-start.7 = (bf16[1,4,256,256]{3,2,1,0:T(8,128)(2,1)S(1)}, bf16[1,4,256,256]{3,2,1,0:T(8,128)(2,1)}, u32[]{:S(2)}) copy-start(bf16[1,4,256,256]{3,2,1,0:T(8,128)(2,1)} %param.11) | copy-start | bytes 1572868
  170.3 39.3 %copy-start.13 = (bf16[1,4,256,256]{3,2,1,0:T(8,128)(2,1)S(1)}, bf16[1,4,256,256]{3,2,1,0:T(8,128)(2,1)}, u32[]{:S(2)}) copy-start(bf16[1,4,256,256]{3,2,1,0:T(8,128)(2,1)} %param.12) | copy-start | bytes 1572868
  170.3 15.1 %collective-permute-start.3 = (bf16[256,1024]{1,0:T(8,128)(2,1)S(1)}, bf16[256,1024]{1,0:T(8,128)(2,1)S(1)}, u32[]{:S(2)}, u32[]{:S(2)}) collective-permute-start(bf16[256,1024]{1,0:T(8,128)(2,1)S(1)} %copy-done.15), channel_id=1, source_target_pairs={{0,64},{64,128},{128,192},{1,65},{65,129},{129,193},{2,66},{66,130... | collective-permute-start | bytes 1572872 | tf_op jit(solution)/shard_map/ppermute | solution.py:330
  173.3 23.2 %collective-permute-start.2 = (bf16[256,1024]{1,0:T(8,128)(2,1)}, bf16[256,1024]{1,0:T(8,128)(2,1)S(1)}, u32[]{:S(2)}, u32[]{:S(2)}) collective-permute-start(bf16[256,1024]{1,0:T(8,128)(2,1)} %channel_relay.6), channel_id=1, source_target_pairs={{0,64},{64,128},{128,192},{1,65},{65,129},{129,193},{2,66},{66,130... | collective-permute-start | bytes 1572872 | tf_op jit(solution)/shard_map/ppermute | solution.py:330
  198.0 40.0 %all-to-all-start.4 = ((bf16[64,8,1024]{2,1,0:T(8,128)(2,1)}), bf16[64,8,1024]{2,1,0:T(8,128)(2,1)}, u32[]{:S(2)}, u32[]{:S(2)}) async-start(bf16[64,8,1024]{2,1,0:T(8,128)(2,1)} %bitcast.64), calls=%async_computation.4 | async-start | bytes 2097152 | tf_op jit(solution)/shard_map/all_to_all | solution.py:302
  244.0 6.5 %copy-start.14 = (bf16[256,1024]{1,0:T(8,128)(2,1)S(1)}, bf16[256,1024]{1,0:T(8,128)(2,1)}, u32[]{:S(2)}) copy-start(bf16[256,1024]{1,0:T(8,128)(2,1)} %channel_relay.4) | copy-start | bytes 1572868
  244.0 6.5 %copy-start.16 = (bf16[256,1024]{1,0:T(8,128)(2,1)S(1)}, bf16[256,1024]{1,0:T(8,128)(2,1)}, u32[]{:S(2)}) copy-start(bf16[256,1024]{1,0:T(8,128)(2,1)} %channel_relay.7) | copy-start | bytes 1572868
  244.0 57.7 %all-to-all-start.5 = ((bf16[64,16,1024]{2,1,0:T(8,128)(2,1)}), bf16[64,16,1024]{2,1,0:T(8,128)(2,1)}, u32[]{:S(2)}, u32[]{:S(2)}) async-start(bf16[64,16,1024]{2,1,0:T(8,128)(2,1)} %bitcast.53), calls=%async_computation.5 | async-start | bytes 4194304 | tf_op jit(solution)/shard_map/all_to_all | solution.py:302
  (3 other events, 3.2 us)

commit v5 on v4

--- a/solution.py
+++ b/solution.py
@@ -58,19 +58,24 @@
 
 def first_kernel(right_ref, rows_ref, out_ref):
     load = lambda block: rows_ref[pl.ds(block * BLOCK, BLOCK), :]
-    out_ref[...] = mix_first_tiles(right_ref, load, right_ref.shape[0]).astype(BF16)
-
-
-def mix_first(right, rows, chunk=256):
-    column = pl.BlockSpec((rows.shape[0], chunk), lambda c: (0, c))
-    return pl.pallas_call(
+    tiles = mix_first_tiles(right_ref, load, 2).astype(BF16)
+    out_ref[...] = tiles.reshape(out_ref.shape)
+
+
+def mix_first(right, rows, chunk=512):
+    count = rows.shape[0]
+    out = pl.pallas_call(
         first_kernel,
-        grid=(WIDTH // chunk,),
-        in_specs=[pl.BlockSpec(right.shape, lambda c: (0, 0, 0)), column],
-        out_specs=column,
-        out_shape=HBM(rows.shape, BF16),
+        grid=(count // (2 * BLOCK), WIDTH // chunk),
+        in_specs=[
+            pl.BlockSpec((2, BLOCK, BLOCK), lambda h, c: (h, 0, 0)),
+            pl.BlockSpec((2 * BLOCK, chunk), lambda h, c: (h, c)),
+        ],
+        out_specs=pl.BlockSpec((DEVICES, 1, 8, chunk), lambda h, c: (0, h, 0, c)),
+        out_shape=HBM((DEVICES, count // (2 * BLOCK), 8, WIDTH), BF16),
         **params("mix_first"),
     )(in_hbm(right), in_hbm(rows))
+    return out.reshape(count, WIDTH)
 
 
 def relayed_kernel(half, chunk, section_ref, right_ref, fresh_ref, *refs):
@@ -120,7 +125,7 @@
             pltpu.SemaphoreType.DMA((WIDTH // chunk,)),
         ],
         **params("mix_first_relayed"),
-    )(section, right, in_hbm(fresh), *(in_vmem(part) for part in received))
+    )(section, in_hbm(right), in_hbm(fresh), *(in_vmem(part) for part in received))
 
 
 def spread_kernel(half, rows_ref, out_ref):
@@ -141,10 +146,10 @@
 
 
 def spread(rows, half=None):
-    columns, place = (4 * BLOCK, VMEM) if half is None else (2 * BLOCK, HBM)
+    columns = 4 * BLOCK if half is None else 2 * BLOCK
     return pl.pallas_call(
         functools.partial(spread_kernel, half),
-        out_shape=place((rows.shape[0], columns), BF16),
+        out_shape=VMEM((rows.shape[0], columns), BF16),
         **params("spread"),
     )(rows)
 
@@ -158,47 +163,26 @@
     return left.transpose(1, 0, 2).reshape(-1, BLOCK)
 
 
-def second_kernel(*refs):
-    *in_refs, out_ref = refs
-    total = sum(
-        jnp.dot(left_ref[...], part_ref[...], preferred_element_type=F32)
-        for left_ref, part_ref in zip(in_refs[0::2], in_refs[1::2])
-    )
-    out_ref[...] = total.astype(BF16)
-
-
-def mix_second_last(lefts, parts, count=256):
-    rows = lefts[0].shape[0]
-    block = lambda width: pl.BlockSpec((count, width), lambda r: (r, 0))
-    specs, arrays = [], []
-    for left, part in zip(lefts, parts):
-        specs += [block(left.shape[1]), pl.BlockSpec(memory_space=VMEM)]
-        arrays += [in_hbm(left), in_vmem(part)]
-    return pl.pallas_call(
-        second_kernel,
-        grid=(rows // count,),
-        in_specs=specs,
-        out_specs=block(WIDTH),
-        out_shape=HBM((rows, WIDTH), BF16),
-        **params("mix_second_last"),
-    )(*arrays)
-
-
-def mix_second(pairs, chunk=256):
-    rows = pairs[0][0].shape[0]
+def second_kernel(left_ref, part_ref, *refs):
+    *held_refs, out_ref = refs
+    total = jnp.dot(left_ref[...], part_ref[...], preferred_element_type=F32)
+    for held_ref in held_refs:
+        total = total + held_ref[...]
+    out_ref[...] = total.astype(out_ref.dtype)
+
+
+def mix_second(left, part, kind=BF16, held=(), chunk=256):
+    rows = left.shape[0]
     column = lambda count: pl.BlockSpec((count, chunk), lambda c: (0, c))
-    specs, arrays = [], []
-    for left, part, place in pairs:
-        specs += [pl.BlockSpec(memory_space=VMEM), column(part.shape[0])]
-        arrays += [in_vmem(left), place(part)]
     return pl.pallas_call(
         second_kernel,
         grid=(WIDTH // chunk,),
-        in_specs=specs,
+        in_specs=[pl.BlockSpec(memory_space=VMEM), column(part.shape[0])]
+        + [column(rows) for _ in held],
         out_specs=column(rows),
-        out_shape=HBM((rows, WIDTH), BF16),
+        out_shape=HBM((rows, WIDTH), kind),
         **params("mix_second"),
-    )(*arrays)
+    )(in_vmem(left), in_vmem(part), *(in_hbm(array) for array in held))
 
 
 def gelu_of_twice(v):
@@ -253,24 +237,19 @@
 def channel_relay(returned, rows, block, weights, count=128):
     first = block % 2 == 0
     steps = BLOCK // count
-    start = 0 if first else block * steps
-    if first:
-        rows = in_vmem(rows[block * BLOCK : (block + 1) * BLOCK])
-        returned = in_vmem(returned)
-    else:
-        rows, returned = in_hbm(rows), in_hbm(returned)
+    returned = in_vmem(returned) if first else in_hbm(returned)
     return pl.pallas_call(
         functools.partial(relay_kernel, block % 2),
         grid=(steps,),
         in_specs=[
             pl.BlockSpec((2 * count, WIDTH), lambda s: (s, 0)),
-            pl.BlockSpec((count, WIDTH), lambda s: (start + s, 0)),
+            pl.BlockSpec((count, WIDTH), lambda s: (block * steps + s, 0)),
             *(fixed(array) for array in weights),
         ],
         out_specs=pl.BlockSpec((count, WIDTH), lambda s: (s, 0)),
         out_shape=HBM((BLOCK, WIDTH), BF16),
         **params("channel_relay"),
-    )(returned, rows, *weights)
+    )(returned, in_hbm(rows), *weights)
 
 
 def last_kernel(returned_ref, *refs):
@@ -319,7 +298,7 @@
     returned = []
     for half in range(2):
         matrix = spread(left_out[512 * half : 512 * half + 512])
-        mixed = mix_second([(matrix, arrived, in_vmem)])
+        mixed = mix_second(matrix, arrived)
         returned.append(exchange(mixed))
     firsts, currents, arrivals = [], [], []
     for half in range(2):
@@ -332,7 +311,9 @@
         currents.append(current.reshape(2, BLOCK, WIDTH))
         arrivals.append(exchange(leaving))
     first_out = jnp.concatenate(firsts)
-    mixed = mix_second_last([spread(by_output, half) for half in range(2)], arrivals)
+    left_in = [spread(by_output, half) for half in range(2)]
+    partial = mix_second(left_in[0], arrivals[0], F32)
+    mixed = mix_second(left_in[1], arrivals[1], BF16, (partial,))
     final = exchange(mixed)
     second_out = channel_last(final, currents, weights)
     return first_out[None], second_out.reshape(1, 1024, WIDTH)

time: 311 us -> 310 us (level)
  Pallas kernels: 43.5 us -> 48.7 us
  waiting for transfers between devices: 189 us -> 185 us
    all_to_all x6, waiting for transfers between devices: 146 us -> 142 us  [exchange(): lax.all_to_all(grouped, 'seq', split_axis=0, concat_axis=0, tiled=True)]
    pallas_call x8 -> x9, Pallas kernels: 20.2 us -> 22.3 us  [the longest x4 16.1 us: mix_second(): pl.pallas_call(second_kernel, grid=(WIDTH // chunk,), in_specs=[pl.BlockS...]
  transfers between devices with their start and end apart: 10 -> 10, of which waited for: 8 -> 8; matrix products, arithmetic and copies ran while one was open for 3% -> 2% of each run, Pallas kernels for 7% -> 9%
where the time goes in v5:
time: 310 us; the launch traced here: 308 us
  waiting for transfers between devices  185 us (60%)
  starting transfers between devices  63.6 us (21%)
  Pallas kernels  48.7 us (16%)
  local copies, waits for them, and re-layouts  6.59 us (2%)
    all_to_all x6, waiting for transfers between devices, exchange(): lax.all_to_all(grouped, 'seq', split_axis=0, concat_axis=0, tiled=True)  142 us
    all_to_all x6, starting transfers between devices, exchange(): lax.all_to_all(grouped, 'seq', split_axis=0, concat_axis=0, tiled=True)  53.8 us
    ppermute x4, waiting for transfers between devices, shards(): received.append(lax.ppermute(out, 'pipe', route))  43 us
    pallas_call x4, Pallas kernels, mix_second(): pl.pallas_call(second_kernel, grid=(WIDTH // chunk,), in_specs=[pl.BlockS...  16.1 us
    pallas_call x4, Pallas kernels, channel_relay(): pl.pallas_call(functools.partial(relay_kernel, block % 2), grid=(steps,),...  13.9 us
    ppermute x4, starting transfers between devices, shards(): received.append(lax.ppermute(out, 'pipe', route))  9.77 us
    pallas_call x1, Pallas kernels, channel_last(): pl.pallas_call(last_kernel, grid=(BLOCK // count,), in_specs=[pl.BlockSpe...  7.22 us
  transfers between devices with their start and end apart: 10, of which 8 were waited for; matrix products, arithmetic and copies ran while one was open for 2% of the time, Pallas kernels for 9%

profile of v5, /device:TPU:17, one launch (start us, length us, event | category | flops | bytes accessed | tf_op | source)
XLA Modules:
  0.0 308.0 jit_solution(6148295378856106493)
XLA Ops:
  0.6 4.5 %mix_first.1 = bf16[64,2,8,1024]{3,2,1,0:T(8,128)(2,1)} custom-call(bf16[4,256,256]{2,1,0:T(8,128)(2,1)} %bitcast.50, bf16[1024,1024]{1,0:T(8,128)(2,1)} %bitcast.43), custom_call_target="tpu_custom_call" | custom-call | tf_op jit(solution)/shard_map/mix_first/pallas_call | solution.py:67
  5.1 12.3 %all-to-all-start = ((bf16[64,16,1024]{2,1,0:T(8,128)(2,1)}), bf16[64,16,1024]{2,1,0:T(8,128)(2,1)S(1)}, u32[]{:S(2)}, u32[]{:S(2)}) async-start(bf16[64,16,1024]{2,1,0:T(8,128)(2,1)} %bitcast.48), calls=%async_computation | async-start | bytes 4194304 | tf_op jit(solution)/shard_map/all_to_all | solution.py:281
  19.7 48.9 %all-to-all-done = bf16[64,16,1024]{2,1,0:T(8,128)(2,1)S(1)} async-done(((bf16[64,16,1024]{2,1,0:T(8,128)(2,1)}), bf16[64,16,1024]{2,1,0:T(8,128)(2,1)S(1)}, u32[]{:S(2)}, u32[]{:S(2)}) %all-to-all-start) | async-done | bytes 2097184 | tf_op jit(solution)/shard_map/all_to_all | solution.py:281
  71.6 5.8 %all-to-all-start.1 = ((bf16[64,8,1024]{2,1,0:T(8,128)(2,1)}), bf16[64,8,1024]{2,1,0:T(8,128)(2,1)S(1)}, u32[]{:S(2)}, u32[]{:S(2)}) async-start(bf16[64,8,1024]{2,1,0:T(8,128)(2,1)} %bitcast.54), calls=%async_computation.1 | async-start | bytes 2097152 | tf_op jit(solution)/shard_map/all_to_all | solution.py:281
  78.9 3.0 mix_second.5
  81.9 24.0 %all-to-all-done.1 = bf16[64,8,1024]{2,1,0:T(8,128)(2,1)S(1)} async-done(((bf16[64,8,1024]{2,1,0:T(8,128)(2,1)}), bf16[64,8,1024]{2,1,0:T(8,128)(2,1)S(1)}, u32[]{:S(2)}, u32[]{:S(2)}) %all-to-all-start.1) | async-done | bytes 1048608 | tf_op jit(solution)/shard_map/all_to_all | solution.py:281
  106.9 6.2 %all-to-all-start.2 = ((bf16[64,8,1024]{2,1,0:T(8,128)(2,1)}), bf16[64,8,1024]{2,1,0:T(8,128)(2,1)S(1)}, u32[]{:S(2)}, u32[]{:S(2)}) async-start(bf16[64,8,1024]{2,1,0:T(8,128)(2,1)} %bitcast.53), calls=%async_computation.2 | async-start | bytes 2097152 | tf_op jit(solution)/shard_map/all_to_all | solution.py:281
  113.2 3.6 %channel_relay.5 = bf16[256,1024]{1,0:T(8,128)(2,1)} custom-call(bf16[512,1024]{1,0:T(8,128)(2,1)} %bitcast.41, bf16[1024,1024]{1,0:T(8,128)(2,1)} %bitcast.44, f32[1,1024]{1,0:T(1,128)S(1)} %copy-done.8, f32[1,1024]{1,0:T(1,128)S(1)} %copy-done.9, f32[1,1024]{1,0:T(1,128)S(1)} %copy-done.10, bf16[4,256,512]{2,1,0:T(8,128)(2,1)S(1)} %bitcast.27, ...), custom_call_target="tpu_custom_call" | custom-call | tf_op jit(solution)/shard_map/channel_relay/pallas_call | solution.py:241
  116.8 3.3 %channel_relay.4 = bf16[256,1024]{1,0:T(8,128)(2,1)} custom-call(bf16[512,1024]{1,0:T(8,128)(2,1)S(1)} %bitcast.42, bf16[1024,1024]{1,0:T(8,128)(2,1)} %bitcast.45, f32[1,1024]{1,0:T(1,128)S(1)} %copy-done.8, f32[1,1024]{1,0:T(1,128)S(1)} %copy-done.9, f32[1,1024]{1,0:T(1,128)S(1)} %copy-done.10, bf16[4,256,512]{2,1,0:T(8,128)(2,1)S(1)} %bitcast.28, ...), custom_call_target="tpu_custom_call" | custom-call | tf_op jit(solution)/shard_map/channel_relay/pallas_call | solution.py:241
  125.0 10.4 %collective-permute-done.2.refs_0_ = bf16[256,1024]{1,0:T(8,128)(2,1)} collective-permute-done((bf16[256,1024]{1,0:T(8,128)(2,1)}, bf16[256,1024]{1,0:T(8,128)(2,1)}, u32[]{:S(2)}, u32[]{:S(2)}) %collective-permute-start.2) | collective-permute-done | bytes 524320 | tf_op jit(solution)/shard_map/ppermute | solution.py:309
  135.4 11.2 %collective-permute-done.3.refs_1_ = bf16[256,1024]{1,0:T(8,128)(2,1)} collective-permute-done((bf16[256,1024]{1,0:T(8,128)(2,1)}, bf16[256,1024]{1,0:T(8,128)(2,1)}, u32[]{:S(2)}, u32[]{:S(2)}) %collective-permute-start.3) | collective-permute-done | bytes 524320 | tf_op jit(solution)/shard_map/ppermute | solution.py:309
  149.5 11.4 %all-to-all-start.4 = ((bf16[64,8,1024]{2,1,0:T(8,128)(2,1)}), bf16[64,8,1024]{2,1,0:T(8,128)(2,1)}, u32[]{:S(2)}, u32[]{:S(2)}) async-start(bf16[64,8,1024]{2,1,0:T(8,128)(2,1)} %bitcast.61), calls=%async_computation.4 | async-start | bytes 2097152 | tf_op jit(solution)/shard_map/all_to_all | solution.py:281
  160.9 3.5 %channel_relay.7 = bf16[256,1024]{1,0:T(8,128)(2,1)} custom-call(bf16[512,1024]{1,0:T(8,128)(2,1)} %bitcast.39, bf16[1024,1024]{1,0:T(8,128)(2,1)} %bitcast.46, f32[1,1024]{1,0:T(1,128)S(1)} %copy-done.8, f32[1,1024]{1,0:T(1,128)S(1)} %copy-done.9, f32[1,1024]{1,0:T(1,128)S(1)} %copy-done.10, bf16[4,256,512]{2,1,0:T(8,128)(2,1)S(1)} %bitcast.29, ...), custom_call_target="tpu_custom_call" | custom-call | tf_op jit(solution)/shard_map/channel_relay/pallas_call | solution.py:241
  165.7 3.4 %channel_relay.6 = bf16[256,1024]{1,0:T(8,128)(2,1)} custom-call(bf16[512,1024]{1,0:T(8,128)(2,1)S(1)} %bitcast.40, bf16[1024,1024]{1,0:T(8,128)(2,1)} %bitcast.47, f32[1,1024]{1,0:T(1,128)S(1)} %copy-done.8, f32[1,1024]{1,0:T(1,128)S(1)} %copy-done.9, f32[1,1024]{1,0:T(1,128)S(1)} %copy-done.10, bf16[4,256,512]{2,1,0:T(8,128)(2,1)S(1)} %bitcast.30, ...), custom_call_target="tpu_custom_call" | custom-call | tf_op jit(solution)/shard_map/channel_relay/pallas_call | solution.py:241
  169.1 3.0 collective-permute-start
  174.0 10.3 %collective-permute-done.refs_0_ = bf16[256,1024]{1,0:T(8,128)(2,1)S(1)} collective-permute-done((bf16[256,1024]{1,0:T(8,128)(2,1)}, bf16[256,1024]{1,0:T(8,128)(2,1)S(1)}, u32[]{:S(2)}, u32[]{:S(2)}) %collective-permute-start) | collective-permute-done | bytes 524320 | tf_op jit(solution)/shard_map/ppermute | solution.py:309
  184.3 11.1 %collective-permute-done.1.refs_1_ = bf16[256,1024]{1,0:T(8,128)(2,1)S(1)} collective-permute-done((bf16[256,1024]{1,0:T(8,128)(2,1)S(1)}, bf16[256,1024]{1,0:T(8,128)(2,1)S(1)}, u32[]{:S(2)}, u32[]{:S(2)}) %collective-permute-start.1) | collective-permute-done | bytes 524320 | tf_op jit(solution)/shard_map/ppermute | solution.py:309
  198.0 11.5 %all-to-all-start.3 = ((bf16[64,8,1024]{2,1,0:T(8,128)(2,1)}), bf16[64,8,1024]{2,1,0:T(8,128)(2,1)}, u32[]{:S(2)}, u32[]{:S(2)}) async-start(bf16[64,8,1024]{2,1,0:T(8,128)(2,1)} %bitcast.62), calls=%async_computation.3 | async-start | bytes 2097152 | tf_op jit(solution)/shard_map/all_to_all | solution.py:281
  212.0 4.9 %mix_second.6.refs_0_ = f32[1024,1024]{1,0:T(8,128)} custom-call(bf16[1024,512]{1,0:T(8,128)(2,1)S(1)} %spread.7.left_ref, bf16[512,1024]{1,0:T(8,128)(2,1)} %bitcast.18.part_ref), custom_call_target="tpu_custom_call" | custom-call | tf_op jit(solution)/shard_map/mix_second/pallas_call | solution.py:177
  216.9 21.1 %all-to-all-done.3 = bf16[64,8,1024]{2,1,0:T(8,128)(2,1)} async-done(((bf16[64,8,1024]{2,1,0:T(8,128)(2,1)}), bf16[64,8,1024]{2,1,0:T(8,128)(2,1)}, u32[]{:S(2)}, u32[]{:S(2)}) %all-to-all-start.3) | async-done | bytes 1048608 | tf_op jit(solution)/shard_map/all_to_all | solution.py:281
  238.0 5.2 %mix_second.7 = bf16[1024,1024]{1,0:T(8,128)(2,1)} custom-call(bf16[1024,512]{1,0:T(8,128)(2,1)S(1)} %copy-done.7, bf16[512,1024]{1,0:T(8,128)(2,1)} %bitcast.16.part_ref, f32[1024,1024]{1,0:T(8,128)} %mix_second.6.refs_0_), custom_call_target="tpu_custom_call" | custom-call | tf_op jit(solution)/shard_map/mix_second/pallas_call | solution.py:177
  243.2 6.5 %all-to-all-start.5 = ((bf16[64,16,1024]{2,1,0:T(8,128)(2,1)}), bf16[64,16,1024]{2,1,0:T(8,128)(2,1)}, u32[]{:S(2)}, u32[]{:S(2)}) async-start(bf16[64,16,1024]{2,1,0:T(8,128)(2,1)} %bitcast.49), calls=%async_computation.5 | async-start | bytes 4194304 | tf_op jit(solution)/shard_map/all_to_all | solution.py:281
  252.6 48.2 %all-to-all-done.5 = bf16[64,16,1024]{2,1,0:T(8,128)(2,1)} async-done(((bf16[64,16,1024]{2,1,0:T(8,128)(2,1)}), bf16[64,16,1024]{2,1,0:T(8,128)(2,1)}, u32[]{:S(2)}, u32[]{:S(2)}) %all-to-all-start.5) | async-done | bytes 2097184 | tf_op jit(solution)/shard_map/all_to_all | solution.py:281
  300.8 7.2 %channel_last.1 = bf16[4,256,1024]{2,1,0:T(8,128)(2,1)} custom-call(bf16[1024,1024]{1,0:T(8,128)(2,1)} %bitcast.20.returned_ref, bf16[2,256,1024]{2,1,0:T(8,128)(2,1)} %bitcast.59, bf16[2,256,1024]{2,1,0:T(8,128)(2,1)} %bitcast.60, f32[1,1024]{1,0:T(1,128)S(1)} %copy-done.8, f32[1,1024]{1,0:T(1,128)S(1)} %copy-done.9, f32[1,1024]{1,0:T(1,128)S(1)} %copy-done.10, ...), custom_call_target="tpu_custom_call" | custom-call | tf_op jit(solution)/shard_map/channel_last/pallas_call | solution.py:265
  (52 shorter events, 26.3 us)
Async XLA Ops:
  5.1 12.3 %copy-start.11 = (bf16[1,4,256,256]{3,2,1,0:T(8,128)(2,1)S(1)}, bf16[1,4,256,256]{3,2,1,0:T(8,128)(2,1)}, u32[]{:S(2)}) copy-start(bf16[1,4,256,256]{3,2,1,0:T(8,128)(2,1)} %param.12) | copy-start | bytes 1572868
  5.1 63.5 %all-to-all-start = ((bf16[64,16,1024]{2,1,0:T(8,128)(2,1)}), bf16[64,16,1024]{2,1,0:T(8,128)(2,1)S(1)}, u32[]{:S(2)}, u32[]{:S(2)}) async-start(bf16[64,16,1024]{2,1,0:T(8,128)(2,1)} %bitcast.48), calls=%async_computation | async-start | bytes 4194304 | tf_op jit(solution)/shard_map/all_to_all | solution.py:281
  71.6 34.4 %all-to-all-start.1 = ((bf16[64,8,1024]{2,1,0:T(8,128)(2,1)}), bf16[64,8,1024]{2,1,0:T(8,128)(2,1)S(1)}, u32[]{:S(2)}, u32[]{:S(2)}) async-start(bf16[64,8,1024]{2,1,0:T(8,128)(2,1)} %bitcast.54), calls=%async_computation.1 | async-start | bytes 2097152 | tf_op jit(solution)/shard_map/all_to_all | solution.py:281
  78.9 34.2 %copy-start.9 = (f32[1,1024]{1,0:T(1,128)S(1)}, f32[1,1024]{1,0:T(1,128)}, u32[]{:S(2)}) copy-start(f32[1,1024]{1,0:T(1,128)} %refs_3_.1) | copy-start | bytes 12292
  78.9 34.2 %copy-start.10 = (f32[1,1024]{1,0:T(1,128)S(1)}, f32[1,1024]{1,0:T(1,128)}, u32[]{:S(2)}) copy-start(f32[1,1024]{1,0:T(1,128)} %refs_4_.1) | copy-start | bytes 12292
  81.9 31.2 %copy-start = (bf16[1,4,256,512]{3,2,1,0:T(8,128)(2,1)S(1)}, bf16[1,4,256,512]{3,2,1,0:T(8,128)(2,1)}, u32[]{:S(2)}) copy-start(bf16[1,4,256,512]{3,2,1,0:T(8,128)(2,1)} %param.16) | copy-start | bytes 3145732
  81.9 31.3 %copy-start.1 = (bf16[1,4,4,128,256]{4,3,2,1,0:T(8,128)(2,1)S(1)}, bf16[1,4,4,128,256]{4,3,2,1,0:T(8,128)(2,1)}, u32[]{:S(2)}) copy-start(bf16[1,4,4,128,256]{4,3,2,1,0:T(8,128)(2,1)} %param.17) | copy-start | bytes 3145732
  81.9 31.3 %copy-start.8 = (f32[1,1024]{1,0:T(1,128)S(1)}, f32[1,1024]{1,0:T(1,128)}, u32[]{:S(2)}) copy-start(f32[1,1024]{1,0:T(1,128)} %refs_2_.9) | copy-start | bytes 12292
  106.9 42.6 %all-to-all-start.2 = ((bf16[64,8,1024]{2,1,0:T(8,128)(2,1)}), bf16[64,8,1024]{2,1,0:T(8,128)(2,1)S(1)}, u32[]{:S(2)}, u32[]{:S(2)}) async-start(bf16[64,8,1024]{2,1,0:T(8,128)(2,1)} %bitcast.53), calls=%async_computation.2 | async-start | bytes 2097152 | tf_op jit(solution)/shard_map/all_to_all | solution.py:281
  113.2 3.6 %copy-start.5 = (bf16[64,8,1024]{2,1,0:T(8,128)(2,1)S(1)}, bf16[64,8,1024]{2,1,0:T(8,128)(2,1)}, u32[]{:S(2)}) copy-start(bf16[64,8,1024]{2,1,0:T(8,128)(2,1)} %copy-done.4) | copy-start | bytes 3145732
  120.1 15.2 %collective-permute-start.2 = (bf16[256,1024]{1,0:T(8,128)(2,1)}, bf16[256,1024]{1,0:T(8,128)(2,1)}, u32[]{:S(2)}, u32[]{:S(2)}) collective-permute-start(bf16[256,1024]{1,0:T(8,128)(2,1)} %channel_relay.4), channel_id=1, source_target_pairs={{0,64},{64,128},{128,192},{1,65},{65,129},{129,193},{2,66},{66,130... | collective-permute-start | bytes 1572872 | tf_op jit(solution)/shard_map/ppermute | solution.py:309
  123.0 23.6 %collective-permute-start.3 = (bf16[256,1024]{1,0:T(8,128)(2,1)}, bf16[256,1024]{1,0:T(8,128)(2,1)}, u32[]{:S(2)}, u32[]{:S(2)}) collective-permute-start(bf16[256,1024]{1,0:T(8,128)(2,1)} %channel_relay.5), channel_id=1, source_target_pairs={{0,64},{64,128},{128,192},{1,65},{65,129},{129,193},{2,66},{66,130... | collective-permute-start | bytes 1572872 | tf_op jit(solution)/shard_map/ppermute | solution.py:309
  149.5 11.5 %copy-start.2 = (bf16[64,8,1024]{2,1,0:T(8,128)(2,1)}, bf16[64,8,1024]{2,1,0:T(8,128)(2,1)S(1)}, u32[]{:S(2)}) copy-start(bf16[64,8,1024]{2,1,0:T(8,128)(2,1)S(1)} %all-to-all-done.2) | copy-start | bytes 3145732
  149.5 48.5 %all-to-all-start.4 = ((bf16[64,8,1024]{2,1,0:T(8,128)(2,1)}), bf16[64,8,1024]{2,1,0:T(8,128)(2,1)}, u32[]{:S(2)}, u32[]{:S(2)}) async-start(bf16[64,8,1024]{2,1,0:T(8,128)(2,1)} %bitcast.61), calls=%async_computation.4 | async-start | bytes 2097152 | tf_op jit(solution)/shard_map/all_to_all | solution.py:281
  164.4 1.2 copy-start.3
  165.7 6.4 %copy-start.14 = (bf16[256,1024]{1,0:T(8,128)(2,1)S(1)}, bf16[256,1024]{1,0:T(8,128)(2,1)}, u32[]{:S(2)}) copy-start(bf16[256,1024]{1,0:T(8,128)(2,1)} %channel_relay.7) | copy-start | bytes 1572868
  169.1 40.5 %copy-start.12 = (bf16[1,4,256,256]{3,2,1,0:T(8,128)(2,1)S(1)}, bf16[1,4,256,256]{3,2,1,0:T(8,128)(2,1)}, u32[]{:S(2)}) copy-start(bf16[1,4,256,256]{3,2,1,0:T(8,128)(2,1)} %param.12) | copy-start | bytes 1572868
  169.1 15.3 %collective-permute-start = (bf16[256,1024]{1,0:T(8,128)(2,1)}, bf16[256,1024]{1,0:T(8,128)(2,1)S(1)}, u32[]{:S(2)}, u32[]{:S(2)}) collective-permute-start(bf16[256,1024]{1,0:T(8,128)(2,1)} %channel_relay.6), channel_id=1, source_target_pairs={{0,64},{64,128},{128,192},{1,65},{65,129},{129,193},{2,66},{66,130... | collective-permute-start | bytes 1572872 | tf_op jit(solution)/shard_map/ppermute | solution.py:309
  172.1 23.4 %collective-permute-start.1 = (bf16[256,1024]{1,0:T(8,128)(2,1)S(1)}, bf16[256,1024]{1,0:T(8,128)(2,1)S(1)}, u32[]{:S(2)}, u32[]{:S(2)}) collective-permute-start(bf16[256,1024]{1,0:T(8,128)(2,1)S(1)} %copy-done.14), channel_id=1, source_target_pairs={{0,64},{64,128},{128,192},{1,65},{65,129},{129,193},{2,66},{66,130... | collective-permute-start | bytes 1572872 | tf_op jit(solution)/shard_map/ppermute | solution.py:309
  198.0 40.0 %all-to-all-start.3 = ((bf16[64,8,1024]{2,1,0:T(8,128)(2,1)}), bf16[64,8,1024]{2,1,0:T(8,128)(2,1)}, u32[]{:S(2)}, u32[]{:S(2)}) async-start(bf16[64,8,1024]{2,1,0:T(8,128)(2,1)} %bitcast.62), calls=%async_computation.3 | async-start | bytes 2097152 | tf_op jit(solution)/shard_map/all_to_all | solution.py:281
  212.0 26.0 %copy-start.7 = (bf16[1024,512]{1,0:T(8,128)(2,1)S(1)}, bf16[1024,512]{1,0:T(8,128)(2,1)}, u32[]{:S(2)}) copy-start(bf16[1024,512]{1,0:T(8,128)(2,1)} %copy-done.6) | copy-start | bytes 3145732
  243.2 6.5 %copy-start.13 = (bf16[256,1024]{1,0:T(8,128)(2,1)S(1)}, bf16[256,1024]{1,0:T(8,128)(2,1)}, u32[]{:S(2)}) copy-start(bf16[256,1024]{1,0:T(8,128)(2,1)} %channel_relay.4) | copy-start | bytes 1572868
  243.2 6.5 %copy-start.15 = (bf16[256,1024]{1,0:T(8,128)(2,1)S(1)}, bf16[256,1024]{1,0:T(8,128)(2,1)}, u32[]{:S(2)}) copy-start(bf16[256,1024]{1,0:T(8,128)(2,1)} %channel_relay.7) | copy-start | bytes 1572868
  243.2 57.6 %all-to-all-start.5 = ((bf16[64,16,1024]{2,1,0:T(8,128)(2,1)}), bf16[64,16,1024]{2,1,0:T(8,128)(2,1)}, u32[]{:S(2)}, u32[]{:S(2)}) async-start(bf16[64,16,1024]{2,1,0:T(8,128)(2,1)} %bitcast.49), calls=%async_computation.5 | async-start | bytes 4194304 | tf_op jit(solution)/shard_map/all_to_all | solution.py:281
  (2 other events, 1.9 us)

commit v6 on v5

--- a/solution.py
+++ b/solution.py
@@ -15,6 +15,7 @@
 BF16 = jnp.bfloat16
 HBM = pltpu.MemorySpace.HBM
 VMEM = pltpu.MemorySpace.VMEM
+WHOLE = pl.BlockSpec(memory_space=VMEM)
 
 
 def in_hbm(array):
@@ -230,26 +231,59 @@
     out_ref[...] = channel_rows((place,), arrived, (rows_ref,), weight_refs)
 
 
-def fixed(array):
-    return pl.BlockSpec(array.shape, lambda s: (0,) * array.ndim)
-
-
 def channel_relay(returned, rows, block, weights, count=128):
-    first = block % 2 == 0
     steps = BLOCK // count
-    returned = in_vmem(returned) if first else in_hbm(returned)
     return pl.pallas_call(
         functools.partial(relay_kernel, block % 2),
         grid=(steps,),
         in_specs=[
             pl.BlockSpec((2 * count, WIDTH), lambda s: (s, 0)),
             pl.BlockSpec((count, WIDTH), lambda s: (block * steps + s, 0)),
-            *(fixed(array) for array in weights),
+            *(WHOLE for _ in weights),
         ],
         out_specs=pl.BlockSpec((count, WIDTH), lambda s: (s, 0)),
         out_shape=HBM((BLOCK, WIDTH), BF16),
         **params("channel_relay"),
-    )(returned, in_hbm(rows), *weights)
+    )(in_hbm(returned), in_hbm(rows), *weights)
+
+
+def relay_first_kernel(start, returned_ref, head_ref, rows_ref, *refs):
+    *weight_refs, out_ref, rows_buf, out_buf, sems = refs
+    count = head_ref.shape[0]
+    rest = pltpu.make_async_copy(
+        rows_ref.at[pl.ds(start + count, count), :], rows_buf, sems.at[0]
+    )
+    rest.start()
+    copies = []
+    for n, source_ref in enumerate((head_ref, rows_buf)):
+        if n:
+            rest.wait()
+        arrived = arrived_tiles(returned_ref.at[pl.ds(2 * n * count, 2 * count), :], 1)
+        part = pl.ds(n * count, count)
+        out_buf[part, :] = channel_rows((0,), arrived, (source_ref,), weight_refs)
+        copy = pltpu.make_async_copy(out_buf.at[part, :], out_ref.at[part, :], sems.at[1 + n])
+        copy.start()
+        copies.append(copy)
+    for copy in copies:
+        copy.wait()
+
+
+def channel_relay_first(returned, rows, block, weights, earlier, count=128):
+    start = block * BLOCK
+    held, *_ = lax.optimization_barrier((rows, *earlier))
+    head = in_vmem(held[start : start + count])
+    return pl.pallas_call(
+        functools.partial(relay_first_kernel, start),
+        in_specs=[WHOLE, WHOLE, pl.BlockSpec(memory_space=pl.ANY), *(WHOLE for _ in weights)],
+        out_specs=pl.BlockSpec(memory_space=pl.ANY),
+        out_shape=HBM((BLOCK, WIDTH), BF16),
+        scratch_shapes=[
+            VMEM((count, WIDTH), BF16),
+            VMEM((BLOCK, WIDTH), BF16),
+            pltpu.SemaphoreType.DMA((3,)),
+        ],
+        **params("channel_relay_first"),
+    )(in_vmem(returned), head, in_hbm(rows), *weights)
 
 
 def last_kernel(returned_ref, *refs):
@@ -268,7 +302,7 @@
         in_specs=[
             pl.BlockSpec((4 * count, WIDTH), lambda s: (s, 0)),
             *(pair for _ in parts),
-            *(fixed(array) for array in weights),
+            *(WHOLE for _ in weights),
         ],
         out_specs=pl.BlockSpec((4, count, WIDTH), lambda s: (0, s, 0)),
         out_shape=HBM((4, BLOCK, WIDTH), BF16),
@@ -289,7 +323,9 @@
     section = lax.axis_index("pipe").reshape(1)
     rows, right, left = in_flight[0], right_factor[0], left_factor[0]
     weights = (gate_gain, gate_bias, norm_gain, w_up[0], w_down[0].reshape(4, 512, 256))
-    route = [(n, n + 1) for n in range(lax.axis_size("pipe") - 1)]
+    weights = tuple(in_vmem(array) for array in weights)
+    sections = lax.axis_size("pipe")
+    route = [(n, (n + 1) % sections) for n in range(sections)]
     leaving = mix_first(right, rows)
     arrived = exchange(leaving)
     left_held, _ = lax.optimization_barrier((left, leaving))
@@ -304,7 +340,12 @@
     for half in range(2):
         received = []
         for block in (2 * half, 2 * half + 1):
-            out = channel_relay(returned[half], rows, block, weights)
+            if block % 2:
+                out = channel_relay(returned[half], rows, block, weights)
+            else:
+                out = channel_relay_first(
+                    returned[half], rows, block, weights, firsts[-1:]
+                )
             firsts.append(out)
             received.append(lax.ppermute(out, "pipe", route))
         leaving, current = mix_first_relayed(section, right, fresh_rows, received, half)

time: 310 us -> 311 us (level)
  the two profiles are of different devices: /device:TPU:17 before, /device:TPU:1 now
where the time goes in v6:
time: 311 us; the launch traced here: 310 us
  waiting for transfers between devices  191 us (61%)
  starting transfers between devices  57.7 us (19%)
  Pallas kernels  49.4 us (16%)
  local copies, waits for them, and re-layouts  8.53 us (3%)
    all_to_all x6, waiting for transfers between devices, exchange(): lax.all_to_all(grouped, 'seq', split_axis=0, concat_axis=0, tiled=True)  142 us
    all_to_all x6, starting transfers between devices, exchange(): lax.all_to_all(grouped, 'seq', split_axis=0, concat_axis=0, tiled=True)  54.7 us
    ppermute x4, waiting for transfers between devices, shards(): received.append(lax.ppermute(out, 'pipe', route))  48.3 us
    pallas_call x4, Pallas kernels, mix_second(): pl.pallas_call(second_kernel, grid=(WIDTH // chunk,), in_specs=[pl.BlockS...  16 us
    pallas_call x2, Pallas kernels, mix_first_relayed(): pl.pallas_call(functools.partial(relayed_kernel, half, chunk), grid=(WIDT...  7.46 us
    pallas_call x1, Pallas kernels, channel_last(): pl.pallas_call(last_kernel, grid=(BLOCK // count,), in_specs=[pl.BlockSpe...  7.13 us
    pallas_call x2, Pallas kernels, channel_relay(): pl.pallas_call(functools.partial(relay_kernel, block % 2), grid=(steps,),...  7.13 us
  transfers between devices with their start and end apart: 10, of which 8 were waited for; matrix products, arithmetic and copies ran while one was open for 3% of the time, Pallas kernels for 10%

profile of v6, /device:TPU:1, one launch (start us, length us, event | category | flops | bytes accessed | tf_op | source)
XLA Modules:
  0.0 310.1 jit_solution(15177751680700202411)
XLA Ops:
  0.6 4.5 %mix_first.1 = bf16[64,2,8,1024]{3,2,1,0:T(8,128)(2,1)} custom-call(bf16[4,256,256]{2,1,0:T(8,128)(2,1)} %bitcast.52, bf16[1024,1024]{1,0:T(8,128)(2,1)} %bitcast.43), custom_call_target="tpu_custom_call" | custom-call | tf_op jit(solution)/shard_map/mix_first/pallas_call | solution.py:68
  5.1 13.1 %all-to-all-start = ((bf16[64,16,1024]{2,1,0:T(8,128)(2,1)}), bf16[64,16,1024]{2,1,0:T(8,128)(2,1)S(1)}, u32[]{:S(2)}, u32[]{:S(2)}) async-start(bf16[64,16,1024]{2,1,0:T(8,128)(2,1)} %bitcast.50), calls=%async_computation | async-start | bytes 4194304 | tf_op jit(solution)/shard_map/all_to_all | solution.py:315
  20.5 48.9 %all-to-all-done = bf16[64,16,1024]{2,1,0:T(8,128)(2,1)S(1)} async-done(((bf16[64,16,1024]{2,1,0:T(8,128)(2,1)}), bf16[64,16,1024]{2,1,0:T(8,128)(2,1)S(1)}, u32[]{:S(2)}, u32[]{:S(2)}) %all-to-all-start) | async-done | bytes 2097184 | tf_op jit(solution)/shard_map/all_to_all | solution.py:315
  69.4 3.0 mix_second.4
  72.4 5.8 %all-to-all-start.1 = ((bf16[64,8,1024]{2,1,0:T(8,128)(2,1)}), bf16[64,8,1024]{2,1,0:T(8,128)(2,1)S(1)}, u32[]{:S(2)}, u32[]{:S(2)}) async-start(bf16[64,8,1024]{2,1,0:T(8,128)(2,1)} %bitcast.56), calls=%async_computation.1 | async-start | bytes 2097152 | tf_op jit(solution)/shard_map/all_to_all | solution.py:315
  79.7 3.0 mix_second.5
  82.7 24.1 %all-to-all-done.1 = bf16[64,8,1024]{2,1,0:T(8,128)(2,1)S(1)} async-done(((bf16[64,8,1024]{2,1,0:T(8,128)(2,1)}), bf16[64,8,1024]{2,1,0:T(8,128)(2,1)S(1)}, u32[]{:S(2)}, u32[]{:S(2)}) %all-to-all-start.1) | async-done | bytes 1048608 | tf_op jit(solution)/shard_map/all_to_all | solution.py:315
  107.7 6.2 %all-to-all-start.2 = ((bf16[64,8,1024]{2,1,0:T(8,128)(2,1)}), bf16[64,8,1024]{2,1,0:T(8,128)(2,1)S(1)}, u32[]{:S(2)}, u32[]{:S(2)}) async-start(bf16[64,8,1024]{2,1,0:T(8,128)(2,1)} %bitcast.55), calls=%async_computation.2 | async-start | bytes 2097152 | tf_op jit(solution)/shard_map/all_to_all | solution.py:315
  115.0 3.6 %channel_relay.2 = bf16[256,1024]{1,0:T(8,128)(2,1)} custom-call(bf16[512,1024]{1,0:T(8,128)(2,1)} %bitcast.41, bf16[1024,1024]{1,0:T(8,128)(2,1)} %bitcast.45, f32[1,1024]{1,0:T(1,128)S(1)} %copy-done.8, f32[1,1024]{1,0:T(1,128)S(1)} %copy-done.9, f32[1,1024]{1,0:T(1,128)S(1)} %copy-done.10, bf16[4,256,512]{2,1,0:T(8,128)(2,1)S(1)} %bitcast.27, ...), custom_call_target="tpu_custom_call" | custom-call | tf_op jit(solution)/shard_map/channel_relay/pallas_call | solution.py:236
  124.0 12.1 %collective-permute-done.3.refs_1_ = bf16[256,1024]{1,0:T(8,128)(2,1)} collective-permute-done((bf16[256,1024]{1,0:T(8,128)(2,1)}, bf16[256,1024]{1,0:T(8,128)(2,1)}, u32[]{:S(2)}, u32[]{:S(2)}) %collective-permute-start.3) | collective-permute-done | bytes 524320 | tf_op jit(solution)/shard_map/ppermute | solution.py:350
  136.1 11.2 %collective-permute-done.2.refs_0_ = bf16[256,1024]{1,0:T(8,128)(2,1)} collective-permute-done((bf16[256,1024]{1,0:T(8,128)(2,1)}, bf16[256,1024]{1,0:T(8,128)(2,1)}, u32[]{:S(2)}, u32[]{:S(2)}) %collective-permute-start.2) | collective-permute-done | bytes 524320 | tf_op jit(solution)/shard_map/ppermute | solution.py:350
  147.3 3.9 %mix_first_relayed.3 = (bf16[512,1024]{1,0:T(8,128)(2,1)}, bf16[512,1024]{1,0:T(8,128)(2,1)}) custom-call(s32[1]{0:T(128)} %bitcast.14.section_ref, bf16[4,256,256]{2,1,0:T(8,128)(2,1)} %bitcast.53, bf16[1024,1024]{1,0:T(8,128)(2,1)} %fresh_ref.3, bf16[256,1024]{1,0:T(8,128)(2,1)} %collective-permute-done.2.refs_0_, ...), custom_call_target="tpu_custom_call" | custom-call | tf_op jit(solution)/shard_map/mix_first_relayed/pallas_call | solution.py:113
  151.2 11.4 %all-to-all-start.4 = ((bf16[64,8,1024]{2,1,0:T(8,128)(2,1)}), bf16[64,8,1024]{2,1,0:T(8,128)(2,1)}, u32[]{:S(2)}, u32[]{:S(2)}) async-start(bf16[64,8,1024]{2,1,0:T(8,128)(2,1)} %bitcast.63), calls=%async_computation.4 | async-start | bytes 2097152 | tf_op jit(solution)/shard_map/all_to_all | solution.py:315
  163.6 3.5 %channel_relay.3 = bf16[256,1024]{1,0:T(8,128)(2,1)} custom-call(bf16[512,1024]{1,0:T(8,128)(2,1)} %bitcast.39, bf16[1024,1024]{1,0:T(8,128)(2,1)} %bitcast.48, f32[1,1024]{1,0:T(1,128)S(1)} %copy-done.8, f32[1,1024]{1,0:T(1,128)S(1)} %copy-done.9, f32[1,1024]{1,0:T(1,128)S(1)} %copy-done.10, bf16[4,256,512]{2,1,0:T(8,128)(2,1)S(1)} %bitcast.29, ...), custom_call_target="tpu_custom_call" | custom-call | tf_op jit(solution)/shard_map/channel_relay/pallas_call | solution.py:236
  171.4 13.8 %collective-permute-done.1.refs_1_ = bf16[256,1024]{1,0:T(8,128)(2,1)S(1)} collective-permute-done((bf16[256,1024]{1,0:T(8,128)(2,1)S(1)}, bf16[256,1024]{1,0:T(8,128)(2,1)S(1)}, u32[]{:S(2)}, u32[]{:S(2)}) %collective-permute-start.1) | collective-permute-done | bytes 524320 | tf_op jit(solution)/shard_map/ppermute | solution.py:350
  185.3 11.1 %collective-permute-done.refs_0_ = bf16[256,1024]{1,0:T(8,128)(2,1)S(1)} collective-permute-done((bf16[256,1024]{1,0:T(8,128)(2,1)}, bf16[256,1024]{1,0:T(8,128)(2,1)S(1)}, u32[]{:S(2)}, u32[]{:S(2)}) %collective-permute-start) | collective-permute-done | bytes 524320 | tf_op jit(solution)/shard_map/ppermute | solution.py:350
  196.4 3.6 %mix_first_relayed.2 = (bf16[512,1024]{1,0:T(8,128)(2,1)}, bf16[512,1024]{1,0:T(8,128)(2,1)}) custom-call(s32[1]{0:T(128)} %bitcast.14.section_ref, bf16[4,256,256]{2,1,0:T(8,128)(2,1)} %bitcast.54, bf16[1024,1024]{1,0:T(8,128)(2,1)} %fresh_ref.3, bf16[256,1024]{1,0:T(8,128)(2,1)S(1)} %collective-permute-done.refs_0_, ...), custom_call_target="tpu_custom_call" | custom-call | tf_op jit(solution)/shard_map/mix_first_relayed/pallas_call | solution.py:113
  200.0 11.7 %all-to-all-start.3 = ((bf16[64,8,1024]{2,1,0:T(8,128)(2,1)}), bf16[64,8,1024]{2,1,0:T(8,128)(2,1)}, u32[]{:S(2)}, u32[]{:S(2)}) async-start(bf16[64,8,1024]{2,1,0:T(8,128)(2,1)} %bitcast.64), calls=%async_computation.3 | async-start | bytes 2097152 | tf_op jit(solution)/shard_map/all_to_all | solution.py:315
  214.1 4.9 %mix_second.6.refs_0_ = f32[1024,1024]{1,0:T(8,128)} custom-call(bf16[1024,512]{1,0:T(8,128)(2,1)S(1)} %spread.7.left_ref, bf16[512,1024]{1,0:T(8,128)(2,1)} %bitcast.18.part_ref), custom_call_target="tpu_custom_call" | custom-call | tf_op jit(solution)/shard_map/mix_second/pallas_call | solution.py:178
  219.0 21.1 %all-to-all-done.3 = bf16[64,8,1024]{2,1,0:T(8,128)(2,1)} async-done(((bf16[64,8,1024]{2,1,0:T(8,128)(2,1)}), bf16[64,8,1024]{2,1,0:T(8,128)(2,1)}, u32[]{:S(2)}, u32[]{:S(2)}) %all-to-all-start.3) | async-done | bytes 1048608 | tf_op jit(solution)/shard_map/all_to_all | solution.py:315
  240.1 5.2 %mix_second.7 = bf16[1024,1024]{1,0:T(8,128)(2,1)} custom-call(bf16[1024,512]{1,0:T(8,128)(2,1)S(1)} %copy-done.7, bf16[512,1024]{1,0:T(8,128)(2,1)} %bitcast.16.part_ref, f32[1024,1024]{1,0:T(8,128)} %mix_second.6.refs_0_), custom_call_target="tpu_custom_call" | custom-call | tf_op jit(solution)/shard_map/mix_second/pallas_call | solution.py:178
  245.3 6.5 %all-to-all-start.5 = ((bf16[64,16,1024]{2,1,0:T(8,128)(2,1)}), bf16[64,16,1024]{2,1,0:T(8,128)(2,1)}, u32[]{:S(2)}, u32[]{:S(2)}) async-start(bf16[64,16,1024]{2,1,0:T(8,128)(2,1)} %bitcast.51), calls=%async_computation.5 | async-start | bytes 4194304 | tf_op jit(solution)/shard_map/all_to_all | solution.py:315
  254.7 48.2 %all-to-all-done.5 = bf16[64,16,1024]{2,1,0:T(8,128)(2,1)} async-done(((bf16[64,16,1024]{2,1,0:T(8,128)(2,1)}), bf16[64,16,1024]{2,1,0:T(8,128)(2,1)}, u32[]{:S(2)}, u32[]{:S(2)}) %all-to-all-start.5) | async-done | bytes 2097184 | tf_op jit(solution)/shard_map/all_to_all | solution.py:315
  302.9 7.1 %channel_last.1 = bf16[4,256,1024]{2,1,0:T(8,128)(2,1)} custom-call(bf16[1024,1024]{1,0:T(8,128)(2,1)} %bitcast.20.returned_ref, bf16[2,256,1024]{2,1,0:T(8,128)(2,1)} %bitcast.61, bf16[2,256,1024]{2,1,0:T(8,128)(2,1)} %bitcast.62, f32[1,1024]{1,0:T(1,128)S(1)} %copy-done.8, f32[1,1024]{1,0:T(1,128)S(1)} %copy-done.9, f32[1,1024]{1,0:T(1,128)S(1)} %copy-done.10, ...), custom_call_target="tpu_custom_call" | custom-call | tf_op jit(solution)/shard_map/channel_last/pallas_call | solution.py:299
  (54 shorter events, 21.6 us)
Async XLA Ops:
  5.1 13.1 %copy-start.11 = (bf16[1,4,256,256]{3,2,1,0:T(8,128)(2,1)S(1)}, bf16[1,4,256,256]{3,2,1,0:T(8,128)(2,1)}, u32[]{:S(2)}) copy-start(bf16[1,4,256,256]{3,2,1,0:T(8,128)(2,1)} %param.12) | copy-start | bytes 1572868
  5.1 64.3 %all-to-all-start = ((bf16[64,16,1024]{2,1,0:T(8,128)(2,1)}), bf16[64,16,1024]{2,1,0:T(8,128)(2,1)S(1)}, u32[]{:S(2)}, u32[]{:S(2)}) async-start(bf16[64,16,1024]{2,1,0:T(8,128)(2,1)} %bitcast.50), calls=%async_computation | async-start | bytes 4194304 | tf_op jit(solution)/shard_map/all_to_all | solution.py:315
  72.4 34.4 %all-to-all-start.1 = ((bf16[64,8,1024]{2,1,0:T(8,128)(2,1)}), bf16[64,8,1024]{2,1,0:T(8,128)(2,1)S(1)}, u32[]{:S(2)}, u32[]{:S(2)}) async-start(bf16[64,8,1024]{2,1,0:T(8,128)(2,1)} %bitcast.56), calls=%async_computation.1 | async-start | bytes 2097152 | tf_op jit(solution)/shard_map/all_to_all | solution.py:315
  82.7 32.2 %copy-start = (bf16[1,4,256,512]{3,2,1,0:T(8,128)(2,1)S(1)}, bf16[1,4,256,512]{3,2,1,0:T(8,128)(2,1)}, u32[]{:S(2)}) copy-start(bf16[1,4,256,512]{3,2,1,0:T(8,128)(2,1)} %param.16) | copy-start | bytes 3145732
  82.7 32.2 %copy-start.1 = (bf16[1,4,4,128,256]{4,3,2,1,0:T(8,128)(2,1)S(1)}, bf16[1,4,4,128,256]{4,3,2,1,0:T(8,128)(2,1)}, u32[]{:S(2)}) copy-start(bf16[1,4,4,128,256]{4,3,2,1,0:T(8,128)(2,1)} %param.17) | copy-start | bytes 3145732
  82.7 32.2 %copy-start.8 = (f32[1,1024]{1,0:T(1,128)S(1)}, f32[1,1024]{1,0:T(1,128)}, u32[]{:S(2)}) copy-start(f32[1,1024]{1,0:T(1,128)} %refs_2_.9) | copy-start | bytes 12292
  82.7 32.2 %copy-start.9 = (f32[1,1024]{1,0:T(1,128)S(1)}, f32[1,1024]{1,0:T(1,128)}, u32[]{:S(2)}) copy-start(f32[1,1024]{1,0:T(1,128)} %refs_3_.1) | copy-start | bytes 12292
  82.7 32.3 %copy-start.10 = (f32[1,1024]{1,0:T(1,128)S(1)}, f32[1,1024]{1,0:T(1,128)}, u32[]{:S(2)}) copy-start(f32[1,1024]{1,0:T(1,128)} %refs_4_.1) | copy-start | bytes 12292
  107.7 43.5 %all-to-all-start.2 = ((bf16[64,8,1024]{2,1,0:T(8,128)(2,1)}), bf16[64,8,1024]{2,1,0:T(8,128)(2,1)S(1)}, u32[]{:S(2)}, u32[]{:S(2)}) async-start(bf16[64,8,1024]{2,1,0:T(8,128)(2,1)} %bitcast.55), calls=%async_computation.2 | async-start | bytes 2097152 | tf_op jit(solution)/shard_map/all_to_all | solution.py:315
  114.9 3.6 %copy-start.5 = (bf16[64,8,1024]{2,1,0:T(8,128)(2,1)S(1)}, bf16[64,8,1024]{2,1,0:T(8,128)(2,1)}, u32[]{:S(2)}) copy-start(bf16[64,8,1024]{2,1,0:T(8,128)(2,1)} %copy-done.4) | copy-start | bytes 3145732
  121.3 14.8 %collective-permute-start.3 = (bf16[256,1024]{1,0:T(8,128)(2,1)}, bf16[256,1024]{1,0:T(8,128)(2,1)}, u32[]{:S(2)}, u32[]{:S(2)}) collective-permute-start(bf16[256,1024]{1,0:T(8,128)(2,1)} %channel_relay.2), channel_id=1, source_target_pairs={{0,64},{64,128},{128,192},{192,0},{1,65},{65,129},{129,193},{193,1... | collective-permute-start | bytes 1572872 | tf_op jit(solution)/shard_map/ppermute | solution.py:350
  122.7 24.6 %collective-permute-start.2 = (bf16[256,1024]{1,0:T(8,128)(2,1)}, bf16[256,1024]{1,0:T(8,128)(2,1)}, u32[]{:S(2)}, u32[]{:S(2)}) collective-permute-start(bf16[256,1024]{1,0:T(8,128)(2,1)} %channel_relay_first.2), channel_id=1, source_target_pairs={{0,64},{64,128},{128,192},{192,0},{1,65},{65,129},{129,193},{193,1... | collective-permute-start | bytes 1572872 | tf_op jit(solution)/shard_map/ppermute | solution.py:350
  151.2 12.4 %copy-start.2 = (bf16[64,8,1024]{2,1,0:T(8,128)(2,1)}, bf16[64,8,1024]{2,1,0:T(8,128)(2,1)S(1)}, u32[]{:S(2)}) copy-start(bf16[64,8,1024]{2,1,0:T(8,128)(2,1)S(1)} %all-to-all-done.2) | copy-start | bytes 3145732
  151.2 48.7 %all-to-all-start.4 = ((bf16[64,8,1024]{2,1,0:T(8,128)(2,1)}), bf16[64,8,1024]{2,1,0:T(8,128)(2,1)}, u32[]{:S(2)}, u32[]{:S(2)}) async-start(bf16[64,8,1024]{2,1,0:T(8,128)(2,1)} %bitcast.63), calls=%async_computation.4 | async-start | bytes 2097152 | tf_op jit(solution)/shard_map/all_to_all | solution.py:315
  167.1 1.2 copy-start.3
  168.3 2.7 copy-start.14
  171.1 40.6 %copy-start.12 = (bf16[1,4,256,256]{3,2,1,0:T(8,128)(2,1)S(1)}, bf16[1,4,256,256]{3,2,1,0:T(8,128)(2,1)}, u32[]{:S(2)}) copy-start(bf16[1,4,256,256]{3,2,1,0:T(8,128)(2,1)} %param.12) | copy-start | bytes 1572868
  171.1 14.2 %collective-permute-start.1 = (bf16[256,1024]{1,0:T(8,128)(2,1)S(1)}, bf16[256,1024]{1,0:T(8,128)(2,1)S(1)}, u32[]{:S(2)}, u32[]{:S(2)}) collective-permute-start(bf16[256,1024]{1,0:T(8,128)(2,1)S(1)} %copy-done.14), channel_id=1, source_target_pairs={{0,64},{64,128},{128,192},{192,0},{1,65},{65,129},{129,193},{193,1... | collective-permute-start | bytes 1572872 | tf_op jit(solution)/shard_map/ppermute | solution.py:350
  171.2 25.2 %collective-permute-start = (bf16[256,1024]{1,0:T(8,128)(2,1)}, bf16[256,1024]{1,0:T(8,128)(2,1)S(1)}, u32[]{:S(2)}, u32[]{:S(2)}) collective-permute-start(bf16[256,1024]{1,0:T(8,128)(2,1)} %channel_relay_first.3), channel_id=1, source_target_pairs={{0,64},{64,128},{128,192},{192,0},{1,65},{65,129},{129,193},{193,1... | collective-permute-start | bytes 1572872 | tf_op jit(solution)/shard_map/ppermute | solution.py:350
  200.0 40.1 %all-to-all-start.3 = ((bf16[64,8,1024]{2,1,0:T(8,128)(2,1)}), bf16[64,8,1024]{2,1,0:T(8,128)(2,1)}, u32[]{:S(2)}, u32[]{:S(2)}) async-start(bf16[64,8,1024]{2,1,0:T(8,128)(2,1)} %bitcast.64), calls=%async_computation.3 | async-start | bytes 2097152 | tf_op jit(solution)/shard_map/all_to_all | solution.py:315
  214.1 26.0 %copy-start.7 = (bf16[1024,512]{1,0:T(8,128)(2,1)S(1)}, bf16[1024,512]{1,0:T(8,128)(2,1)}, u32[]{:S(2)}) copy-start(bf16[1024,512]{1,0:T(8,128)(2,1)} %copy-done.6) | copy-start | bytes 3145732
  245.3 6.5 %copy-start.13 = (bf16[256,1024]{1,0:T(8,128)(2,1)S(1)}, bf16[256,1024]{1,0:T(8,128)(2,1)}, u32[]{:S(2)}) copy-start(bf16[256,1024]{1,0:T(8,128)(2,1)} %channel_relay_first.2) | copy-start | bytes 1572868
  245.3 6.5 %copy-start.15 = (bf16[256,1024]{1,0:T(8,128)(2,1)S(1)}, bf16[256,1024]{1,0:T(8,128)(2,1)}, u32[]{:S(2)}) copy-start(bf16[256,1024]{1,0:T(8,128)(2,1)} %channel_relay.3) | copy-start | bytes 1572868
  245.3 57.6 %all-to-all-start.5 = ((bf16[64,16,1024]{2,1,0:T(8,128)(2,1)}), bf16[64,16,1024]{2,1,0:T(8,128)(2,1)}, u32[]{:S(2)}, u32[]{:S(2)}) async-start(bf16[64,16,1024]{2,1,0:T(8,128)(2,1)} %bitcast.51), calls=%async_computation.5 | async-start | bytes 4194304 | tf_op jit(solution)/shard_map/all_to_all | solution.py:315
  (2 other events, 1.9 us)

commit v7 on v6

--- a/solution.py
+++ b/solution.py
@@ -63,7 +63,7 @@
     out_ref[...] = tiles.reshape(out_ref.shape)
 
 
-def mix_first(right, rows, chunk=512):
+def mix_first(right, rows, chunk=1024):
     count = rows.shape[0]
     out = pl.pallas_call(
         first_kernel,
@@ -172,7 +172,7 @@
     out_ref[...] = total.astype(out_ref.dtype)
 
 
-def mix_second(left, part, kind=BF16, held=(), chunk=256):
+def mix_second(left, part, kind=BF16, held=(), chunk=WIDTH):
     rows = left.shape[0]
     column = lambda count: pl.BlockSpec((count, chunk), lambda c: (0, c))
     return pl.pallas_call(
@@ -191,8 +191,8 @@
     return v + v * jnp.tanh(inner)
 
 
-def channel_rows(which, arrived, rows_refs, weight_refs):
-    slope_ref, shift_ref, gain_ref, up_ref, down_ref = weight_refs
+def gated_rows(which, arrived, rows_refs, weight_refs):
+    slope_ref, shift_ref, gain_ref, *_ = weight_refs
     width = arrived.shape[-1]
     mixed = []
     for place in which:
@@ -207,17 +207,24 @@
     gate = jnp.tanh(wide * (0.5 * slope_ref[...]) + 0.5 * shift_ref[...])
     residual = wide + mixed + mixed * gate
     scale = lax.rsqrt(jnp.mean(residual * residual, axis=-1, keepdims=True) + 1e-06)
-    normed = (residual * scale * (0.5 * gain_ref[...])).astype(BF16)
+    return residual, (residual * scale * (0.5 * gain_ref[...])).astype(BF16)
+
+
+def mlp_columns(residual, normed, weight_refs):
+    *_, up_ref, down_ref = weight_refs
     hidden = []
     for b in range(4):
         up = jnp.dot(normed[:, b * 256 : (b + 1) * 256], up_ref[b], preferred_element_type=F32)
         hidden.append(gelu_of_twice(up.astype(BF16)))
-    out = []
     for k in range(4):
         taken = jnp.concatenate([h[:, k * 128 : (k + 1) * 128] for h in hidden], axis=1)
         down = jnp.dot(taken, down_ref[k], preferred_element_type=F32)
-        out.append((residual[:, k * 256 : (k + 1) * 256] + down).astype(BF16))
-    return jnp.concatenate(out, axis=1)
+        yield (residual[:, k * 256 : (k + 1) * 256] + down).astype(BF16)
+
+
+def channel_rows(which, arrived, rows_refs, weight_refs):
+    residual, normed = gated_rows(which, arrived, rows_refs, weight_refs)
+    return jnp.concatenate(list(mlp_columns(residual, normed, weight_refs)), axis=1)
 
 
 def arrived_tiles(returned_ref, pairs):
@@ -249,36 +256,42 @@
 
 def relay_first_kernel(start, returned_ref, head_ref, rows_ref, *refs):
     *weight_refs, out_ref, rows_buf, out_buf, sems = refs
-    count = head_ref.shape[0]
+    held, count = head_ref.shape[0], rows_buf.shape[0]
     rest = pltpu.make_async_copy(
-        rows_ref.at[pl.ds(start + count, count), :], rows_buf, sems.at[0]
+        rows_ref.at[pl.ds(start + held, count), :], rows_buf, sems.at[0]
     )
     rest.start()
+    first = arrived_tiles(returned_ref.at[pl.ds(0, 2 * held), :], 1)
+    pieces = [gated_rows((0,), first, (head_ref,), weight_refs)]
+    rest.wait()
+    second = arrived_tiles(returned_ref.at[pl.ds(2 * held, 2 * count), :], 1)
+    pieces.append(gated_rows((0,), second, (rows_buf,), weight_refs))
+    residual, normed = (jnp.concatenate(piece) for piece in zip(*pieces))
     copies = []
-    for n, source_ref in enumerate((head_ref, rows_buf)):
-        if n:
-            rest.wait()
-        arrived = arrived_tiles(returned_ref.at[pl.ds(2 * n * count, 2 * count), :], 1)
-        part = pl.ds(n * count, count)
-        out_buf[part, :] = channel_rows((0,), arrived, (source_ref,), weight_refs)
-        copy = pltpu.make_async_copy(out_buf.at[part, :], out_ref.at[part, :], sems.at[1 + n])
-        copy.start()
-        copies.append(copy)
+    for k, out in enumerate(mlp_columns(residual, normed, weight_refs)):
+        part = pl.ds(k * 256, 256)
+        out_buf[:, part] = out
+        if k % 2:
+            part = pl.ds((k - 1) * 256, 512)
+            sem = sems.at[1 + k // 2]
+            copy = pltpu.make_async_copy(out_buf.at[:, part], out_ref.at[:, part], sem)
+            copy.start()
+            copies.append(copy)
     for copy in copies:
         copy.wait()
 
 
-def channel_relay_first(returned, rows, block, weights, earlier, count=128):
+def channel_relay_first(returned, rows, block, weights, earlier, held=192):
     start = block * BLOCK
-    held, *_ = lax.optimization_barrier((rows, *earlier))
-    head = in_vmem(held[start : start + count])
+    source, *_ = lax.optimization_barrier((rows, *earlier))
+    head = in_vmem(source[start : start + held])
     return pl.pallas_call(
         functools.partial(relay_first_kernel, start),
         in_specs=[WHOLE, WHOLE, pl.BlockSpec(memory_space=pl.ANY), *(WHOLE for _ in weights)],
         out_specs=pl.BlockSpec(memory_space=pl.ANY),
         out_shape=HBM((BLOCK, WIDTH), BF16),
         scratch_shapes=[
-            VMEM((count, WIDTH), BF16),
+            VMEM((BLOCK - held, WIDTH), BF16),
             VMEM((BLOCK, WIDTH), BF16),
             pltpu.SemaphoreType.DMA((3,)),
         ],
@@ -353,8 +366,8 @@
         arrivals.append(exchange(leaving))
     first_out = jnp.concatenate(firsts)
     left_in = [spread(by_output, half) for half in range(2)]
-    partial = mix_second(left_in[0], arrivals[0], F32)
-    mixed = mix_second(left_in[1], arrivals[1], BF16, (partial,))
+    partial = mix_second(left_in[0], arrivals[0], F32, (), 512)
+    mixed = mix_second(left_in[1], arrivals[1], BF16, (partial,), 512)
     final = exchange(mixed)
     second_out = channel_last(final, currents, weights)
     return first_out[None], second_out.reshape(1, 1024, WIDTH)

time: 311 us -> 308 us (level)
  Pallas kernels: 49.4 us -> 44.5 us
    pallas_call x4, Pallas kernels: 16 us -> 12.7 us  [mix_second(): pl.pallas_call(second_kernel, grid=(WIDTH // chunk,), in_specs=[pl.BlockS...]
  transfers between devices with their start and end apart: 10 -> 10, of which waited for: 8 -> 8; matrix products, arithmetic and copies ran while one was open for 3% -> 3% of each run, Pallas kernels for 10% -> 9%
where the time goes in v7:
time: 308 us; the launch traced here: 307 us
  waiting for transfers between devices  192 us (62%)
  starting transfers between devices  57.6 us (19%)
  Pallas kernels  44.5 us (14%)
  local copies, waits for them, and re-layouts  8.64 us (3%)
    all_to_all x6, waiting for transfers between devices, exchange(): lax.all_to_all(grouped, 'seq', split_axis=0, concat_axis=0, tiled=True)  144 us
    all_to_all x6, starting transfers between devices, exchange(): lax.all_to_all(grouped, 'seq', split_axis=0, concat_axis=0, tiled=True)  54.6 us
    ppermute x4, waiting for transfers between devices, shards(): received.append(lax.ppermute(out, 'pipe', route))  48.4 us
    pallas_call x4, Pallas kernels, mix_second(): pl.pallas_call(second_kernel, grid=(WIDTH // chunk,), in_specs=[pl.BlockS...  12.7 us
    pallas_call x2, Pallas kernels, mix_first_relayed(): pl.pallas_call(functools.partial(relayed_kernel, half, chunk), grid=(WIDT...  7.46 us
    pallas_call x1, Pallas kernels, channel_last(): pl.pallas_call(last_kernel, grid=(BLOCK // count,), in_specs=[pl.BlockSpe...  7.14 us
    pallas_call x2, Pallas kernels, channel_relay(): pl.pallas_call(functools.partial(relay_kernel, block % 2), grid=(steps,),...  7.11 us
  transfers between devices with their start and end apart: 10, of which 8 were waited for; matrix products, arithmetic and copies ran while one was open for 3% of the time, Pallas kernels for 9%

profile of v7, /device:TPU:1, one launch (start us, length us, event | category | flops | bytes accessed | tf_op | source)
XLA Modules:
  0.0 307.0 jit_solution(5147949646793241760)
XLA Ops:
  0.6 3.3 %mix_first.1 = bf16[64,2,8,1024]{3,2,1,0:T(8,128)(2,1)} custom-call(bf16[4,256,256]{2,1,0:T(8,128)(2,1)} %bitcast.52, bf16[1024,1024]{1,0:T(8,128)(2,1)} %bitcast.43), custom_call_target="tpu_custom_call" | custom-call | tf_op jit(solution)/shard_map/mix_first/pallas_call | solution.py:68
  3.9 13.1 %all-to-all-start = ((bf16[64,16,1024]{2,1,0:T(8,128)(2,1)}), bf16[64,16,1024]{2,1,0:T(8,128)(2,1)S(1)}, u32[]{:S(2)}, u32[]{:S(2)}) async-start(bf16[64,16,1024]{2,1,0:T(8,128)(2,1)} %bitcast.50), calls=%async_computation | async-start | bytes 4194304 | tf_op jit(solution)/shard_map/all_to_all | solution.py:328
  19.3 48.9 %all-to-all-done = bf16[64,16,1024]{2,1,0:T(8,128)(2,1)S(1)} async-done(((bf16[64,16,1024]{2,1,0:T(8,128)(2,1)}), bf16[64,16,1024]{2,1,0:T(8,128)(2,1)S(1)}, u32[]{:S(2)}, u32[]{:S(2)}) %all-to-all-start) | async-done | bytes 2097184 | tf_op jit(solution)/shard_map/all_to_all | solution.py:328
  70.5 5.8 %all-to-all-start.1 = ((bf16[64,8,1024]{2,1,0:T(8,128)(2,1)}), bf16[64,8,1024]{2,1,0:T(8,128)(2,1)S(1)}, u32[]{:S(2)}, u32[]{:S(2)}) async-start(bf16[64,8,1024]{2,1,0:T(8,128)(2,1)} %bitcast.56), calls=%async_computation.1 | async-start | bytes 2097152 | tf_op jit(solution)/shard_map/all_to_all | solution.py:328
  80.0 24.8 %all-to-all-done.1 = bf16[64,8,1024]{2,1,0:T(8,128)(2,1)S(1)} async-done(((bf16[64,8,1024]{2,1,0:T(8,128)(2,1)}), bf16[64,8,1024]{2,1,0:T(8,128)(2,1)S(1)}, u32[]{:S(2)}, u32[]{:S(2)}) %all-to-all-start.1) | async-done | bytes 1048608 | tf_op jit(solution)/shard_map/all_to_all | solution.py:328
  105.8 6.2 %all-to-all-start.2 = ((bf16[64,8,1024]{2,1,0:T(8,128)(2,1)}), bf16[64,8,1024]{2,1,0:T(8,128)(2,1)S(1)}, u32[]{:S(2)}, u32[]{:S(2)}) async-start(bf16[64,8,1024]{2,1,0:T(8,128)(2,1)} %bitcast.55), calls=%async_computation.2 | async-start | bytes 2097152 | tf_op jit(solution)/shard_map/all_to_all | solution.py:328
  113.1 3.6 %channel_relay.2 = bf16[256,1024]{1,0:T(8,128)(2,1)} custom-call(bf16[512,1024]{1,0:T(8,128)(2,1)} %bitcast.41, bf16[1024,1024]{1,0:T(8,128)(2,1)} %bitcast.45, f32[1,1024]{1,0:T(1,128)S(1)} %copy-done.8, f32[1,1024]{1,0:T(1,128)S(1)} %copy-done.9, f32[1,1024]{1,0:T(1,128)S(1)} %copy-done.10, bf16[4,256,512]{2,1,0:T(8,128)(2,1)S(1)} %bitcast.27, ...), custom_call_target="tpu_custom_call" | custom-call | tf_op jit(solution)/shard_map/channel_relay/pallas_call | solution.py:243
  121.9 12.1 %collective-permute-done.3.refs_1_ = bf16[256,1024]{1,0:T(8,128)(2,1)} collective-permute-done((bf16[256,1024]{1,0:T(8,128)(2,1)}, bf16[256,1024]{1,0:T(8,128)(2,1)}, u32[]{:S(2)}, u32[]{:S(2)}) %collective-permute-start.3) | collective-permute-done | bytes 524320 | tf_op jit(solution)/shard_map/ppermute | solution.py:363
  134.0 11.2 %collective-permute-done.2.refs_0_ = bf16[256,1024]{1,0:T(8,128)(2,1)} collective-permute-done((bf16[256,1024]{1,0:T(8,128)(2,1)}, bf16[256,1024]{1,0:T(8,128)(2,1)}, u32[]{:S(2)}, u32[]{:S(2)}) %collective-permute-start.2) | collective-permute-done | bytes 524320 | tf_op jit(solution)/shard_map/ppermute | solution.py:363
  145.2 3.9 %mix_first_relayed.3 = (bf16[512,1024]{1,0:T(8,128)(2,1)}, bf16[512,1024]{1,0:T(8,128)(2,1)}) custom-call(s32[1]{0:T(128)} %bitcast.14.section_ref, bf16[4,256,256]{2,1,0:T(8,128)(2,1)} %bitcast.53, bf16[1024,1024]{1,0:T(8,128)(2,1)} %fresh_ref.3, bf16[256,1024]{1,0:T(8,128)(2,1)} %collective-permute-done.2.refs_0_, ...), custom_call_target="tpu_custom_call" | custom-call | tf_op jit(solution)/shard_map/mix_first_relayed/pallas_call | solution.py:113
  149.1 11.4 %all-to-all-start.4 = ((bf16[64,8,1024]{2,1,0:T(8,128)(2,1)}), bf16[64,8,1024]{2,1,0:T(8,128)(2,1)}, u32[]{:S(2)}, u32[]{:S(2)}) async-start(bf16[64,8,1024]{2,1,0:T(8,128)(2,1)} %bitcast.63), calls=%async_computation.4 | async-start | bytes 2097152 | tf_op jit(solution)/shard_map/all_to_all | solution.py:328
  161.6 3.5 %channel_relay.3 = bf16[256,1024]{1,0:T(8,128)(2,1)} custom-call(bf16[512,1024]{1,0:T(8,128)(2,1)} %bitcast.39, bf16[1024,1024]{1,0:T(8,128)(2,1)} %bitcast.48, f32[1,1024]{1,0:T(1,128)S(1)} %copy-done.8, f32[1,1024]{1,0:T(1,128)S(1)} %copy-done.9, f32[1,1024]{1,0:T(1,128)S(1)} %copy-done.10, bf16[4,256,512]{2,1,0:T(8,128)(2,1)S(1)} %bitcast.29, ...), custom_call_target="tpu_custom_call" | custom-call | tf_op jit(solution)/shard_map/channel_relay/pallas_call | solution.py:243
  166.3 2.6 channel_relay_first.3
  169.3 14.0 %collective-permute-done.1.refs_1_ = bf16[256,1024]{1,0:T(8,128)(2,1)S(1)} collective-permute-done((bf16[256,1024]{1,0:T(8,128)(2,1)S(1)}, bf16[256,1024]{1,0:T(8,128)(2,1)S(1)}, u32[]{:S(2)}, u32[]{:S(2)}) %collective-permute-start.1) | collective-permute-done | bytes 524320 | tf_op jit(solution)/shard_map/ppermute | solution.py:363
  183.2 11.1 %collective-permute-done.refs_0_ = bf16[256,1024]{1,0:T(8,128)(2,1)S(1)} collective-permute-done((bf16[256,1024]{1,0:T(8,128)(2,1)}, bf16[256,1024]{1,0:T(8,128)(2,1)S(1)}, u32[]{:S(2)}, u32[]{:S(2)}) %collective-permute-start) | collective-permute-done | bytes 524320 | tf_op jit(solution)/shard_map/ppermute | solution.py:363
  194.4 3.6 %mix_first_relayed.2 = (bf16[512,1024]{1,0:T(8,128)(2,1)}, bf16[512,1024]{1,0:T(8,128)(2,1)}) custom-call(s32[1]{0:T(128)} %bitcast.14.section_ref, bf16[4,256,256]{2,1,0:T(8,128)(2,1)} %bitcast.54, bf16[1024,1024]{1,0:T(8,128)(2,1)} %fresh_ref.3, bf16[256,1024]{1,0:T(8,128)(2,1)S(1)} %collective-permute-done.refs_0_, ...), custom_call_target="tpu_custom_call" | custom-call | tf_op jit(solution)/shard_map/mix_first_relayed/pallas_call | solution.py:113
  198.0 11.5 %all-to-all-start.3 = ((bf16[64,8,1024]{2,1,0:T(8,128)(2,1)}), bf16[64,8,1024]{2,1,0:T(8,128)(2,1)}, u32[]{:S(2)}, u32[]{:S(2)}) async-start(bf16[64,8,1024]{2,1,0:T(8,128)(2,1)} %bitcast.64), calls=%async_computation.3 | async-start | bytes 2097152 | tf_op jit(solution)/shard_map/all_to_all | solution.py:328
  211.9 3.9 %mix_second.6.refs_0_ = f32[1024,1024]{1,0:T(8,128)} custom-call(bf16[1024,512]{1,0:T(8,128)(2,1)S(1)} %spread.7.left_ref, bf16[512,1024]{1,0:T(8,128)(2,1)} %bitcast.18.part_ref), custom_call_target="tpu_custom_call" | custom-call | tf_op jit(solution)/shard_map/mix_second/pallas_call | solution.py:178
  215.9 22.1 %all-to-all-done.3 = bf16[64,8,1024]{2,1,0:T(8,128)(2,1)} async-done(((bf16[64,8,1024]{2,1,0:T(8,128)(2,1)}), bf16[64,8,1024]{2,1,0:T(8,128)(2,1)}, u32[]{:S(2)}, u32[]{:S(2)}) %all-to-all-start.3) | async-done | bytes 1048608 | tf_op jit(solution)/shard_map/all_to_all | solution.py:328
  238.0 4.3 %mix_second.7 = bf16[1024,1024]{1,0:T(8,128)(2,1)} custom-call(bf16[1024,512]{1,0:T(8,128)(2,1)S(1)} %copy-done.7, bf16[512,1024]{1,0:T(8,128)(2,1)} %bitcast.16.part_ref, f32[1024,1024]{1,0:T(8,128)} %mix_second.6.refs_0_), custom_call_target="tpu_custom_call" | custom-call | tf_op jit(solution)/shard_map/mix_second/pallas_call | solution.py:178
  242.2 6.5 %all-to-all-start.5 = ((bf16[64,16,1024]{2,1,0:T(8,128)(2,1)}), bf16[64,16,1024]{2,1,0:T(8,128)(2,1)}, u32[]{:S(2)}, u32[]{:S(2)}) async-start(bf16[64,16,1024]{2,1,0:T(8,128)(2,1)} %bitcast.51), calls=%async_computation.5 | async-start | bytes 4194304 | tf_op jit(solution)/shard_map/all_to_all | solution.py:328
  248.8 2.9 maximum_bitcast_fusion
  251.6 48.2 %all-to-all-done.5 = bf16[64,16,1024]{2,1,0:T(8,128)(2,1)} async-done(((bf16[64,16,1024]{2,1,0:T(8,128)(2,1)}), bf16[64,16,1024]{2,1,0:T(8,128)(2,1)}, u32[]{:S(2)}, u32[]{:S(2)}) %all-to-all-start.5) | async-done | bytes 2097184 | tf_op jit(solution)/shard_map/all_to_all | solution.py:328
  299.9 7.1 %channel_last.1 = bf16[4,256,1024]{2,1,0:T(8,128)(2,1)} custom-call(bf16[1024,1024]{1,0:T(8,128)(2,1)} %bitcast.20.returned_ref, bf16[2,256,1024]{2,1,0:T(8,128)(2,1)} %bitcast.61, bf16[2,256,1024]{2,1,0:T(8,128)(2,1)} %bitcast.62, f32[1,1024]{1,0:T(1,128)S(1)} %copy-done.8, f32[1,1024]{1,0:T(1,128)S(1)} %copy-done.9, f32[1,1024]{1,0:T(1,128)S(1)} %copy-done.10, ...), custom_call_target="tpu_custom_call" | custom-call | tf_op jit(solution)/shard_map/channel_last/pallas_call | solution.py:312
  (54 shorter events, 20.4 us)
Async XLA Ops:
  3.9 13.1 %copy-start.11 = (bf16[1,4,256,256]{3,2,1,0:T(8,128)(2,1)S(1)}, bf16[1,4,256,256]{3,2,1,0:T(8,128)(2,1)}, u32[]{:S(2)}) copy-start(bf16[1,4,256,256]{3,2,1,0:T(8,128)(2,1)} %param.12) | copy-start | bytes 1572868
  3.9 64.3 %all-to-all-start = ((bf16[64,16,1024]{2,1,0:T(8,128)(2,1)}), bf16[64,16,1024]{2,1,0:T(8,128)(2,1)S(1)}, u32[]{:S(2)}, u32[]{:S(2)}) async-start(bf16[64,16,1024]{2,1,0:T(8,128)(2,1)} %bitcast.50), calls=%async_computation | async-start | bytes 4194304 | tf_op jit(solution)/shard_map/all_to_all | solution.py:328
  70.5 34.4 %all-to-all-start.1 = ((bf16[64,8,1024]{2,1,0:T(8,128)(2,1)}), bf16[64,8,1024]{2,1,0:T(8,128)(2,1)S(1)}, u32[]{:S(2)}, u32[]{:S(2)}) async-start(bf16[64,8,1024]{2,1,0:T(8,128)(2,1)} %bitcast.56), calls=%async_computation.1 | async-start | bytes 2097152 | tf_op jit(solution)/shard_map/all_to_all | solution.py:328
  80.0 33.0 %copy-start = (bf16[1,4,256,512]{3,2,1,0:T(8,128)(2,1)S(1)}, bf16[1,4,256,512]{3,2,1,0:T(8,128)(2,1)}, u32[]{:S(2)}) copy-start(bf16[1,4,256,512]{3,2,1,0:T(8,128)(2,1)} %param.16) | copy-start | bytes 3145732
  80.0 33.0 %copy-start.1 = (bf16[1,4,4,128,256]{4,3,2,1,0:T(8,128)(2,1)S(1)}, bf16[1,4,4,128,256]{4,3,2,1,0:T(8,128)(2,1)}, u32[]{:S(2)}) copy-start(bf16[1,4,4,128,256]{4,3,2,1,0:T(8,128)(2,1)} %param.17) | copy-start | bytes 3145732
  80.0 33.0 %copy-start.8 = (f32[1,1024]{1,0:T(1,128)S(1)}, f32[1,1024]{1,0:T(1,128)}, u32[]{:S(2)}) copy-start(f32[1,1024]{1,0:T(1,128)} %refs_2_.9) | copy-start | bytes 12292
  80.0 33.0 %copy-start.9 = (f32[1,1024]{1,0:T(1,128)S(1)}, f32[1,1024]{1,0:T(1,128)}, u32[]{:S(2)}) copy-start(f32[1,1024]{1,0:T(1,128)} %refs_3_.1) | copy-start | bytes 12292
  80.0 33.0 %copy-start.10 = (f32[1,1024]{1,0:T(1,128)S(1)}, f32[1,1024]{1,0:T(1,128)}, u32[]{:S(2)}) copy-start(f32[1,1024]{1,0:T(1,128)} %refs_4_.1) | copy-start | bytes 12292
  105.8 43.3 %all-to-all-start.2 = ((bf16[64,8,1024]{2,1,0:T(8,128)(2,1)}), bf16[64,8,1024]{2,1,0:T(8,128)(2,1)S(1)}, u32[]{:S(2)}, u32[]{:S(2)}) async-start(bf16[64,8,1024]{2,1,0:T(8,128)(2,1)} %bitcast.55), calls=%async_computation.2 | async-start | bytes 2097152 | tf_op jit(solution)/shard_map/all_to_all | solution.py:328
  113.1 3.6 %copy-start.5 = (bf16[64,8,1024]{2,1,0:T(8,128)(2,1)S(1)}, bf16[64,8,1024]{2,1,0:T(8,128)(2,1)}, u32[]{:S(2)}) copy-start(bf16[64,8,1024]{2,1,0:T(8,128)(2,1)} %copy-done.4) | copy-start | bytes 3145732
  119.2 14.7 %collective-permute-start.3 = (bf16[256,1024]{1,0:T(8,128)(2,1)}, bf16[256,1024]{1,0:T(8,128)(2,1)}, u32[]{:S(2)}, u32[]{:S(2)}) collective-permute-start(bf16[256,1024]{1,0:T(8,128)(2,1)} %channel_relay.2), channel_id=1, source_target_pairs={{0,64},{64,128},{128,192},{192,0},{1,65},{65,129},{129,193},{193,1... | collective-permute-start | bytes 1572872 | tf_op jit(solution)/shard_map/ppermute | solution.py:363
  120.6 24.6 %collective-permute-start.2 = (bf16[256,1024]{1,0:T(8,128)(2,1)}, bf16[256,1024]{1,0:T(8,128)(2,1)}, u32[]{:S(2)}, u32[]{:S(2)}) collective-permute-start(bf16[256,1024]{1,0:T(8,128)(2,1)} %channel_relay_first.2), channel_id=1, source_target_pairs={{0,64},{64,128},{128,192},{192,0},{1,65},{65,129},{129,193},{193,1... | collective-permute-start | bytes 1572872 | tf_op jit(solution)/shard_map/ppermute | solution.py:363
  149.1 12.4 %copy-start.2 = (bf16[64,8,1024]{2,1,0:T(8,128)(2,1)}, bf16[64,8,1024]{2,1,0:T(8,128)(2,1)S(1)}, u32[]{:S(2)}) copy-start(bf16[64,8,1024]{2,1,0:T(8,128)(2,1)S(1)} %all-to-all-done.2) | copy-start | bytes 3145732
  149.1 48.8 %all-to-all-start.4 = ((bf16[64,8,1024]{2,1,0:T(8,128)(2,1)}), bf16[64,8,1024]{2,1,0:T(8,128)(2,1)}, u32[]{:S(2)}, u32[]{:S(2)}) async-start(bf16[64,8,1024]{2,1,0:T(8,128)(2,1)} %bitcast.63), calls=%async_computation.4 | async-start | bytes 2097152 | tf_op jit(solution)/shard_map/all_to_all | solution.py:328
  165.1 1.2 copy-start.3
  166.3 2.6 copy-start.13
  168.9 40.6 %copy-start.12 = (bf16[1,4,256,256]{3,2,1,0:T(8,128)(2,1)S(1)}, bf16[1,4,256,256]{3,2,1,0:T(8,128)(2,1)}, u32[]{:S(2)}) copy-start(bf16[1,4,256,256]{3,2,1,0:T(8,128)(2,1)} %param.12) | copy-start | bytes 1572868
  168.9 14.3 %collective-permute-start.1 = (bf16[256,1024]{1,0:T(8,128)(2,1)S(1)}, bf16[256,1024]{1,0:T(8,128)(2,1)S(1)}, u32[]{:S(2)}, u32[]{:S(2)}) collective-permute-start(bf16[256,1024]{1,0:T(8,128)(2,1)S(1)} %copy-done.13), channel_id=1, source_target_pairs={{0,64},{64,128},{128,192},{192,0},{1,65},{65,129},{129,193},{193,1... | collective-permute-start | bytes 1572872 | tf_op jit(solution)/shard_map/ppermute | solution.py:363
  169.0 25.4 %collective-permute-start = (bf16[256,1024]{1,0:T(8,128)(2,1)}, bf16[256,1024]{1,0:T(8,128)(2,1)S(1)}, u32[]{:S(2)}, u32[]{:S(2)}) collective-permute-start(bf16[256,1024]{1,0:T(8,128)(2,1)} %channel_relay_first.3), channel_id=1, source_target_pairs={{0,64},{64,128},{128,192},{192,0},{1,65},{65,129},{129,193},{193,1... | collective-permute-start | bytes 1572872 | tf_op jit(solution)/shard_map/ppermute | solution.py:363
  198.0 40.0 %all-to-all-start.3 = ((bf16[64,8,1024]{2,1,0:T(8,128)(2,1)}), bf16[64,8,1024]{2,1,0:T(8,128)(2,1)}, u32[]{:S(2)}, u32[]{:S(2)}) async-start(bf16[64,8,1024]{2,1,0:T(8,128)(2,1)} %bitcast.64), calls=%async_computation.3 | async-start | bytes 2097152 | tf_op jit(solution)/shard_map/all_to_all | solution.py:328
  211.9 26.0 %copy-start.7 = (bf16[1024,512]{1,0:T(8,128)(2,1)S(1)}, bf16[1024,512]{1,0:T(8,128)(2,1)}, u32[]{:S(2)}) copy-start(bf16[1024,512]{1,0:T(8,128)(2,1)} %copy-done.6) | copy-start | bytes 3145732
  242.2 6.5 %copy-start.14 = (bf16[256,1024]{1,0:T(8,128)(2,1)S(1)}, bf16[256,1024]{1,0:T(8,128)(2,1)}, u32[]{:S(2)}) copy-start(bf16[256,1024]{1,0:T(8,128)(2,1)} %channel_relay.3) | copy-start | bytes 1572868
  242.2 6.5 %copy-start.15 = (bf16[256,1024]{1,0:T(8,128)(2,1)S(1)}, bf16[256,1024]{1,0:T(8,128)(2,1)}, u32[]{:S(2)}) copy-start(bf16[256,1024]{1,0:T(8,128)(2,1)} %channel_relay_first.2) | copy-start | bytes 1572868
  242.2 57.6 %all-to-all-start.5 = ((bf16[64,16,1024]{2,1,0:T(8,128)(2,1)}), bf16[64,16,1024]{2,1,0:T(8,128)(2,1)}, u32[]{:S(2)}, u32[]{:S(2)}) async-start(bf16[64,16,1024]{2,1,0:T(8,128)(2,1)} %bitcast.51), calls=%async_computation.5 | async-start | bytes 4194304 | tf_op jit(solution)/shard_map/all_to_all | solution.py:328
  (2 other events, 1.9 us)

commit v8 on v7

--- a/solution.py
+++ b/solution.py
@@ -299,28 +299,64 @@
     )(in_vmem(returned), head, in_hbm(rows), *weights)
 
 
-def last_kernel(returned_ref, *refs):
-    *rest, out_ref = refs
-    rows_refs, weight_refs = rest[:2], rest[2:]
-    arrived = arrived_tiles(returned_ref, 2)
-    out = channel_rows((0, 1, 2, 3), arrived, rows_refs, weight_refs)
-    out_ref[...] = out.reshape(out_ref.shape)
-
-
-def channel_last(returned, parts, weights, count=64):
-    pair = pl.BlockSpec((2, count, WIDTH), lambda s: (0, s, 0))
-    return pl.pallas_call(
-        last_kernel,
-        grid=(BLOCK // count,),
-        in_specs=[
-            pl.BlockSpec((4 * count, WIDTH), lambda s: (s, 0)),
-            *(pair for _ in parts),
-            *(WHOLE for _ in weights),
-        ],
-        out_specs=pl.BlockSpec((4, count, WIDTH), lambda s: (0, s, 0)),
+def last_kernel(counts, returned_ref, *refs):
+    parts_refs, weight_refs, out_ref = refs[:2], refs[2:7], refs[7]
+    returned_buf, rows_buf, out_buf, sems, out_sems = refs[8:]
+    starts = [sum(counts[:n]) for n in range(len(counts))]
+    arriving = []
+    for n, (start, count) in enumerate(zip(starts, counts)):
+        taken = pl.ds(4 * start, 4 * count)
+        copies = [
+            pltpu.make_async_copy(
+                returned_ref.at[taken, :], returned_buf.at[taken, :], sems.at[n, 0]
+            )
+        ]
+        for half, part_ref in enumerate(parts_refs):
+            place = pl.ds(start, count)
+            copies.append(
+                pltpu.make_async_copy(
+                    part_ref.at[:, place, :],
+                    rows_buf.at[pl.ds(2 * half, 2), place, :],
+                    sems.at[n, 1 + half],
+                )
+            )
+        for copy in copies:
+            copy.start()
+        arriving.append(copies)
+    leaving = []
+    for n, (start, count) in enumerate(zip(starts, counts)):
+        for copy in arriving[n]:
+            copy.wait()
+        place = pl.ds(start, count)
+        arrived = arrived_tiles(returned_buf.at[pl.ds(4 * start, 4 * count), :], 2)
+        rows_refs = (rows_buf.at[:, place, :],)
+        out = channel_rows((0, 1, 2, 3), arrived, rows_refs, weight_refs)
+        out_buf[:, place, :] = out.reshape(4, count, WIDTH)
+        copy = pltpu.make_async_copy(
+            out_buf.at[:, place, :], out_ref.at[:, place, :], out_sems.at[n]
+        )
+        copy.start()
+        leaving.append(copy)
+    for copy in leaving:
+        copy.wait()
+
+
+def channel_last(returned, parts, weights, counts=(64, 128, 64)):
+    anywhere = pl.BlockSpec(memory_space=pl.ANY)
+    return pl.pallas_call(
+        functools.partial(last_kernel, counts),
+        in_specs=[anywhere, *(anywhere for _ in parts), *(WHOLE for _ in weights)],
+        out_specs=anywhere,
         out_shape=HBM((4, BLOCK, WIDTH), BF16),
+        scratch_shapes=[
+            VMEM((4 * BLOCK, WIDTH), BF16),
+            VMEM((4, BLOCK, WIDTH), BF16),
+            VMEM((4, BLOCK, WIDTH), BF16),
+            pltpu.SemaphoreType.DMA((len(counts), 3)),
+            pltpu.SemaphoreType.DMA((len(counts),)),
+        ],
         **params("channel_last"),
-    )(in_hbm(returned), *(in_hbm(p) for p in parts), *weights)
+    )(in_hbm(returned), *(in_hbm(part) for part in parts), *weights)
 
 
 def exchange(rows):

time: 308 us -> 308 us (level)
  no operation moved by 1% of the time
where the time goes in v8:
time: 308 us; the launch traced here: 307 us
  waiting for transfers between devices  192 us (62%)
  starting transfers between devices  57.6 us (19%)
  Pallas kernels  44 us (14%)
  local copies, waits for them, and re-layouts  8.64 us (3%)
    all_to_all x6, waiting for transfers between devices, exchange(): lax.all_to_all(grouped, 'seq', split_axis=0, concat_axis=0, tiled=True)  144 us
    all_to_all x6, starting transfers between devices, exchange(): lax.all_to_all(grouped, 'seq', split_axis=0, concat_axis=0, tiled=True)  54.6 us
    ppermute x4, waiting for transfers between devices, shards(): received.append(lax.ppermute(out, 'pipe', route))  48.4 us
    pallas_call x4, Pallas kernels, mix_second(): pl.pallas_call(second_kernel, grid=(WIDTH // chunk,), in_specs=[pl.BlockS...  12.7 us
    pallas_call x2, Pallas kernels, mix_first_relayed(): pl.pallas_call(functools.partial(relayed_kernel, half, chunk), grid=(WIDT...  7.46 us
    pallas_call x2, Pallas kernels, channel_relay(): pl.pallas_call(functools.partial(relay_kernel, block % 2), grid=(steps,),...  7.11 us
    pallas_call x1, Pallas kernels, channel_last(): pl.pallas_call(functools.partial(last_kernel, counts), in_specs=[anywhere...  6.61 us
  transfers between devices with their start and end apart: 10, of which 8 were waited for; matrix products, arithmetic and copies ran while one was open for 3% of the time, Pallas kernels for 9%

profile of v8, /device:TPU:1, one launch (start us, length us, event | category | flops | bytes accessed | tf_op | source)
XLA Modules:
  0.0 306.6 jit_solution(17899569245341186537)
XLA Ops:
  0.6 3.3 %mix_first.1 = bf16[64,2,8,1024]{3,2,1,0:T(8,128)(2,1)} custom-call(bf16[4,256,256]{2,1,0:T(8,128)(2,1)} %bitcast.52, bf16[1024,1024]{1,0:T(8,128)(2,1)} %bitcast.43), custom_call_target="tpu_custom_call" | custom-call | tf_op jit(solution)/shard_map/mix_first/pallas_call | solution.py:68
  3.9 13.1 %all-to-all-start = ((bf16[64,16,1024]{2,1,0:T(8,128)(2,1)}), bf16[64,16,1024]{2,1,0:T(8,128)(2,1)S(1)}, u32[]{:S(2)}, u32[]{:S(2)}) async-start(bf16[64,16,1024]{2,1,0:T(8,128)(2,1)} %bitcast.50), calls=%async_computation | async-start | bytes 4194304 | tf_op jit(solution)/shard_map/all_to_all | solution.py:364
  19.3 48.9 %all-to-all-done = bf16[64,16,1024]{2,1,0:T(8,128)(2,1)S(1)} async-done(((bf16[64,16,1024]{2,1,0:T(8,128)(2,1)}), bf16[64,16,1024]{2,1,0:T(8,128)(2,1)S(1)}, u32[]{:S(2)}, u32[]{:S(2)}) %all-to-all-start) | async-done | bytes 2097184 | tf_op jit(solution)/shard_map/all_to_all | solution.py:364
  70.5 5.8 %all-to-all-start.1 = ((bf16[64,8,1024]{2,1,0:T(8,128)(2,1)}), bf16[64,8,1024]{2,1,0:T(8,128)(2,1)S(1)}, u32[]{:S(2)}, u32[]{:S(2)}) async-start(bf16[64,8,1024]{2,1,0:T(8,128)(2,1)} %bitcast.56), calls=%async_computation.1 | async-start | bytes 2097152 | tf_op jit(solution)/shard_map/all_to_all | solution.py:364
  80.0 24.8 %all-to-all-done.1 = bf16[64,8,1024]{2,1,0:T(8,128)(2,1)S(1)} async-done(((bf16[64,8,1024]{2,1,0:T(8,128)(2,1)}), bf16[64,8,1024]{2,1,0:T(8,128)(2,1)S(1)}, u32[]{:S(2)}, u32[]{:S(2)}) %all-to-all-start.1) | async-done | bytes 1048608 | tf_op jit(solution)/shard_map/all_to_all | solution.py:364
  105.8 6.2 %all-to-all-start.2 = ((bf16[64,8,1024]{2,1,0:T(8,128)(2,1)}), bf16[64,8,1024]{2,1,0:T(8,128)(2,1)S(1)}, u32[]{:S(2)}, u32[]{:S(2)}) async-start(bf16[64,8,1024]{2,1,0:T(8,128)(2,1)} %bitcast.55), calls=%async_computation.2 | async-start | bytes 2097152 | tf_op jit(solution)/shard_map/all_to_all | solution.py:364
  113.1 3.6 %channel_relay.2 = bf16[256,1024]{1,0:T(8,128)(2,1)} custom-call(bf16[512,1024]{1,0:T(8,128)(2,1)} %bitcast.41, bf16[1024,1024]{1,0:T(8,128)(2,1)} %bitcast.45, f32[1,1024]{1,0:T(1,128)S(1)} %copy-done.8, f32[1,1024]{1,0:T(1,128)S(1)} %copy-done.9, f32[1,1024]{1,0:T(1,128)S(1)} %copy-done.10, bf16[4,256,512]{2,1,0:T(8,128)(2,1)S(1)} %bitcast.27, ...), custom_call_target="tpu_custom_call" | custom-call | tf_op jit(solution)/shard_map/channel_relay/pallas_call | solution.py:243
  121.9 12.1 %collective-permute-done.3.refs_1_ = bf16[256,1024]{1,0:T(8,128)(2,1)} collective-permute-done((bf16[256,1024]{1,0:T(8,128)(2,1)}, bf16[256,1024]{1,0:T(8,128)(2,1)}, u32[]{:S(2)}, u32[]{:S(2)}) %collective-permute-start.3) | collective-permute-done | bytes 524320 | tf_op jit(solution)/shard_map/ppermute | solution.py:399
  134.0 11.2 %collective-permute-done.2.refs_0_ = bf16[256,1024]{1,0:T(8,128)(2,1)} collective-permute-done((bf16[256,1024]{1,0:T(8,128)(2,1)}, bf16[256,1024]{1,0:T(8,128)(2,1)}, u32[]{:S(2)}, u32[]{:S(2)}) %collective-permute-start.2) | collective-permute-done | bytes 524320 | tf_op jit(solution)/shard_map/ppermute | solution.py:399
  145.2 3.9 %mix_first_relayed.3 = (bf16[512,1024]{1,0:T(8,128)(2,1)}, bf16[512,1024]{1,0:T(8,128)(2,1)}) custom-call(s32[1]{0:T(128)} %bitcast.14.section_ref, bf16[4,256,256]{2,1,0:T(8,128)(2,1)} %bitcast.53, bf16[1024,1024]{1,0:T(8,128)(2,1)} %fresh_ref.3, bf16[256,1024]{1,0:T(8,128)(2,1)} %collective-permute-done.2.refs_0_, ...), custom_call_target="tpu_custom_call" | custom-call | tf_op jit(solution)/shard_map/mix_first_relayed/pallas_call | solution.py:113
  149.1 11.4 %all-to-all-start.4 = ((bf16[64,8,1024]{2,1,0:T(8,128)(2,1)}), bf16[64,8,1024]{2,1,0:T(8,128)(2,1)}, u32[]{:S(2)}, u32[]{:S(2)}) async-start(bf16[64,8,1024]{2,1,0:T(8,128)(2,1)} %bitcast.63), calls=%async_computation.4 | async-start | bytes 2097152 | tf_op jit(solution)/shard_map/all_to_all | solution.py:364
  161.6 3.5 %channel_relay.3 = bf16[256,1024]{1,0:T(8,128)(2,1)} custom-call(bf16[512,1024]{1,0:T(8,128)(2,1)} %bitcast.39, bf16[1024,1024]{1,0:T(8,128)(2,1)} %bitcast.48, f32[1,1024]{1,0:T(1,128)S(1)} %copy-done.8, f32[1,1024]{1,0:T(1,128)S(1)} %copy-done.9, f32[1,1024]{1,0:T(1,128)S(1)} %copy-done.10, bf16[4,256,512]{2,1,0:T(8,128)(2,1)S(1)} %bitcast.29, ...), custom_call_target="tpu_custom_call" | custom-call | tf_op jit(solution)/shard_map/channel_relay/pallas_call | solution.py:243
  166.3 2.6 channel_relay_first.3
  169.3 14.0 %collective-permute-done.1.refs_1_ = bf16[256,1024]{1,0:T(8,128)(2,1)S(1)} collective-permute-done((bf16[256,1024]{1,0:T(8,128)(2,1)S(1)}, bf16[256,1024]{1,0:T(8,128)(2,1)S(1)}, u32[]{:S(2)}, u32[]{:S(2)}) %collective-permute-start.1) | collective-permute-done | bytes 524320 | tf_op jit(solution)/shard_map/ppermute | solution.py:399
  183.2 11.1 %collective-permute-done.refs_0_ = bf16[256,1024]{1,0:T(8,128)(2,1)S(1)} collective-permute-done((bf16[256,1024]{1,0:T(8,128)(2,1)}, bf16[256,1024]{1,0:T(8,128)(2,1)S(1)}, u32[]{:S(2)}, u32[]{:S(2)}) %collective-permute-start) | collective-permute-done | bytes 524320 | tf_op jit(solution)/shard_map/ppermute | solution.py:399
  194.4 3.6 %mix_first_relayed.2 = (bf16[512,1024]{1,0:T(8,128)(2,1)}, bf16[512,1024]{1,0:T(8,128)(2,1)}) custom-call(s32[1]{0:T(128)} %bitcast.14.section_ref, bf16[4,256,256]{2,1,0:T(8,128)(2,1)} %bitcast.54, bf16[1024,1024]{1,0:T(8,128)(2,1)} %fresh_ref.3, bf16[256,1024]{1,0:T(8,128)(2,1)S(1)} %collective-permute-done.refs_0_, ...), custom_call_target="tpu_custom_call" | custom-call | tf_op jit(solution)/shard_map/mix_first_relayed/pallas_call | solution.py:113
  198.0 11.5 %all-to-all-start.3 = ((bf16[64,8,1024]{2,1,0:T(8,128)(2,1)}), bf16[64,8,1024]{2,1,0:T(8,128)(2,1)}, u32[]{:S(2)}, u32[]{:S(2)}) async-start(bf16[64,8,1024]{2,1,0:T(8,128)(2,1)} %bitcast.64), calls=%async_computation.3 | async-start | bytes 2097152 | tf_op jit(solution)/shard_map/all_to_all | solution.py:364
  211.9 3.9 %mix_second.6.refs_0_ = f32[1024,1024]{1,0:T(8,128)} custom-call(bf16[1024,512]{1,0:T(8,128)(2,1)S(1)} %spread.7.left_ref, bf16[512,1024]{1,0:T(8,128)(2,1)} %bitcast.18.part_ref), custom_call_target="tpu_custom_call" | custom-call | tf_op jit(solution)/shard_map/mix_second/pallas_call | solution.py:178
  215.9 22.1 %all-to-all-done.3 = bf16[64,8,1024]{2,1,0:T(8,128)(2,1)} async-done(((bf16[64,8,1024]{2,1,0:T(8,128)(2,1)}), bf16[64,8,1024]{2,1,0:T(8,128)(2,1)}, u32[]{:S(2)}, u32[]{:S(2)}) %all-to-all-start.3) | async-done | bytes 1048608 | tf_op jit(solution)/shard_map/all_to_all | solution.py:364
  238.0 4.3 %mix_second.7 = bf16[1024,1024]{1,0:T(8,128)(2,1)} custom-call(bf16[1024,512]{1,0:T(8,128)(2,1)S(1)} %copy-done.7, bf16[512,1024]{1,0:T(8,128)(2,1)} %bitcast.16.part_ref, f32[1024,1024]{1,0:T(8,128)} %mix_second.6.refs_0_), custom_call_target="tpu_custom_call" | custom-call | tf_op jit(solution)/shard_map/mix_second/pallas_call | solution.py:178
  242.2 6.5 %all-to-all-start.5 = ((bf16[64,16,1024]{2,1,0:T(8,128)(2,1)}), bf16[64,16,1024]{2,1,0:T(8,128)(2,1)}, u32[]{:S(2)}, u32[]{:S(2)}) async-start(bf16[64,16,1024]{2,1,0:T(8,128)(2,1)} %bitcast.51), calls=%async_computation.5 | async-start | bytes 4194304 | tf_op jit(solution)/shard_map/all_to_all | solution.py:364
  248.8 2.9 maximum_bitcast_fusion
  251.6 48.2 %all-to-all-done.5 = bf16[64,16,1024]{2,1,0:T(8,128)(2,1)} async-done(((bf16[64,16,1024]{2,1,0:T(8,128)(2,1)}), bf16[64,16,1024]{2,1,0:T(8,128)(2,1)}, u32[]{:S(2)}, u32[]{:S(2)}) %all-to-all-start.5) | async-done | bytes 2097184 | tf_op jit(solution)/shard_map/all_to_all | solution.py:364
  299.9 6.6 %channel_last.1 = bf16[4,256,1024]{2,1,0:T(8,128)(2,1)} custom-call(bf16[1024,1024]{1,0:T(8,128)(2,1)} %bitcast.20.returned_ref, bf16[2,256,1024]{2,1,0:T(8,128)(2,1)} %bitcast.61, bf16[2,256,1024]{2,1,0:T(8,128)(2,1)} %bitcast.62, f32[1,1024]{1,0:T(1,128)S(1)} %copy-done.8, f32[1,1024]{1,0:T(1,128)S(1)} %copy-done.9, f32[1,1024]{1,0:T(1,128)S(1)} %copy-done.10, ...), custom_call_target="tpu_custom_call" | custom-call | tf_op jit(solution)/shard_map/channel_last/pallas_call | solution.py:346
  (54 shorter events, 20.4 us)
Async XLA Ops:
  3.9 13.1 %copy-start.11 = (bf16[1,4,256,256]{3,2,1,0:T(8,128)(2,1)S(1)}, bf16[1,4,256,256]{3,2,1,0:T(8,128)(2,1)}, u32[]{:S(2)}) copy-start(bf16[1,4,256,256]{3,2,1,0:T(8,128)(2,1)} %param.12) | copy-start | bytes 1572868
  3.9 64.3 %all-to-all-start = ((bf16[64,16,1024]{2,1,0:T(8,128)(2,1)}), bf16[64,16,1024]{2,1,0:T(8,128)(2,1)S(1)}, u32[]{:S(2)}, u32[]{:S(2)}) async-start(bf16[64,16,1024]{2,1,0:T(8,128)(2,1)} %bitcast.50), calls=%async_computation | async-start | bytes 4194304 | tf_op jit(solution)/shard_map/all_to_all | solution.py:364
  70.5 34.4 %all-to-all-start.1 = ((bf16[64,8,1024]{2,1,0:T(8,128)(2,1)}), bf16[64,8,1024]{2,1,0:T(8,128)(2,1)S(1)}, u32[]{:S(2)}, u32[]{:S(2)}) async-start(bf16[64,8,1024]{2,1,0:T(8,128)(2,1)} %bitcast.56), calls=%async_computation.1 | async-start | bytes 2097152 | tf_op jit(solution)/shard_map/all_to_all | solution.py:364
  80.0 33.0 %copy-start = (bf16[1,4,256,512]{3,2,1,0:T(8,128)(2,1)S(1)}, bf16[1,4,256,512]{3,2,1,0:T(8,128)(2,1)}, u32[]{:S(2)}) copy-start(bf16[1,4,256,512]{3,2,1,0:T(8,128)(2,1)} %param.16) | copy-start | bytes 3145732
  80.0 33.0 %copy-start.1 = (bf16[1,4,4,128,256]{4,3,2,1,0:T(8,128)(2,1)S(1)}, bf16[1,4,4,128,256]{4,3,2,1,0:T(8,128)(2,1)}, u32[]{:S(2)}) copy-start(bf16[1,4,4,128,256]{4,3,2,1,0:T(8,128)(2,1)} %param.17) | copy-start | bytes 3145732
  80.0 33.0 %copy-start.8 = (f32[1,1024]{1,0:T(1,128)S(1)}, f32[1,1024]{1,0:T(1,128)}, u32[]{:S(2)}) copy-start(f32[1,1024]{1,0:T(1,128)} %refs_2_.9) | copy-start | bytes 12292
  80.0 33.0 %copy-start.9 = (f32[1,1024]{1,0:T(1,128)S(1)}, f32[1,1024]{1,0:T(1,128)}, u32[]{:S(2)}) copy-start(f32[1,1024]{1,0:T(1,128)} %refs_3_.1) | copy-start | bytes 12292
  80.0 33.0 %copy-start.10 = (f32[1,1024]{1,0:T(1,128)S(1)}, f32[1,1024]{1,0:T(1,128)}, u32[]{:S(2)}) copy-start(f32[1,1024]{1,0:T(1,128)} %refs_4_.1) | copy-start | bytes 12292
  105.8 43.3 %all-to-all-start.2 = ((bf16[64,8,1024]{2,1,0:T(8,128)(2,1)}), bf16[64,8,1024]{2,1,0:T(8,128)(2,1)S(1)}, u32[]{:S(2)}, u32[]{:S(2)}) async-start(bf16[64,8,1024]{2,1,0:T(8,128)(2,1)} %bitcast.55), calls=%async_computation.2 | async-start | bytes 2097152 | tf_op jit(solution)/shard_map/all_to_all | solution.py:364
  113.1 3.6 %copy-start.5 = (bf16[64,8,1024]{2,1,0:T(8,128)(2,1)S(1)}, bf16[64,8,1024]{2,1,0:T(8,128)(2,1)}, u32[]{:S(2)}) copy-start(bf16[64,8,1024]{2,1,0:T(8,128)(2,1)} %copy-done.4) | copy-start | bytes 3145732
  119.2 14.7 %collective-permute-start.3 = (bf16[256,1024]{1,0:T(8,128)(2,1)}, bf16[256,1024]{1,0:T(8,128)(2,1)}, u32[]{:S(2)}, u32[]{:S(2)}) collective-permute-start(bf16[256,1024]{1,0:T(8,128)(2,1)} %channel_relay.2), channel_id=1, source_target_pairs={{0,64},{64,128},{128,192},{192,0},{1,65},{65,129},{129,193},{193,1... | collective-permute-start | bytes 1572872 | tf_op jit(solution)/shard_map/ppermute | solution.py:399
  120.6 24.6 %collective-permute-start.2 = (bf16[256,1024]{1,0:T(8,128)(2,1)}, bf16[256,1024]{1,0:T(8,128)(2,1)}, u32[]{:S(2)}, u32[]{:S(2)}) collective-permute-start(bf16[256,1024]{1,0:T(8,128)(2,1)} %channel_relay_first.2), channel_id=1, source_target_pairs={{0,64},{64,128},{128,192},{192,0},{1,65},{65,129},{129,193},{193,1... | collective-permute-start | bytes 1572872 | tf_op jit(solution)/shard_map/ppermute | solution.py:399
  149.1 12.4 %copy-start.2 = (bf16[64,8,1024]{2,1,0:T(8,128)(2,1)}, bf16[64,8,1024]{2,1,0:T(8,128)(2,1)S(1)}, u32[]{:S(2)}) copy-start(bf16[64,8,1024]{2,1,0:T(8,128)(2,1)S(1)} %all-to-all-done.2) | copy-start | bytes 3145732
  149.1 48.8 %all-to-all-start.4 = ((bf16[64,8,1024]{2,1,0:T(8,128)(2,1)}), bf16[64,8,1024]{2,1,0:T(8,128)(2,1)}, u32[]{:S(2)}, u32[]{:S(2)}) async-start(bf16[64,8,1024]{2,1,0:T(8,128)(2,1)} %bitcast.63), calls=%async_computation.4 | async-start | bytes 2097152 | tf_op jit(solution)/shard_map/all_to_all | solution.py:364
  165.1 1.2 copy-start.3
  166.3 2.6 copy-start.13
  168.9 40.6 %copy-start.12 = (bf16[1,4,256,256]{3,2,1,0:T(8,128)(2,1)S(1)}, bf16[1,4,256,256]{3,2,1,0:T(8,128)(2,1)}, u32[]{:S(2)}) copy-start(bf16[1,4,256,256]{3,2,1,0:T(8,128)(2,1)} %param.12) | copy-start | bytes 1572868
  168.9 14.3 %collective-permute-start.1 = (bf16[256,1024]{1,0:T(8,128)(2,1)S(1)}, bf16[256,1024]{1,0:T(8,128)(2,1)S(1)}, u32[]{:S(2)}, u32[]{:S(2)}) collective-permute-start(bf16[256,1024]{1,0:T(8,128)(2,1)S(1)} %copy-done.13), channel_id=1, source_target_pairs={{0,64},{64,128},{128,192},{192,0},{1,65},{65,129},{129,193},{193,1... | collective-permute-start | bytes 1572872 | tf_op jit(solution)/shard_map/ppermute | solution.py:399
  169.0 25.4 %collective-permute-start = (bf16[256,1024]{1,0:T(8,128)(2,1)}, bf16[256,1024]{1,0:T(8,128)(2,1)S(1)}, u32[]{:S(2)}, u32[]{:S(2)}) collective-permute-start(bf16[256,1024]{1,0:T(8,128)(2,1)} %channel_relay_first.3), channel_id=1, source_target_pairs={{0,64},{64,128},{128,192},{192,0},{1,65},{65,129},{129,193},{193,1... | collective-permute-start | bytes 1572872 | tf_op jit(solution)/shard_map/ppermute | solution.py:399
  198.0 40.0 %all-to-all-start.3 = ((bf16[64,8,1024]{2,1,0:T(8,128)(2,1)}), bf16[64,8,1024]{2,1,0:T(8,128)(2,1)}, u32[]{:S(2)}, u32[]{:S(2)}) async-start(bf16[64,8,1024]{2,1,0:T(8,128)(2,1)} %bitcast.64), calls=%async_computation.3 | async-start | bytes 2097152 | tf_op jit(solution)/shard_map/all_to_all | solution.py:364
  211.9 26.0 %copy-start.7 = (bf16[1024,512]{1,0:T(8,128)(2,1)S(1)}, bf16[1024,512]{1,0:T(8,128)(2,1)}, u32[]{:S(2)}) copy-start(bf16[1024,512]{1,0:T(8,128)(2,1)} %copy-done.6) | copy-start | bytes 3145732
  242.2 6.5 %copy-start.14 = (bf16[256,1024]{1,0:T(8,128)(2,1)S(1)}, bf16[256,1024]{1,0:T(8,128)(2,1)}, u32[]{:S(2)}) copy-start(bf16[256,1024]{1,0:T(8,128)(2,1)} %channel_relay.3) | copy-start | bytes 1572868
  242.2 6.5 %copy-start.15 = (bf16[256,1024]{1,0:T(8,128)(2,1)S(1)}, bf16[256,1024]{1,0:T(8,128)(2,1)}, u32[]{:S(2)}) copy-start(bf16[256,1024]{1,0:T(8,128)(2,1)} %channel_relay_first.2) | copy-start | bytes 1572868
  242.2 57.6 %all-to-all-start.5 = ((bf16[64,16,1024]{2,1,0:T(8,128)(2,1)}), bf16[64,16,1024]{2,1,0:T(8,128)(2,1)}, u32[]{:S(2)}, u32[]{:S(2)}) async-start(bf16[64,16,1024]{2,1,0:T(8,128)(2,1)} %bitcast.51), calls=%async_computation.5 | async-start | bytes 4194304 | tf_op jit(solution)/shard_map/all_to_all | solution.py:364
  (2 other events, 1.9 us)
